TPU v7x, 256 devices: a whole 4x4x8 slice. The times are simulated.
256 devices in a mesh: tm: 16 (over z, x_lo), space: 16 (over x_hi, y, core).
Axes of the slice: x: 4 (x_hi: 2, x_lo: 2; x = x_hi * 2 + x_lo), y: 4, z: 8, core: 2. Of those that a mesh axis runs over, the one named last changes fastest.
Arguments:
- slice_starts: float32 [16, 64, 512, 128], P('tm', 'space'), may hold values from -6 to 6
- diffusion: float32 [64, 512, 128], P('space'), may hold values from 0.01 to 0.05
- courant: float32 [64, 512, 128], P('space'), may hold values from 0.3 to 0.6
- loss: float32 [64, 512, 128], P('space'), may hold values from 0.002 to 0.02
- heating: float32 [64, 512, 128], P('space'), may hold values from -0.6 to 0.6
Outputs:
- end_states: float32 [16, 64, 512, 128], P('tm', 'space')
- next_starts: float32 [16, 64, 512, 128], P('tm', 'space')
All inputs are finite; a program needn't handle non-finite values.
Results may differ from a plain program's by a relative error of at most 0.00002.
Values sent between devices are 32-bit elements; how exact they have to be, the bound alone decides.
No kernel may reach another device: no remote copies, remote signals or barrier semaphores. Data moves between devices by JAX's collectives and lax.ppermute only.
A program may use at most 128 MiB of HBM per device.

v0:
```python
import jax
import jax.numpy as jnp
from jax import lax
from jax.sharding import PartitionSpec as P

FINE = 8


def extended(x, sides, width):
    for axis, dim in sides:
        devices, length = (lax.axis_size(axis), x.shape[dim])
        up = [(i, (i + 1) % devices) for i in range(devices - 1)]
        down = [(j, i) for i, j in up]
        last = lax.slice_in_dim(x, length - width, length, axis=dim)
        first = lax.slice_in_dim(x, 0, width, axis=dim)
        before = lax.ppermute(last, axis, up)
        after = lax.ppermute(first, axis, down)
        x = jnp.concatenate([before, x, after], axis=dim)
    return x


def shifted(block, axis, distance):
    devices = range(lax.axis_size(axis))
    route = [(i - distance, i) for i in devices if i - distance in devices]
    return lax.ppermute(block, axis, route)


def stencil(wide):
    padded = jnp.pad(wide, ((0, 0), (1, 1), (1, 1)))
    total = padded[2:, 1:-1, 1:-1] + padded[:-2, 1:-1, 1:-1]
    total = total + padded[1:-1, 2:, 1:-1] + padded[1:-1, :-2, 1:-1]
    total = total + padded[1:-1, 1:-1, 2:] + padded[1:-1, 1:-1, :-2]
    return (total, padded[:-2, 1:-1, 1:-1])


def neighbours(v):
    wide = extended(v, (("space", 0),), 1)
    return stencil(wide)


def on_device(slice_starts, diffusion, courant, loss, heating):
    start = slice_starts[0]
    denom = 1.0 + FINE * (6.0 * diffusion + courant + loss)

    def linear_part(v):
        total, upwind = neighbours(v)
        return (v + FINE * (diffusion * total + courant * upwind)) / denom

    state = start
    for step in range(FINE):
        total, upwind = neighbours(state)
        state = (
            state
            + diffusion * (total - 6.0 * state)
            - courant * (state - upwind)
            - loss * state
            + heating
        )
    slot = lax.axis_index("tm")
    coarse_old = linear_part(start)
    element = jnp.where(slot > 0, state - coarse_old, state)

    def one_round(index, carried):
        received = shifted(carried, "tm", 1)
        return element + linear_part(received)

    accumulated = lax.fori_loop(0, lax.axis_size("tm") - 1, one_round, element)
    arrived = shifted(accumulated, "tm", 1)
    following = jnp.where(slot == 0, start, arrived)
    return (accumulated[None], following[None])


def solution(mesh):
    return jax.shard_map(
        on_device,
        mesh=mesh,
        in_specs=(
            P("tm", "space", None, None),
            P("space", None, None),
            P("space", None, None),
            P("space", None, None),
            P("space", None, None),
        ),
        out_specs=(P("tm", "space", None, None), P("tm", "space", None, None)),
        check_vma=False,
    )
```

profile of v0, /device:TPU:102, one launch (start us, length us, event | category | flops | bytes accessed | tf_op | source)
XLA Modules:
  0.0 901.6 jit_solution(7668507432825602021)
XLA Ops:
  144.7 737.7 %while.12 = (s32[]{:T(128)}, f32[4,512,128]{2,1,0:T(8,128)}, f32[4,512,128]{2,1,0:T(8,128)S(1)}, f32[4,512,128]{2,1,0:T(8,128)S(1)}, f32[4,512,128]{2,1,0:T(8,128)}, /*index=5*/f32[4,512,128]{2,1,0:T(8,128)}, s32[]{:T(128)}) while((s32[]{:T(128)}, f32[4,512,128]{2,1,0:T(8,128)}, f32[4,512,128]{2,1,0:T(8,128)S(1)}, ...), condition=%wide.region_1.2_spmd, body=%wide.region_0.1_spmd.sunk | while | flops 9683818 | bytes 29915484 | solution.py:67
  149.1 17.3 %collective-permute-done = f32[4,512,128]{2,1,0:T(8,128)S(1)} collective-permute-done((f32[4,512,128]{2,1,0:T(8,128)}, f32[4,512,128]{2,1,0:T(8,128)S(1)}, u32[]{:S(2)}, u32[]{:S(2)}) %collective-permute-start) | collective-permute-done | bytes 1048608 | tf_op jit(solution)/shard_map/while/body/eval_jaxpr/ppermute | solution.py:25
  193.8 15.5 %collective-permute-done = f32[4,512,128]{2,1,0:T(8,128)S(1)} collective-permute-done((f32[4,512,128]{2,1,0:T(8,128)}, f32[4,512,128]{2,1,0:T(8,128)S(1)}, u32[]{:S(2)}, u32[]{:S(2)}) %collective-permute-start) | collective-permute-done | bytes 1048608 | tf_op jit(solution)/shard_map/while/body/eval_jaxpr/ppermute | solution.py:25
  216.2 18.7 %collective-permute-done.2 = f32[1,512,128]{2,1,0:T(8,128)} collective-permute-done((f32[1,512,128]{2,1,0:T(8,128)}, f32[1,512,128]{2,1,0:T(8,128)}, u32[]{:S(2)}, u32[]{:S(2)}) %collective-permute-start.2) | collective-permute-done | bytes 262176 | tf_op jit(solution)/shard_map/while/body/eval_jaxpr/ppermute | solution.py:16
  241.7 15.0 %collective-permute-done = f32[4,512,128]{2,1,0:T(8,128)S(1)} collective-permute-done((f32[4,512,128]{2,1,0:T(8,128)}, f32[4,512,128]{2,1,0:T(8,128)S(1)}, u32[]{:S(2)}, u32[]{:S(2)}) %collective-permute-start) | collective-permute-done | bytes 1048608 | tf_op jit(solution)/shard_map/while/body/eval_jaxpr/ppermute | solution.py:25
  263.6 29.9 %collective-permute-done.2 = f32[1,512,128]{2,1,0:T(8,128)} collective-permute-done((f32[1,512,128]{2,1,0:T(8,128)}, f32[1,512,128]{2,1,0:T(8,128)}, u32[]{:S(2)}, u32[]{:S(2)}) %collective-permute-start.2) | collective-permute-done | bytes 262176 | tf_op jit(solution)/shard_map/while/body/eval_jaxpr/ppermute | solution.py:16
  300.4 15.0 %collective-permute-done = f32[4,512,128]{2,1,0:T(8,128)S(1)} collective-permute-done((f32[4,512,128]{2,1,0:T(8,128)}, f32[4,512,128]{2,1,0:T(8,128)S(1)}, u32[]{:S(2)}, u32[]{:S(2)}) %collective-permute-start) | collective-permute-done | bytes 1048608 | tf_op jit(solution)/shard_map/while/body/eval_jaxpr/ppermute | solution.py:25
  338.7 17.4 %collective-permute-done = f32[4,512,128]{2,1,0:T(8,128)S(1)} collective-permute-done((f32[4,512,128]{2,1,0:T(8,128)}, f32[4,512,128]{2,1,0:T(8,128)S(1)}, u32[]{:S(2)}, u32[]{:S(2)}) %collective-permute-start) | collective-permute-done | bytes 1048608 | tf_op jit(solution)/shard_map/while/body/eval_jaxpr/ppermute | solution.py:25
  363.1 17.8 %collective-permute-done.2 = f32[1,512,128]{2,1,0:T(8,128)} collective-permute-done((f32[1,512,128]{2,1,0:T(8,128)}, f32[1,512,128]{2,1,0:T(8,128)}, u32[]{:S(2)}, u32[]{:S(2)}) %collective-permute-start.2) | collective-permute-done | bytes 262176 | tf_op jit(solution)/shard_map/while/body/eval_jaxpr/ppermute | solution.py:16
  387.7 15.0 %collective-permute-done = f32[4,512,128]{2,1,0:T(8,128)S(1)} collective-permute-done((f32[4,512,128]{2,1,0:T(8,128)}, f32[4,512,128]{2,1,0:T(8,128)S(1)}, u32[]{:S(2)}, u32[]{:S(2)}) %collective-permute-start) | collective-permute-done | bytes 1048608 | tf_op jit(solution)/shard_map/while/body/eval_jaxpr/ppermute | solution.py:25
  409.6 29.9 %collective-permute-done.2 = f32[1,512,128]{2,1,0:T(8,128)} collective-permute-done((f32[1,512,128]{2,1,0:T(8,128)}, f32[1,512,128]{2,1,0:T(8,128)}, u32[]{:S(2)}, u32[]{:S(2)}) %collective-permute-start.2) | collective-permute-done | bytes 262176 | tf_op jit(solution)/shard_map/while/body/eval_jaxpr/ppermute | solution.py:16
  484.7 17.4 %collective-permute-done = f32[4,512,128]{2,1,0:T(8,128)S(1)} collective-permute-done((f32[4,512,128]{2,1,0:T(8,128)}, f32[4,512,128]{2,1,0:T(8,128)S(1)}, u32[]{:S(2)}, u32[]{:S(2)}) %collective-permute-start) | collective-permute-done | bytes 1048608 | tf_op jit(solution)/shard_map/while/body/eval_jaxpr/ppermute | solution.py:25
  509.1 17.8 %collective-permute-done.2 = f32[1,512,128]{2,1,0:T(8,128)} collective-permute-done((f32[1,512,128]{2,1,0:T(8,128)}, f32[1,512,128]{2,1,0:T(8,128)}, u32[]{:S(2)}, u32[]{:S(2)}) %collective-permute-start.2) | collective-permute-done | bytes 262176 | tf_op jit(solution)/shard_map/while/body/eval_jaxpr/ppermute | solution.py:16
  533.7 15.0 %collective-permute-done = f32[4,512,128]{2,1,0:T(8,128)S(1)} collective-permute-done((f32[4,512,128]{2,1,0:T(8,128)}, f32[4,512,128]{2,1,0:T(8,128)S(1)}, u32[]{:S(2)}, u32[]{:S(2)}) %collective-permute-start) | collective-permute-done | bytes 1048608 | tf_op jit(solution)/shard_map/while/body/eval_jaxpr/ppermute | solution.py:25
  555.6 29.9 %collective-permute-done.2 = f32[1,512,128]{2,1,0:T(8,128)} collective-permute-done((f32[1,512,128]{2,1,0:T(8,128)}, f32[1,512,128]{2,1,0:T(8,128)}, u32[]{:S(2)}, u32[]{:S(2)}) %collective-permute-start.2) | collective-permute-done | bytes 262176 | tf_op jit(solution)/shard_map/while/body/eval_jaxpr/ppermute | solution.py:16
  592.3 15.0 %collective-permute-done = f32[4,512,128]{2,1,0:T(8,128)S(1)} collective-permute-done((f32[4,512,128]{2,1,0:T(8,128)}, f32[4,512,128]{2,1,0:T(8,128)S(1)}, u32[]{:S(2)}, u32[]{:S(2)}) %collective-permute-start) | collective-permute-done | bytes 1048608 | tf_op jit(solution)/shard_map/while/body/eval_jaxpr/ppermute | solution.py:25
  630.7 17.4 %collective-permute-done = f32[4,512,128]{2,1,0:T(8,128)S(1)} collective-permute-done((f32[4,512,128]{2,1,0:T(8,128)}, f32[4,512,128]{2,1,0:T(8,128)S(1)}, u32[]{:S(2)}, u32[]{:S(2)}) %collective-permute-start) | collective-permute-done | bytes 1048608 | tf_op jit(solution)/shard_map/while/body/eval_jaxpr/ppermute | solution.py:25
  655.1 17.8 %collective-permute-done.2 = f32[1,512,128]{2,1,0:T(8,128)} collective-permute-done((f32[1,512,128]{2,1,0:T(8,128)}, f32[1,512,128]{2,1,0:T(8,128)}, u32[]{:S(2)}, u32[]{:S(2)}) %collective-permute-start.2) | collective-permute-done | bytes 262176 | tf_op jit(solution)/shard_map/while/body/eval_jaxpr/ppermute | solution.py:16
  701.6 29.9 %collective-permute-done.2 = f32[1,512,128]{2,1,0:T(8,128)} collective-permute-done((f32[1,512,128]{2,1,0:T(8,128)}, f32[1,512,128]{2,1,0:T(8,128)}, u32[]{:S(2)}, u32[]{:S(2)}) %collective-permute-start.2) | collective-permute-done | bytes 262176 | tf_op jit(solution)/shard_map/while/body/eval_jaxpr/ppermute | solution.py:16
  738.3 15.0 %collective-permute-done = f32[4,512,128]{2,1,0:T(8,128)S(1)} collective-permute-done((f32[4,512,128]{2,1,0:T(8,128)}, f32[4,512,128]{2,1,0:T(8,128)S(1)}, u32[]{:S(2)}, u32[]{:S(2)}) %collective-permute-start) | collective-permute-done | bytes 1048608 | tf_op jit(solution)/shard_map/while/body/eval_jaxpr/ppermute | solution.py:25
  776.7 17.4 %collective-permute-done = f32[4,512,128]{2,1,0:T(8,128)S(1)} collective-permute-done((f32[4,512,128]{2,1,0:T(8,128)}, f32[4,512,128]{2,1,0:T(8,128)S(1)}, u32[]{:S(2)}, u32[]{:S(2)}) %collective-permute-start) | collective-permute-done | bytes 1048608 | tf_op jit(solution)/shard_map/while/body/eval_jaxpr/ppermute | solution.py:25
  801.1 17.8 %collective-permute-done.2 = f32[1,512,128]{2,1,0:T(8,128)} collective-permute-done((f32[1,512,128]{2,1,0:T(8,128)}, f32[1,512,128]{2,1,0:T(8,128)}, u32[]{:S(2)}, u32[]{:S(2)}) %collective-permute-start.2) | collective-permute-done | bytes 262176 | tf_op jit(solution)/shard_map/while/body/eval_jaxpr/ppermute | solution.py:16
  825.7 15.0 %collective-permute-done = f32[4,512,128]{2,1,0:T(8,128)S(1)} collective-permute-done((f32[4,512,128]{2,1,0:T(8,128)}, f32[4,512,128]{2,1,0:T(8,128)S(1)}, u32[]{:S(2)}, u32[]{:S(2)}) %collective-permute-start) | collective-permute-done | bytes 1048608 | tf_op jit(solution)/shard_map/while/body/eval_jaxpr/ppermute | solution.py:25
  847.6 29.9 %collective-permute-done.2 = f32[1,512,128]{2,1,0:T(8,128)} collective-permute-done((f32[1,512,128]{2,1,0:T(8,128)}, f32[1,512,128]{2,1,0:T(8,128)}, u32[]{:S(2)}, u32[]{:S(2)}) %collective-permute-start.2) | collective-permute-done | bytes 262176 | tf_op jit(solution)/shard_map/while/body/eval_jaxpr/ppermute | solution.py:16
  (254 shorter events, 452.7 us)
Async XLA Ops:
  144.7 21.7 %collective-permute-start = (f32[4,512,128]{2,1,0:T(8,128)}, f32[4,512,128]{2,1,0:T(8,128)S(1)}, u32[]{:S(2)}, u32[]{:S(2)}) collective-permute-start(f32[4,512,128]{2,1,0:T(8,128)} %get-tuple-element.161), channel_id=1, source_target_pairs={{0,16},{16,32},{32,48},{48,64},{64,80},{80,96},{96,112},{112,128},... | collective-permute-start | bytes 3145736 | tf_op jit(solution)/shard_map/while/body/eval_jaxpr/ppermute | solution.py:25
  185.6 23.7 %collective-permute-start = (f32[4,512,128]{2,1,0:T(8,128)}, f32[4,512,128]{2,1,0:T(8,128)S(1)}, u32[]{:S(2)}, u32[]{:S(2)}) collective-permute-start(f32[4,512,128]{2,1,0:T(8,128)} %get-tuple-element.161), channel_id=1, source_target_pairs={{0,16},{16,32},{32,48},{48,64},{64,80},{80,96},{96,112},{112,128},... | collective-permute-start | bytes 3145736 | tf_op jit(solution)/shard_map/while/body/eval_jaxpr/ppermute | solution.py:25
  212.1 22.9 %collective-permute-start.2 = (f32[1,512,128]{2,1,0:T(8,128)}, f32[1,512,128]{2,1,0:T(8,128)}, u32[]{:S(2)}, u32[]{:S(2)}) collective-permute-start(f32[1,512,128]{2,1,0:T(8,128)} %get-tuple-element.152), channel_id=1, source_target_pairs={{0,1},{1,2},{2,3},{3,4},{4,5},{5,6},{6,7},{7,8},{8,9},{9,10},{10,1... | collective-permute-start | bytes 786440 | tf_op jit(solution)/shard_map/while/body/eval_jaxpr/ppermute | solution.py:16
  239.8 16.9 %collective-permute-start = (f32[4,512,128]{2,1,0:T(8,128)}, f32[4,512,128]{2,1,0:T(8,128)S(1)}, u32[]{:S(2)}, u32[]{:S(2)}) collective-permute-start(f32[4,512,128]{2,1,0:T(8,128)} %get-tuple-element.161), channel_id=1, source_target_pairs={{0,16},{16,32},{32,48},{48,64},{64,80},{80,96},{96,112},{112,128},... | collective-permute-start | bytes 3145736 | tf_op jit(solution)/shard_map/while/body/eval_jaxpr/ppermute | solution.py:25
  259.5 34.1 %collective-permute-start.2 = (f32[1,512,128]{2,1,0:T(8,128)}, f32[1,512,128]{2,1,0:T(8,128)}, u32[]{:S(2)}, u32[]{:S(2)}) collective-permute-start(f32[1,512,128]{2,1,0:T(8,128)} %get-tuple-element.152), channel_id=1, source_target_pairs={{0,1},{1,2},{2,3},{3,4},{4,5},{5,6},{6,7},{7,8},{8,9},{9,10},{10,1... | collective-permute-start | bytes 786440 | tf_op jit(solution)/shard_map/while/body/eval_jaxpr/ppermute | solution.py:16
  298.5 16.9 %collective-permute-start = (f32[4,512,128]{2,1,0:T(8,128)}, f32[4,512,128]{2,1,0:T(8,128)S(1)}, u32[]{:S(2)}, u32[]{:S(2)}) collective-permute-start(f32[4,512,128]{2,1,0:T(8,128)} %get-tuple-element.161), channel_id=1, source_target_pairs={{0,16},{16,32},{32,48},{48,64},{64,80},{80,96},{96,112},{112,128},... | collective-permute-start | bytes 3145736 | tf_op jit(solution)/shard_map/while/body/eval_jaxpr/ppermute | solution.py:25
  334.6 21.6 %collective-permute-start = (f32[4,512,128]{2,1,0:T(8,128)}, f32[4,512,128]{2,1,0:T(8,128)S(1)}, u32[]{:S(2)}, u32[]{:S(2)}) collective-permute-start(f32[4,512,128]{2,1,0:T(8,128)} %get-tuple-element.161), channel_id=1, source_target_pairs={{0,16},{16,32},{32,48},{48,64},{64,80},{80,96},{96,112},{112,128},... | collective-permute-start | bytes 3145736 | tf_op jit(solution)/shard_map/while/body/eval_jaxpr/ppermute | solution.py:25
  358.9 22.0 %collective-permute-start.2 = (f32[1,512,128]{2,1,0:T(8,128)}, f32[1,512,128]{2,1,0:T(8,128)}, u32[]{:S(2)}, u32[]{:S(2)}) collective-permute-start(f32[1,512,128]{2,1,0:T(8,128)} %get-tuple-element.152), channel_id=1, source_target_pairs={{0,1},{1,2},{2,3},{3,4},{4,5},{5,6},{6,7},{7,8},{8,9},{9,10},{10,1... | collective-permute-start | bytes 786440 | tf_op jit(solution)/shard_map/while/body/eval_jaxpr/ppermute | solution.py:16
  385.8 16.9 %collective-permute-start = (f32[4,512,128]{2,1,0:T(8,128)}, f32[4,512,128]{2,1,0:T(8,128)S(1)}, u32[]{:S(2)}, u32[]{:S(2)}) collective-permute-start(f32[4,512,128]{2,1,0:T(8,128)} %get-tuple-element.161), channel_id=1, source_target_pairs={{0,16},{16,32},{32,48},{48,64},{64,80},{80,96},{96,112},{112,128},... | collective-permute-start | bytes 3145736 | tf_op jit(solution)/shard_map/while/body/eval_jaxpr/ppermute | solution.py:25
  405.4 34.1 %collective-permute-start.2 = (f32[1,512,128]{2,1,0:T(8,128)}, f32[1,512,128]{2,1,0:T(8,128)}, u32[]{:S(2)}, u32[]{:S(2)}) collective-permute-start(f32[1,512,128]{2,1,0:T(8,128)} %get-tuple-element.152), channel_id=1, source_target_pairs={{0,1},{1,2},{2,3},{3,4},{4,5},{5,6},{6,7},{7,8},{8,9},{9,10},{10,1... | collective-permute-start | bytes 786440 | tf_op jit(solution)/shard_map/while/body/eval_jaxpr/ppermute | solution.py:16
  444.4 16.9 %collective-permute-start = (f32[4,512,128]{2,1,0:T(8,128)}, f32[4,512,128]{2,1,0:T(8,128)S(1)}, u32[]{:S(2)}, u32[]{:S(2)}) collective-permute-start(f32[4,512,128]{2,1,0:T(8,128)} %get-tuple-element.161), channel_id=1, source_target_pairs={{0,16},{16,32},{32,48},{48,64},{64,80},{80,96},{96,112},{112,128},... | collective-permute-start | bytes 3145736 | tf_op jit(solution)/shard_map/while/body/eval_jaxpr/ppermute | solution.py:25
  480.6 21.6 %collective-permute-start = (f32[4,512,128]{2,1,0:T(8,128)}, f32[4,512,128]{2,1,0:T(8,128)S(1)}, u32[]{:S(2)}, u32[]{:S(2)}) collective-permute-start(f32[4,512,128]{2,1,0:T(8,128)} %get-tuple-element.161), channel_id=1, source_target_pairs={{0,16},{16,32},{32,48},{48,64},{64,80},{80,96},{96,112},{112,128},... | collective-permute-start | bytes 3145736 | tf_op jit(solution)/shard_map/while/body/eval_jaxpr/ppermute | solution.py:25
  504.9 22.0 %collective-permute-start.2 = (f32[1,512,128]{2,1,0:T(8,128)}, f32[1,512,128]{2,1,0:T(8,128)}, u32[]{:S(2)}, u32[]{:S(2)}) collective-permute-start(f32[1,512,128]{2,1,0:T(8,128)} %get-tuple-element.152), channel_id=1, source_target_pairs={{0,1},{1,2},{2,3},{3,4},{4,5},{5,6},{6,7},{7,8},{8,9},{9,10},{10,1... | collective-permute-start | bytes 786440 | tf_op jit(solution)/shard_map/while/body/eval_jaxpr/ppermute | solution.py:16
  531.8 16.9 %collective-permute-start = (f32[4,512,128]{2,1,0:T(8,128)}, f32[4,512,128]{2,1,0:T(8,128)S(1)}, u32[]{:S(2)}, u32[]{:S(2)}) collective-permute-start(f32[4,512,128]{2,1,0:T(8,128)} %get-tuple-element.161), channel_id=1, source_target_pairs={{0,16},{16,32},{32,48},{48,64},{64,80},{80,96},{96,112},{112,128},... | collective-permute-start | bytes 3145736 | tf_op jit(solution)/shard_map/while/body/eval_jaxpr/ppermute | solution.py:25
  551.4 34.1 %collective-permute-start.2 = (f32[1,512,128]{2,1,0:T(8,128)}, f32[1,512,128]{2,1,0:T(8,128)}, u32[]{:S(2)}, u32[]{:S(2)}) collective-permute-start(f32[1,512,128]{2,1,0:T(8,128)} %get-tuple-element.152), channel_id=1, source_target_pairs={{0,1},{1,2},{2,3},{3,4},{4,5},{5,6},{6,7},{7,8},{8,9},{9,10},{10,1... | collective-permute-start | bytes 786440 | tf_op jit(solution)/shard_map/while/body/eval_jaxpr/ppermute | solution.py:16
  590.4 16.9 %collective-permute-start = (f32[4,512,128]{2,1,0:T(8,128)}, f32[4,512,128]{2,1,0:T(8,128)S(1)}, u32[]{:S(2)}, u32[]{:S(2)}) collective-permute-start(f32[4,512,128]{2,1,0:T(8,128)} %get-tuple-element.161), channel_id=1, source_target_pairs={{0,16},{16,32},{32,48},{48,64},{64,80},{80,96},{96,112},{112,128},... | collective-permute-start | bytes 3145736 | tf_op jit(solution)/shard_map/while/body/eval_jaxpr/ppermute | solution.py:25
  626.6 21.6 %collective-permute-start = (f32[4,512,128]{2,1,0:T(8,128)}, f32[4,512,128]{2,1,0:T(8,128)S(1)}, u32[]{:S(2)}, u32[]{:S(2)}) collective-permute-start(f32[4,512,128]{2,1,0:T(8,128)} %get-tuple-element.161), channel_id=1, source_target_pairs={{0,16},{16,32},{32,48},{48,64},{64,80},{80,96},{96,112},{112,128},... | collective-permute-start | bytes 3145736 | tf_op jit(solution)/shard_map/while/body/eval_jaxpr/ppermute | solution.py:25
  650.9 22.0 %collective-permute-start.2 = (f32[1,512,128]{2,1,0:T(8,128)}, f32[1,512,128]{2,1,0:T(8,128)}, u32[]{:S(2)}, u32[]{:S(2)}) collective-permute-start(f32[1,512,128]{2,1,0:T(8,128)} %get-tuple-element.152), channel_id=1, source_target_pairs={{0,1},{1,2},{2,3},{3,4},{4,5},{5,6},{6,7},{7,8},{8,9},{9,10},{10,1... | collective-permute-start | bytes 786440 | tf_op jit(solution)/shard_map/while/body/eval_jaxpr/ppermute | solution.py:16
  697.4 34.1 %collective-permute-start.2 = (f32[1,512,128]{2,1,0:T(8,128)}, f32[1,512,128]{2,1,0:T(8,128)}, u32[]{:S(2)}, u32[]{:S(2)}) collective-permute-start(f32[1,512,128]{2,1,0:T(8,128)} %get-tuple-element.152), channel_id=1, source_target_pairs={{0,1},{1,2},{2,3},{3,4},{4,5},{5,6},{6,7},{7,8},{8,9},{9,10},{10,1... | collective-permute-start | bytes 786440 | tf_op jit(solution)/shard_map/while/body/eval_jaxpr/ppermute | solution.py:16
  772.6 21.6 %collective-permute-start = (f32[4,512,128]{2,1,0:T(8,128)}, f32[4,512,128]{2,1,0:T(8,128)S(1)}, u32[]{:S(2)}, u32[]{:S(2)}) collective-permute-start(f32[4,512,128]{2,1,0:T(8,128)} %get-tuple-element.161), channel_id=1, source_target_pairs={{0,16},{16,32},{32,48},{48,64},{64,80},{80,96},{96,112},{112,128},... | collective-permute-start | bytes 3145736 | tf_op jit(solution)/shard_map/while/body/eval_jaxpr/ppermute | solution.py:25
  796.9 22.0 %collective-permute-start.2 = (f32[1,512,128]{2,1,0:T(8,128)}, f32[1,512,128]{2,1,0:T(8,128)}, u32[]{:S(2)}, u32[]{:S(2)}) collective-permute-start(f32[1,512,128]{2,1,0:T(8,128)} %get-tuple-element.152), channel_id=1, source_target_pairs={{0,1},{1,2},{2,3},{3,4},{4,5},{5,6},{6,7},{7,8},{8,9},{9,10},{10,1... | collective-permute-start | bytes 786440 | tf_op jit(solution)/shard_map/while/body/eval_jaxpr/ppermute | solution.py:16
  823.8 16.9 %collective-permute-start = (f32[4,512,128]{2,1,0:T(8,128)}, f32[4,512,128]{2,1,0:T(8,128)S(1)}, u32[]{:S(2)}, u32[]{:S(2)}) collective-permute-start(f32[4,512,128]{2,1,0:T(8,128)} %get-tuple-element.161), channel_id=1, source_target_pairs={{0,16},{16,32},{32,48},{48,64},{64,80},{80,96},{96,112},{112,128},... | collective-permute-start | bytes 3145736 | tf_op jit(solution)/shard_map/while/body/eval_jaxpr/ppermute | solution.py:25
  843.4 34.1 %collective-permute-start.2 = (f32[1,512,128]{2,1,0:T(8,128)}, f32[1,512,128]{2,1,0:T(8,128)}, u32[]{:S(2)}, u32[]{:S(2)}) collective-permute-start(f32[1,512,128]{2,1,0:T(8,128)} %get-tuple-element.152), channel_id=1, source_target_pairs={{0,1},{1,2},{2,3},{3,4},{4,5},{5,6},{6,7},{7,8},{8,9},{9,10},{10,1... | collective-permute-start | bytes 786440 | tf_op jit(solution)/shard_map/while/body/eval_jaxpr/ppermute | solution.py:16
  882.4 16.9 %collective-permute-start.19 = (f32[4,512,128]{2,1,0:T(8,128)}, f32[4,512,128]{2,1,0:T(8,128)S(1)}, u32[]{:S(2)}, u32[]{:S(2)}) collective-permute-start(f32[4,512,128]{2,1,0:T(8,128)} %get-tuple-element.79), channel_id=1, source_target_pairs={{0,16},{16,32},{32,48},{48,64},{64,80},{80,96},{96,112},{112,128},... | collective-permute-start | bytes 3145736 | tf_op jit(solution)/shard_map/ppermute | solution.py:25
  (79 other events, 1138.2 us)
where the time goes:
time: 904 us; the launch traced here: 902 us
  waiting for transfers between devices  622 us (69%)
  starting transfers between devices  160 us (18%)
  other arithmetic  99.2 us (11%)
  local copies, waits for them, and re-layouts  17.6 us (2%)
    ppermute x23, waiting for transfers between devices, extended(): before = lax.ppermute(last, axis, up)  331 us
    ppermute x16, waiting for transfers between devices, shifted(): return lax.ppermute(block, axis, route)  252 us
    ppermute x23, starting transfers between devices, extended(): after = lax.ppermute(first, axis, down)  58.2 us
    ppermute x23, starting transfers between devices, extended(): before = lax.ppermute(last, axis, up)  54.1 us
    ppermute x16, starting transfers between devices, shifted(): return lax.ppermute(block, axis, route)  48.1 us
    add x15, other arithmetic, one_round(): return element + linear_part(received)  45.6 us
    ppermute x23, waiting for transfers between devices, extended(): after = lax.ppermute(first, axis, down)  39.2 us
    concatenate x23, other arithmetic, extended(): x = jnp.concatenate([before, x, after], axis=dim)  37.4 us
  transfers between devices with their start and end apart: 62, of which 62 were waited for; matrix products, arithmetic and copies ran while one was open for 0% of the time, Pallas kernels for 0%

commit v1 on v0

v1 whole, which is shorter than its diff:
```python
import jax
import jax.numpy as jnp
from jax import lax
from jax.sharding import PartitionSpec as P

FINE = 8
SPAN = 4
ROUNDS = 2


def swaps(pairs):
    return [route for a, b in pairs for route in ((a, b), (b, a))]


def exchanged(low, high, even):
    devices = lax.axis_size("space")
    near = swaps([(i, i + 1) for i in range(0, devices - 1, 2)])
    far = swaps([(i, i + 1) for i in range(1, devices - 1, 2)])
    across = lax.ppermute(jnp.where(even, low, high), "space", far)
    beside = lax.ppermute(jnp.where(even, high, low), "space", near)
    return jnp.where(even, across, beside), jnp.where(even, beside, across)


def around(wide):
    padded = jnp.pad(wide, ((0, 0), (1, 1), (1, 1)))
    total = padded[2:, 1:-1, 1:-1] + padded[:-2, 1:-1, 1:-1]
    total = total + padded[1:-1, 2:, 1:-1] + padded[1:-1, :-2, 1:-1]
    total = total + padded[1:-1, 1:-1, 2:] + padded[1:-1, 1:-1, :-2]
    return total, wide[:-2]


def on_device(slice_starts, diffusion, courant, loss, heating):
    start = slice_starts[0]
    planes, rows, lanes = start.shape
    slices = lax.axis_size("tm")
    slot = lax.axis_index("tm")
    even = lax.axis_index("space") % 2 == 0
    part = rows // slices
    halo = slices
    window = part + 2 * halo

    denom = 1.0 + FINE * (6.0 * diffusion + courant + loss)
    own = 1.0 / denom
    side = FINE * diffusion / denom
    west = FINE * courant / denom

    fine_terms = jnp.stack([diffusion, courant, loss, heating])
    tall = jnp.pad(jnp.stack([own, side, west]), ((0, 0), (0, 0), (halo, halo), (0, 0)))
    coarse_terms = lax.dynamic_slice_in_dim(tall, slot * part, window, axis=2)
    deep = SPAN - 1
    edge = ROUNDS - 1

    def flat(*arrays):
        return jnp.concatenate([a.reshape(-1, lanes) for a in arrays])

    before, after = exchanged(
        flat(fine_terms[:, :edge], coarse_terms[:, :deep]),
        flat(fine_terms[:, planes - edge :], coarse_terms[:, planes - deep :]),
        even,
    )
    cut = 4 * edge * rows

    def fine_part(x):
        return x[:cut].reshape(4, edge, rows, lanes)

    def coarse_part(x):
        return x[cut:].reshape(3, deep, window, lanes)

    fine_terms = jnp.concatenate([fine_part(before), fine_terms, fine_part(after)], axis=1)
    coarse_terms = jnp.concatenate([coarse_part(before), coarse_terms, coarse_part(after)], axis=1)

    state = start
    first = None
    for _ in range(FINE // ROUNDS):
        before, after = exchanged(state[:ROUNDS], state[planes - ROUNDS :], even)
        state = jnp.concatenate([before, state, after])
        if first is None:
            first = state[ROUNDS - 1 : ROUNDS + planes + 1]
        for step in range(ROUNDS):
            total, upwind = around(state)
            centre = state[1:-1]
            trim = step
            d, c, l, h = (t[trim : t.shape[0] - trim] for t in fine_terms)
            state = centre + d * (total - 6.0 * centre) - c * (centre - upwind) - l * centre + h
    total, upwind = around(first)
    coarse_old = own * start + side * total + west * upwind
    element = jnp.where(slot > 0, state - coarse_old, state)

    blocks = jnp.pad(element, ((0, 0), (halo, halo), (0, 0))).reshape(planes, -1, part, lanes)
    widened = jnp.concatenate([blocks[:, :-1], blocks[:, 1:]], axis=2)
    terms = lax.all_to_all(widened.transpose(1, 0, 2, 3), "tm", 0, 0, tiled=True)

    depth = [SPAN] + [(SPAN - n) % SPAN for n in range(1, slices)]
    before, after = exchanged(
        jnp.concatenate([terms[n, :k] for n, k in enumerate(depth) if k]),
        jnp.concatenate([terms[n, planes - k :] for n, k in enumerate(depth) if k]),
        even,
    )
    offsets = [sum(depth[:n]) for n in range(slices)]

    def term(n):
        k, o = depth[n], offsets[n]
        return jnp.concatenate([before[o : o + k], terms[n], after[o : o + k]]) if k else terms[n]

    state = term(0)
    ends = [terms[0]]
    for n in range(1, slices):
        if n > 1 and n % SPAN == 1:
            low, high = exchanged(state, state, even)
            state = jnp.concatenate([low, state, high])
        k = depth[n]
        trim = deep - k
        o, s, w = (t[trim : t.shape[0] - trim] for t in coarse_terms)
        total, upwind = around(state)
        state = o * state[1:-1] + s * total + w * upwind + term(n)
        ends.append(state[k : k + planes])

    ends = jnp.stack(ends)[:, :, halo : halo + part]
    back = lax.all_to_all(ends, "tm", 0, 0, tiled=True)
    end_state = back.transpose(1, 0, 2, 3).reshape(planes, rows, lanes)
    arrived = lax.ppermute(end_state, "tm", [(i, i + 1) for i in range(slices - 1)])
    following = jnp.where(slot == 0, start, arrived)
    return end_state[None], following[None]


def solution(mesh):
    return jax.shard_map(
        on_device,
        mesh=mesh,
        in_specs=(
            P("tm", "space", None, None),
            P("space", None, None),
            P("space", None, None),
            P("space", None, None),
            P("space", None, None),
        ),
        out_specs=(P("tm", "space", None, None), P("tm", "space", None, None)),
        check_vma=False,
    )
```

time: 904 us -> 262 us (0.29)
  the two profiles are of different devices: /device:TPU:102 before, /device:TPU:25 now
where the time goes in v1:
time: 262 us; the launch traced here: 259 us
  waiting for transfers between devices  91.9 us (35%)
  blocking collectives  82.7 us (32%)
  starting transfers between devices  47.4 us (18%)
  other arithmetic  27.5 us (10%)
  local copies, waits for them, and re-layouts  8.08 us (3%)
    ppermute x9, waiting for transfers between devices, exchanged(): across = lax.ppermute(jnp.where(even, low, high), 'space', far)  71.1 us
    all_to_all x1, blocking collectives, on_device(): lax.all_to_all(widened.transpose(1, 0, 2, 3), 'tm', 0, 0, tiled=True)  53.2 us
    ppermute x9, starting transfers between devices, exchanged(): across = lax.ppermute(jnp.where(even, low, high), 'space', far)  44.9 us
    all_to_all x1, blocking collectives, on_device(): back = lax.all_to_all(ends, 'tm', 0, 0, tiled=True)  29.6 us
    ppermute x1, waiting for transfers between devices, on_device(): lax.ppermute(end_state, 'tm', [(i, i + 1) for i in range(slices - 1)])  20.8 us
    add x6, other arithmetic, on_device(): centre + d * (total - 6.0 * centre) - c * (centre - upwind) - l * centre + h  8.57 us
  transfers between devices with their start and end apart: 19, of which 9 were waited for; matrix products, arithmetic and copies ran while one was open for 1% of the time, Pallas kernels for 0%

profile of v1, /device:TPU:25, one launch (start us, length us, event | category | flops | bytes accessed | tf_op | source)
XLA Modules:
  0.0 259.3 jit_solution(17604942193942088226)
XLA Ops:
  0.6 2.3 fusion.109
  5.4 5.0 %collective-permute-start.2 = (f32[2624,128]{1,0:T(8,128)S(1)}, f32[2624,128]{1,0:T(8,128)S(1)}, u32[]{:S(2)}, u32[]{:S(2)}) collective-permute-start(f32[2624,128]{1,0:T(8,128)S(1)} %get-tuple-element.15), channel_id=1, source_target_pairs={{1,2},{2,1},{3,4},{4,3},{5,6},{6,5},{7,8},{8,7},{9,10},{10,9},{11,... | collective-permute-start | bytes 4030472 | tf_op jit(solution)/shard_map/ppermute | solution.py:19
  10.6 4.3 %collective-permute-start = (f32[2,512,128]{2,1,0:T(8,128)S(1)}, f32[2,512,128]{2,1,0:T(8,128)S(1)}, u32[]{:S(2)}, u32[]{:S(2)}) collective-permute-start(f32[2,512,128]{2,1,0:T(8,128)S(1)} %get-tuple-element.75), channel_id=1, source_target_pairs={{1,2},{2,1},{3,4},{4,3},{5,6},{6,5},{7,8},{8,7},{9,10},{10,9},{11,... | collective-permute-start | bytes 1572872 | tf_op jit(solution)/shard_map/ppermute | solution.py:19
  15.0 19.0 %collective-permute-done = f32[2,512,128]{2,1,0:T(8,128)S(1)} collective-permute-done((f32[2,512,128]{2,1,0:T(8,128)S(1)}, f32[2,512,128]{2,1,0:T(8,128)S(1)}, u32[]{:S(2)}, u32[]{:S(2)}) %collective-permute-start) | collective-permute-done | bytes 524320 | tf_op jit(solution)/shard_map/ppermute | solution.py:19
  36.7 3.1 %fusion.248 = (f32[6,512,128]{2,1,0:T(8,128)}, f32[6,512,128]{2,1,0:T(8,128)S(1)}) fusion(f32[8,512,128]{2,1,0:T(8,128)S(1)} %pad_maximum_fusion.1, f32[4,6,512,128]{3,2,1,0:T(8,128)S(1)} %pad_maximum_fusion, f32[4,512,128]{2,1,0:T(8,128)S(1)} %bitcast.389, f32[2,512,128]{2,1,0:T(8,128)S(1)} %get-tuple-element.73, f32[2,512,128]{2,1,0:T(8,128)S(1)} %get-tuple-element.74), kind=kLoop, calls=%fused_computation.535 | loop fusion | flops 6684672 | bytes 15204352 | tf_op jit(solution)/shard_map/slice | solution.py:81
  40.7 4.9 %collective-permute-start.4 = (f32[2,512,128]{2,1,0:T(8,128)S(1)}, f32[2,512,128]{2,1,0:T(8,128)S(1)}, u32[]{:S(2)}, u32[]{:S(2)}) collective-permute-start(f32[2,512,128]{2,1,0:T(8,128)S(1)} %get-tuple-element.71), channel_id=1, source_target_pairs={{1,2},{2,1},{3,4},{4,3},{5,6},{6,5},{7,8},{8,7},{9,10},{10,9},{11,... | collective-permute-start | bytes 1572872 | tf_op jit(solution)/shard_map/ppermute | solution.py:19
  45.7 9.1 %collective-permute-done.4 = f32[2,512,128]{2,1,0:T(8,128)S(1)} collective-permute-done((f32[2,512,128]{2,1,0:T(8,128)S(1)}, f32[2,512,128]{2,1,0:T(8,128)S(1)}, u32[]{:S(2)}, u32[]{:S(2)}) %collective-permute-start.4) | collective-permute-done | bytes 524320 | tf_op jit(solution)/shard_map/ppermute | solution.py:19
  57.5 4.9 %collective-permute-start.6 = (f32[2,512,128]{2,1,0:T(8,128)S(1)}, f32[2,512,128]{2,1,0:T(8,128)S(1)}, u32[]{:S(2)}, u32[]{:S(2)}) collective-permute-start(f32[2,512,128]{2,1,0:T(8,128)S(1)} %get-tuple-element.67), channel_id=1, source_target_pairs={{1,2},{2,1},{3,4},{4,3},{5,6},{6,5},{7,8},{8,7},{9,10},{10,9},{11,... | collective-permute-start | bytes 1572872 | tf_op jit(solution)/shard_map/ppermute | solution.py:19
  62.5 9.1 %collective-permute-done.6 = f32[2,512,128]{2,1,0:T(8,128)S(1)} collective-permute-done((f32[2,512,128]{2,1,0:T(8,128)S(1)}, f32[2,512,128]{2,1,0:T(8,128)S(1)}, u32[]{:S(2)}, u32[]{:S(2)}) %collective-permute-start.6) | collective-permute-done | bytes 524320 | tf_op jit(solution)/shard_map/ppermute | solution.py:19
  76.3 4.9 %collective-permute-start.8 = (f32[2,512,128]{2,1,0:T(8,128)}, f32[2,512,128]{2,1,0:T(8,128)}, u32[]{:S(2)}, u32[]{:S(2)}) collective-permute-start(f32[2,512,128]{2,1,0:T(8,128)} %get-tuple-element.63), channel_id=1, source_target_pairs={{1,2},{2,1},{3,4},{4,3},{5,6},{6,5},{7,8},{8,7},{9,10},{10,9},{11,... | collective-permute-start | bytes 1572872 | tf_op jit(solution)/shard_map/ppermute | solution.py:19
  81.5 9.3 %collective-permute-done.8 = f32[2,512,128]{2,1,0:T(8,128)} collective-permute-done((f32[2,512,128]{2,1,0:T(8,128)}, f32[2,512,128]{2,1,0:T(8,128)}, u32[]{:S(2)}, u32[]{:S(2)}) %collective-permute-start.8) | collective-permute-done | bytes 524320 | tf_op jit(solution)/shard_map/ppermute | solution.py:19
  94.2 3.0 %fusion.40 = f32[6,512,128]{2,1,0:T(8,128)S(1)} fusion(f32[8,512,128]{2,1,0:T(8,128)S(1)} %pad_maximum_fusion.4, f32[2,512,128]{2,1,0:T(8,128)S(1)} %get-tuple-element.62, f32[4,512,128]{2,1,0:T(8,128)} %copy-done.10, f32[2,512,128]{2,1,0:T(8,128)S(1)} %get-tuple-element.61, f32[4,6,512,128]{3,2,1,0:T(8,128)S(1)} %copy-done.1), kind=kLoop, calls=%fused_computation.92 | loop fusion | flops 6684672 | bytes 13631488 | tf_op jit(solution)/shard_map/add | solution.py:84
  97.2 2.3 subtract_select_fusion
  100.0 53.2 %all_to_all.10 = f32[16,4,64,128]{3,2,1,0:T(8,128)S(1)} all-to-all(f32[16,4,64,128]{3,2,1,0:T(8,128)S(1)} %copy_bitcast_fusion), channel_id=1, replica_groups=mesh['tm'=16,'space'=16] {'tm'}, dimensions={0} | all-to-all | bytes 4194304 | tf_op jit(solution)/shard_map/all_to_all | solution.py:91
  153.7 5.2 %collective-permute-start.10 = (f32[28,64,128]{2,1,0:T(8,128)S(1)}, f32[28,64,128]{2,1,0:T(8,128)S(1)}, u32[]{:S(2)}, u32[]{:S(2)}) collective-permute-start(f32[28,64,128]{2,1,0:T(8,128)S(1)} %get-tuple-element.57), channel_id=1, source_target_pairs={{1,2},{2,1},{3,4},{4,3},{5,6},{6,5},{7,8},{8,7},{9,10},{10,9},{11,... | collective-permute-start | bytes 2752520 | tf_op jit(solution)/shard_map/ppermute | solution.py:19
  161.3 10.7 %collective-permute-done.10 = f32[28,64,128]{2,1,0:T(8,128)S(1)} collective-permute-done((f32[28,64,128]{2,1,0:T(8,128)S(1)}, f32[28,64,128]{2,1,0:T(8,128)S(1)}, u32[]{:S(2)}, u32[]{:S(2)}) %collective-permute-start.10) | collective-permute-done | bytes 917536 | tf_op jit(solution)/shard_map/ppermute | solution.py:19
  173.4 5.2 %collective-permute-start.12 = (f32[4,64,128]{2,1,0:T(8,128)S(1)}, f32[4,64,128]{2,1,0:T(8,128)S(1)}, u32[]{:S(2)}, u32[]{:S(2)}) collective-permute-start(f32[4,64,128]{2,1,0:T(8,128)S(1)} %get-tuple-element.7), channel_id=1, source_target_pairs={{1,2},{2,1},{3,4},{4,3},{5,6},{6,5},{7,8},{8,7},{9,10},{10,9},{11,... | collective-permute-start | bytes 393224 | tf_op jit(solution)/shard_map/ppermute | solution.py:19
  178.7 4.6 %collective-permute-done.12 = f32[4,64,128]{2,1,0:T(8,128)S(1)} collective-permute-done((f32[4,64,128]{2,1,0:T(8,128)S(1)}, f32[4,64,128]{2,1,0:T(8,128)S(1)}, u32[]{:S(2)}, u32[]{:S(2)}) %collective-permute-start.12) | collective-permute-done | bytes 131104 | tf_op jit(solution)/shard_map/ppermute | solution.py:19
  184.4 5.2 %collective-permute-start.14 = (f32[4,64,128]{2,1,0:T(8,128)S(1)}, f32[4,64,128]{2,1,0:T(8,128)S(1)}, u32[]{:S(2)}, u32[]{:S(2)}) collective-permute-start(f32[4,64,128]{2,1,0:T(8,128)S(1)} %get-tuple-element.5), channel_id=1, source_target_pairs={{1,2},{2,1},{3,4},{4,3},{5,6},{6,5},{7,8},{8,7},{9,10},{10,9},{11,... | collective-permute-start | bytes 393224 | tf_op jit(solution)/shard_map/ppermute | solution.py:19
  189.6 4.6 %collective-permute-done.14 = f32[4,64,128]{2,1,0:T(8,128)S(1)} collective-permute-done((f32[4,64,128]{2,1,0:T(8,128)S(1)}, f32[4,64,128]{2,1,0:T(8,128)S(1)}, u32[]{:S(2)}, u32[]{:S(2)}) %collective-permute-start.14) | collective-permute-done | bytes 131104 | tf_op jit(solution)/shard_map/ppermute | solution.py:19
  195.3 5.2 %collective-permute-start.16 = (f32[4,64,128]{2,1,0:T(8,128)S(1)}, f32[4,64,128]{2,1,0:T(8,128)S(1)}, u32[]{:S(2)}, u32[]{:S(2)}) collective-permute-start(f32[4,64,128]{2,1,0:T(8,128)S(1)} %get-tuple-element.3), channel_id=1, source_target_pairs={{1,2},{2,1},{3,4},{4,3},{5,6},{6,5},{7,8},{8,7},{9,10},{10,9},{11,... | collective-permute-start | bytes 393224 | tf_op jit(solution)/shard_map/ppermute | solution.py:19
  200.7 4.6 %collective-permute-done.16 = f32[4,64,128]{2,1,0:T(8,128)S(1)} collective-permute-done((f32[4,64,128]{2,1,0:T(8,128)S(1)}, f32[4,64,128]{2,1,0:T(8,128)S(1)}, u32[]{:S(2)}, u32[]{:S(2)}) %collective-permute-start.16) | collective-permute-done | bytes 131104 | tf_op jit(solution)/shard_map/ppermute | solution.py:19
  206.2 29.6 %all_to_all.11 = f32[16,4,32,128]{3,2,1,0:T(8,128)S(1)} all-to-all(f32[16,4,32,128]{3,2,1,0:T(8,128)S(1)} %slice.1425), channel_id=1, replica_groups=mesh['tm'=16,'space'=16] {'tm'}, dimensions={0} | all-to-all | bytes 2097152 | tf_op jit(solution)/shard_map/all_to_all | solution.py:119
  237.4 20.8 %collective-permute-done.18 = f32[4,512,128]{2,1,0:T(8,128)S(1)} collective-permute-done((f32[4,512,128]{2,1,0:T(8,128)S(1)}, f32[4,512,128]{2,1,0:T(8,128)S(1)}, u32[]{:S(2)}, u32[]{:S(2)}) %collective-permute-start.18) | collective-permute-done | bytes 1048608 | tf_op jit(solution)/shard_map/ppermute | solution.py:121
  (150 shorter events, 27.4 us)
Async XLA Ops:
  5.2 5.3 %copy-start.7 = (f32[1,4,512,128]{3,2,1,0:T(8,128)S(1)}, f32[1,4,512,128]{3,2,1,0:T(8,128)}, u32[]{:S(2)}) copy-start(f32[1,4,512,128]{3,2,1,0:T(8,128)} %param.5) | copy-start | bytes 3145732
  5.4 28.9 %collective-permute-start.2 = (f32[2624,128]{1,0:T(8,128)S(1)}, f32[2624,128]{1,0:T(8,128)S(1)}, u32[]{:S(2)}, u32[]{:S(2)}) collective-permute-start(f32[2624,128]{1,0:T(8,128)S(1)} %get-tuple-element.15), channel_id=1, source_target_pairs={{1,2},{2,1},{3,4},{4,3},{5,6},{6,5},{7,8},{8,7},{9,10},{10,9},{11,... | collective-permute-start | bytes 4030472 | tf_op jit(solution)/shard_map/ppermute | solution.py:19
  10.4 23.9 %collective-permute-start.3 = (f32[2624,128]{1,0:T(8,128)S(1)}, f32[2624,128]{1,0:T(8,128)S(1)}, u32[]{:S(2)}, u32[]{:S(2)}) collective-permute-start(f32[2624,128]{1,0:T(8,128)S(1)} %get-tuple-element.16), channel_id=1, source_target_pairs={{0,1},{1,0},{2,3},{3,2},{4,5},{5,4},{6,7},{7,6},{8,9},{9,8},{10,11... | collective-permute-start | bytes 4030472 | tf_op jit(solution)/shard_map/ppermute | solution.py:20
  10.6 23.4 %collective-permute-start = (f32[2,512,128]{2,1,0:T(8,128)S(1)}, f32[2,512,128]{2,1,0:T(8,128)S(1)}, u32[]{:S(2)}, u32[]{:S(2)}) collective-permute-start(f32[2,512,128]{2,1,0:T(8,128)S(1)} %get-tuple-element.75), channel_id=1, source_target_pairs={{1,2},{2,1},{3,4},{4,3},{5,6},{6,5},{7,8},{8,7},{9,10},{10,9},{11,... | collective-permute-start | bytes 1572872 | tf_op jit(solution)/shard_map/ppermute | solution.py:19
  14.9 19.1 %collective-permute-start.1 = (f32[2,512,128]{2,1,0:T(8,128)S(1)}, f32[2,512,128]{2,1,0:T(8,128)S(1)}, u32[]{:S(2)}, u32[]{:S(2)}) collective-permute-start(f32[2,512,128]{2,1,0:T(8,128)S(1)} %get-tuple-element.76), channel_id=1, source_target_pairs={{0,1},{1,0},{2,3},{3,2},{4,5},{5,4},{6,7},{7,6},{8,9},{9,8},{10,11... | collective-permute-start | bytes 1572872 | tf_op jit(solution)/shard_map/ppermute | solution.py:20
  36.7 35.2 %copy-start = (f32[4,6,512,128]{3,2,1,0:T(8,128)}, f32[4,6,512,128]{3,2,1,0:T(8,128)S(1)}, u32[]{:S(2)}) copy-start(f32[4,6,512,128]{3,2,1,0:T(8,128)S(1)} %pad_maximum_fusion) | copy-start | bytes 18874372
  40.7 14.1 %collective-permute-start.4 = (f32[2,512,128]{2,1,0:T(8,128)S(1)}, f32[2,512,128]{2,1,0:T(8,128)S(1)}, u32[]{:S(2)}, u32[]{:S(2)}) collective-permute-start(f32[2,512,128]{2,1,0:T(8,128)S(1)} %get-tuple-element.71), channel_id=1, source_target_pairs={{1,2},{2,1},{3,4},{4,3},{5,6},{6,5},{7,8},{8,7},{9,10},{10,9},{11,... | collective-permute-start | bytes 1572872 | tf_op jit(solution)/shard_map/ppermute | solution.py:19
  45.6 9.2 %collective-permute-start.5 = (f32[2,512,128]{2,1,0:T(8,128)S(1)}, f32[2,512,128]{2,1,0:T(8,128)S(1)}, u32[]{:S(2)}, u32[]{:S(2)}) collective-permute-start(f32[2,512,128]{2,1,0:T(8,128)S(1)} %get-tuple-element.72), channel_id=1, source_target_pairs={{0,1},{1,0},{2,3},{3,2},{4,5},{5,4},{6,7},{7,6},{8,9},{9,8},{10,11... | collective-permute-start | bytes 1572872 | tf_op jit(solution)/shard_map/ppermute | solution.py:20
  57.5 14.1 %collective-permute-start.6 = (f32[2,512,128]{2,1,0:T(8,128)S(1)}, f32[2,512,128]{2,1,0:T(8,128)S(1)}, u32[]{:S(2)}, u32[]{:S(2)}) collective-permute-start(f32[2,512,128]{2,1,0:T(8,128)S(1)} %get-tuple-element.67), channel_id=1, source_target_pairs={{1,2},{2,1},{3,4},{4,3},{5,6},{6,5},{7,8},{8,7},{9,10},{10,9},{11,... | collective-permute-start | bytes 1572872 | tf_op jit(solution)/shard_map/ppermute | solution.py:19
  62.4 9.2 %collective-permute-start.7 = (f32[2,512,128]{2,1,0:T(8,128)S(1)}, f32[2,512,128]{2,1,0:T(8,128)S(1)}, u32[]{:S(2)}, u32[]{:S(2)}) collective-permute-start(f32[2,512,128]{2,1,0:T(8,128)S(1)} %get-tuple-element.68), channel_id=1, source_target_pairs={{0,1},{1,0},{2,3},{3,2},{4,5},{5,4},{6,7},{7,6},{8,9},{9,8},{10,11... | collective-permute-start | bytes 1572872 | tf_op jit(solution)/shard_map/ppermute | solution.py:20
  76.3 14.4 %collective-permute-start.8 = (f32[2,512,128]{2,1,0:T(8,128)}, f32[2,512,128]{2,1,0:T(8,128)}, u32[]{:S(2)}, u32[]{:S(2)}) collective-permute-start(f32[2,512,128]{2,1,0:T(8,128)} %get-tuple-element.63), channel_id=1, source_target_pairs={{1,2},{2,1},{3,4},{4,3},{5,6},{6,5},{7,8},{8,7},{9,10},{10,9},{11,... | collective-permute-start | bytes 1572872 | tf_op jit(solution)/shard_map/ppermute | solution.py:19
  81.2 9.6 %collective-permute-start.9 = (f32[2,512,128]{2,1,0:T(8,128)}, f32[2,512,128]{2,1,0:T(8,128)}, u32[]{:S(2)}, u32[]{:S(2)}) collective-permute-start(f32[2,512,128]{2,1,0:T(8,128)} %get-tuple-element.64), channel_id=1, source_target_pairs={{0,1},{1,0},{2,3},{3,2},{4,5},{5,4},{6,7},{7,6},{8,9},{9,8},{10,11... | collective-permute-start | bytes 1572872 | tf_op jit(solution)/shard_map/ppermute | solution.py:20
  90.7 3.4 %copy-start.1 = (f32[4,6,512,128]{3,2,1,0:T(8,128)S(1)}, f32[4,6,512,128]{3,2,1,0:T(8,128)}, u32[]{:S(2)}) copy-start(f32[4,6,512,128]{3,2,1,0:T(8,128)} %copy-done) | copy-start | bytes 18874372
  153.7 18.3 %collective-permute-start.10 = (f32[28,64,128]{2,1,0:T(8,128)S(1)}, f32[28,64,128]{2,1,0:T(8,128)S(1)}, u32[]{:S(2)}, u32[]{:S(2)}) collective-permute-start(f32[28,64,128]{2,1,0:T(8,128)S(1)} %get-tuple-element.57), channel_id=1, source_target_pairs={{1,2},{2,1},{3,4},{4,3},{5,6},{6,5},{7,8},{8,7},{9,10},{10,9},{11,... | collective-permute-start | bytes 2752520 | tf_op jit(solution)/shard_map/ppermute | solution.py:19
  158.9 13.1 %collective-permute-start.11 = (f32[28,64,128]{2,1,0:T(8,128)S(1)}, f32[28,64,128]{2,1,0:T(8,128)S(1)}, u32[]{:S(2)}, u32[]{:S(2)}) collective-permute-start(f32[28,64,128]{2,1,0:T(8,128)S(1)} %get-tuple-element.58), channel_id=1, source_target_pairs={{0,1},{1,0},{2,3},{3,2},{4,5},{5,4},{6,7},{7,6},{8,9},{9,8},{10,11... | collective-permute-start | bytes 2752520 | tf_op jit(solution)/shard_map/ppermute | solution.py:20
  173.3 5.4 %collective-permute-start.13 = (f32[4,64,128]{2,1,0:T(8,128)S(1)}, f32[4,64,128]{2,1,0:T(8,128)S(1)}, u32[]{:S(2)}, u32[]{:S(2)}) collective-permute-start(f32[4,64,128]{2,1,0:T(8,128)S(1)} %get-tuple-element.7), channel_id=1, source_target_pairs={{0,1},{1,0},{2,3},{3,2},{4,5},{5,4},{6,7},{7,6},{8,9},{9,8},{10,11... | collective-permute-start | bytes 393224 | tf_op jit(solution)/shard_map/ppermute | solution.py:20
  173.4 9.9 %collective-permute-start.12 = (f32[4,64,128]{2,1,0:T(8,128)S(1)}, f32[4,64,128]{2,1,0:T(8,128)S(1)}, u32[]{:S(2)}, u32[]{:S(2)}) collective-permute-start(f32[4,64,128]{2,1,0:T(8,128)S(1)} %get-tuple-element.7), channel_id=1, source_target_pairs={{1,2},{2,1},{3,4},{4,3},{5,6},{6,5},{7,8},{8,7},{9,10},{10,9},{11,... | collective-permute-start | bytes 393224 | tf_op jit(solution)/shard_map/ppermute | solution.py:19
  184.3 5.4 %collective-permute-start.15 = (f32[4,64,128]{2,1,0:T(8,128)S(1)}, f32[4,64,128]{2,1,0:T(8,128)S(1)}, u32[]{:S(2)}, u32[]{:S(2)}) collective-permute-start(f32[4,64,128]{2,1,0:T(8,128)S(1)} %get-tuple-element.5), channel_id=1, source_target_pairs={{0,1},{1,0},{2,3},{3,2},{4,5},{5,4},{6,7},{7,6},{8,9},{9,8},{10,11... | collective-permute-start | bytes 393224 | tf_op jit(solution)/shard_map/ppermute | solution.py:20
  184.4 9.9 %collective-permute-start.14 = (f32[4,64,128]{2,1,0:T(8,128)S(1)}, f32[4,64,128]{2,1,0:T(8,128)S(1)}, u32[]{:S(2)}, u32[]{:S(2)}) collective-permute-start(f32[4,64,128]{2,1,0:T(8,128)S(1)} %get-tuple-element.5), channel_id=1, source_target_pairs={{1,2},{2,1},{3,4},{4,3},{5,6},{6,5},{7,8},{8,7},{9,10},{10,9},{11,... | collective-permute-start | bytes 393224 | tf_op jit(solution)/shard_map/ppermute | solution.py:19
  195.2 5.4 %collective-permute-start.17 = (f32[4,64,128]{2,1,0:T(8,128)S(1)}, f32[4,64,128]{2,1,0:T(8,128)S(1)}, u32[]{:S(2)}, u32[]{:S(2)}) collective-permute-start(f32[4,64,128]{2,1,0:T(8,128)S(1)} %get-tuple-element.3), channel_id=1, source_target_pairs={{0,1},{1,0},{2,3},{3,2},{4,5},{5,4},{6,7},{7,6},{8,9},{9,8},{10,11... | collective-permute-start | bytes 393224 | tf_op jit(solution)/shard_map/ppermute | solution.py:20
  195.3 9.9 %collective-permute-start.16 = (f32[4,64,128]{2,1,0:T(8,128)S(1)}, f32[4,64,128]{2,1,0:T(8,128)S(1)}, u32[]{:S(2)}, u32[]{:S(2)}) collective-permute-start(f32[4,64,128]{2,1,0:T(8,128)S(1)} %get-tuple-element.3), channel_id=1, source_target_pairs={{1,2},{2,1},{3,4},{4,3},{5,6},{6,5},{7,8},{8,7},{9,10},{10,9},{11,... | collective-permute-start | bytes 393224 | tf_op jit(solution)/shard_map/ppermute | solution.py:19
  235.8 22.4 %copy-start.9 = (f32[1,4,512,128]{3,2,1,0:T(8,128)S(1)}, f32[1,4,512,128]{3,2,1,0:T(8,128)}, u32[]{:S(2)}) copy-start(f32[1,4,512,128]{3,2,1,0:T(8,128)} %param.5) | copy-start | bytes 3145732
  235.9 23.4 %copy-start.18 = (f32[16,4,32,128]{3,2,0,1:T(8,128)}, f32[16,4,32,128]{3,2,0,1:T(8,128)S(1)}, u32[]{:S(2)}) copy-start(f32[16,4,32,128]{3,2,0,1:T(8,128)S(1)} %copy.29) | copy-start | bytes 3145732
  235.9 22.3 %collective-permute-start.18 = (f32[4,512,128]{2,1,0:T(8,128)S(1)}, f32[4,512,128]{2,1,0:T(8,128)S(1)}, u32[]{:S(2)}, u32[]{:S(2)}) collective-permute-start(f32[4,512,128]{2,1,0:T(8,128)S(1)} %bitcast.400), channel_id=1, source_target_pairs={{0,16},{16,32},{32,48},{48,64},{64,80},{80,96},{96,112},{112,128},... | collective-permute-start | bytes 3145736 | tf_op jit(solution)/shard_map/ppermute | solution.py:121
  (14 other events, 30.5 us)

commit v2 on v1

--- a/solution.py
+++ b/solution.py
@@ -6,6 +6,7 @@
 FINE = 8
 SPAN = 4
 ROUNDS = 2
+STREAMS = 2
 
 
 def swaps(pairs):
@@ -39,52 +40,73 @@
     halo = slices
     window = part + 2 * halo
 
-    denom = 1.0 + FINE * (6.0 * diffusion + courant + loss)
-    own = 1.0 / denom
-    side = FINE * diffusion / denom
-    west = FINE * courant / denom
-
-    fine_terms = jnp.stack([diffusion, courant, loss, heating])
-    tall = jnp.pad(jnp.stack([own, side, west]), ((0, 0), (0, 0), (halo, halo), (0, 0)))
-    coarse_terms = lax.dynamic_slice_in_dim(tall, slot * part, window, axis=2)
     deep = SPAN - 1
     edge = ROUNDS - 1
+    fine_terms = (diffusion, courant, loss, heating)
+
+    def cut_window(x):
+        tall = jnp.pad(x, ((0, 0), (halo, halo), (0, 0)))
+        return lax.dynamic_slice_in_dim(tall, slot * part, window, axis=1)
 
     def flat(*arrays):
         return jnp.concatenate([a.reshape(-1, lanes) for a in arrays])
 
-    before, after = exchanged(
-        flat(fine_terms[:, :edge], coarse_terms[:, :deep]),
-        flat(fine_terms[:, planes - edge :], coarse_terms[:, planes - deep :]),
-        even,
-    )
-    cut = 4 * edge * rows
+    coarse_terms = [cut_window(x) for x in fine_terms[:3]]
+    half = rows // STREAMS
+    bounds = [(max(0, i * half - FINE), min(rows, (i + 1) * half + FINE)) for i in range(STREAMS)]
+    starts = [start[:, lo:hi] for lo, hi in bounds]
 
-    def fine_part(x):
-        return x[:cut].reshape(4, edge, rows, lanes)
+    def edges(x, width):
+        return x[:width], x[x.shape[0] - width :]
 
-    def coarse_part(x):
-        return x[cut:].reshape(3, deep, window, lanes)
+    ends_of = [edges(x, edge) for x in fine_terms] + [edges(x, deep) for x in coarse_terms] + [edges(starts[0], ROUNDS)]
+    before, after = exchanged(flat(*[x for x, _ in ends_of]), flat(*[x for _, x in ends_of]), even)
 
-    fine_terms = jnp.concatenate([fine_part(before), fine_terms, fine_part(after)], axis=1)
-    coarse_terms = jnp.concatenate([coarse_part(before), coarse_terms, coarse_part(after)], axis=1)
+    def split(x):
+        out, at = [], 0
+        for piece, _ in ends_of:
+            size = piece.shape[0] * piece.shape[1]
+            out.append(x[at : at + size].reshape(piece.shape))
+            at += size
+        return out
 
-    state = start
-    first = None
-    for _ in range(FINE // ROUNDS):
-        before, after = exchanged(state[:ROUNDS], state[planes - ROUNDS :], even)
-        state = jnp.concatenate([before, state, after])
-        if first is None:
-            first = state[ROUNDS - 1 : ROUNDS + planes + 1]
-        for step in range(ROUNDS):
-            total, upwind = around(state)
-            centre = state[1:-1]
-            trim = step
-            d, c, l, h = (t[trim : t.shape[0] - trim] for t in fine_terms)
-            state = centre + d * (total - 6.0 * centre) - c * (centre - upwind) - l * centre + h
-    total, upwind = around(first)
-    coarse_old = own * start + side * total + west * upwind
-    element = jnp.where(slot > 0, state - coarse_old, state)
+    wide = [jnp.concatenate([lo, x, hi]) for lo, x, hi in zip(split(before), list(fine_terms) + coarse_terms + [starts[0]], split(after))]
+    fine_wide, coarse_wide, firsts = wide[:4], wide[4:7], [wide[7]]
+    for x in starts[1:]:
+        before, after = exchanged(*edges(x, ROUNDS), even)
+        firsts.append(jnp.concatenate([before, x, after]))
+
+    def coarse_factors(d, c, l, inside=1.0):
+        denom = 1.0 + FINE * (6.0 * d + c + l)
+        return inside / denom, FINE * d / denom, FINE * c / denom
+
+    states = list(firsts)
+    for turn in range(FINE // ROUNDS):
+        for i, (lo, hi) in enumerate(bounds):
+            state = states[i]
+            if turn:
+                before, after = exchanged(*edges(state, ROUNDS), even)
+                state = jnp.concatenate([before, state, after])
+            for step in range(ROUNDS):
+                total, upwind = around(state)
+                centre = state[1:-1]
+                d, c, l, h = (t[step : t.shape[0] - step, lo:hi] for t in fine_wide)
+                state = centre + d * (total - 6.0 * centre) - c * (centre - upwind) - l * centre + h
+            states[i] = state
+
+    elements = []
+    for i, (lo, hi) in enumerate(bounds):
+        total, upwind = around(firsts[i][ROUNDS - 1 : ROUNDS + planes + 1])
+        o, s, w = coarse_factors(*(x[:, lo:hi] for x in fine_terms[:3]))
+        old = o * starts[i] + s * total + w * upwind
+        element = jnp.where(slot > 0, states[i] - old, states[i])
+        elements.append(element[:, i * half - lo : (i + 1) * half - lo])
+    element = jnp.concatenate(elements, axis=1)
+
+    line = slot * part - halo + lax.broadcasted_iota(jnp.int32, (1, window, 1), 1)
+    place = lax.axis_index("space") * planes - deep + lax.broadcasted_iota(jnp.int32, (planes + 2 * deep, 1, 1), 0)
+    inside = (line >= 0) & (line < rows) & (place >= 0) & (place < planes * lax.axis_size("space"))
+    coarse_terms = coarse_factors(*coarse_wide, inside=inside.astype(jnp.float32))
 
     blocks = jnp.pad(element, ((0, 0), (halo, halo), (0, 0))).reshape(planes, -1, part, lanes)
     widened = jnp.concatenate([blocks[:, :-1], blocks[:, 1:]], axis=2)

time: 262 us -> 291 us (1.11)
  blocking collectives: 82.7 us -> 31 us
  waiting for transfers between devices: 91.9 us -> 131 us
  starting transfers between devices: 47.4 us -> 69.5 us
  local copies, waits for them, and re-layouts: 8.08 us -> 25.4 us
    all_to_all x1 -> x0, blocking collectives: 53.2 us -> none  [on_device(): lax.all_to_all(widened.transpose(1, 0, 2, 3), 'tm', 0, 0, tiled=True)]
    all_to_all x0 -> x1, waiting for transfers between devices: none -> 44.9 us  [on_device(): lax.all_to_all(widened.transpose(1, 0, 2, 3), 'tm', 0, 0, tiled=True)]
    unnamed x63 -> x58, local copies, waits for them, and re-layouts: 5.1 us -> 17.7 us
    ppermute x9 -> x12, starting transfers between devices: 44.9 us -> 57.4 us  [exchanged(): across = lax.ppermute(jnp.where(even, low, high), 'space', far)]
    all_to_all x0 -> x1, starting transfers between devices: none -> 9.29 us  [on_device(): lax.all_to_all(widened.transpose(1, 0, 2, 3), 'tm', 0, 0, tiled=True)]
    ppermute x9 -> x12, waiting for transfers between devices: 71.1 us -> 65.4 us  [exchanged(): across = lax.ppermute(jnp.where(even, low, high), 'space', far)]
    add x6 -> x10, other arithmetic: 8.57 us -> 7.81 us  [on_device(): centre + d * (total - 6.0 * centre) - c * (centre - upwind) - l * centre + h]
  transfers between devices with their start and end apart: 19 -> 26, of which waited for: 9 -> 13; matrix products, arithmetic and copies ran while one was open for 1% -> 3% of each run, Pallas kernels for 0% -> 0%
where the time goes in v2:
time: 291 us; the launch traced here: 287 us
  waiting for transfers between devices  131 us (45%)
  starting transfers between devices  69.5 us (24%)
  blocking collectives  31 us (11%)
  other arithmetic  27.9 us (10%)
  local copies, waits for them, and re-layouts  25.4 us (9%)
    ppermute x12, waiting for transfers between devices, exchanged(): across = lax.ppermute(jnp.where(even, low, high), 'space', far)  65.4 us
    ppermute x12, starting transfers between devices, exchanged(): across = lax.ppermute(jnp.where(even, low, high), 'space', far)  57.4 us
    all_to_all x1, waiting for transfers between devices, on_device(): lax.all_to_all(widened.transpose(1, 0, 2, 3), 'tm', 0, 0, tiled=True)  44.9 us
    all_to_all x1, blocking collectives, on_device(): back = lax.all_to_all(ends, 'tm', 0, 0, tiled=True)  31 us
    ppermute x1, waiting for transfers between devices, on_device(): lax.ppermute(end_state, 'tm', [(i, i + 1) for i in range(slices - 1)])  20.8 us
    unnamed x58, local copies, waits for them, and re-layouts  17.7 us
    all_to_all x1, starting transfers between devices, on_device(): lax.all_to_all(widened.transpose(1, 0, 2, 3), 'tm', 0, 0, tiled=True)  9.29 us
    add x10, other arithmetic, on_device(): centre + d * (total - 6.0 * centre) - c * (centre - upwind) - l * centre + h  7.81 us
  transfers between devices with their start and end apart: 26, of which 13 were waited for; matrix products, arithmetic and copies ran while one was open for 3% of the time, Pallas kernels for 0%

profile of v2, /device:TPU:25, one launch (start us, length us, event | category | flops | bytes accessed | tf_op | source)
XLA Modules:
  0.0 286.8 jit_solution(1100597094179455701)
XLA Ops:
  7.9 4.9 %collective-permute-start = (f32[3152,128]{1,0:T(8,128)}, f32[3152,128]{1,0:T(8,128)}, u32[]{:S(2)}, u32[]{:S(2)}) collective-permute-start(f32[3152,128]{1,0:T(8,128)} %get-tuple-element.22), channel_id=1, source_target_pairs={{1,2},{2,1},{3,4},{4,3},{5,6},{6,5},{7,8},{8,7},{9,10},{10,9},{11,... | collective-permute-start | bytes 4841480 | tf_op jit(solution)/shard_map/ppermute | solution.py:20
  12.9 4.3 %collective-permute-start.8 = (f32[2,264,128]{2,1,0:T(8,128)}, f32[2,264,128]{2,1,0:T(8,128)}, u32[]{:S(2)}, u32[]{:S(2)}) collective-permute-start(f32[2,264,128]{2,1,0:T(8,128)} %get-tuple-element.100), channel_id=1, source_target_pairs={{1,2},{2,1},{3,4},{4,3},{5,6},{6,5},{7,8},{8,7},{9,10},{10,9},{11,... | collective-permute-start | bytes 811016 | tf_op jit(solution)/shard_map/ppermute | solution.py:20
  18.6 18.3 %collective-permute-done.8 = f32[2,264,128]{2,1,0:T(8,128)} collective-permute-done((f32[2,264,128]{2,1,0:T(8,128)}, f32[2,264,128]{2,1,0:T(8,128)}, u32[]{:S(2)}, u32[]{:S(2)}) %collective-permute-start.8) | collective-permute-done | bytes 270368 | tf_op jit(solution)/shard_map/ppermute | solution.py:20
  45.1 4.9 %collective-permute-start.2 = (f32[2,264,128]{2,1,0:T(8,128)S(1)}, f32[2,264,128]{2,1,0:T(8,128)S(1)}, u32[]{:S(2)}, u32[]{:S(2)}) collective-permute-start(f32[2,264,128]{2,1,0:T(8,128)S(1)} %get-tuple-element.160), channel_id=1, source_target_pairs={{1,2},{2,1},{3,4},{4,3},{5,6},{6,5},{7,8},{8,7},{9,10},{10,9},{11,... | collective-permute-start | bytes 811016 | tf_op jit(solution)/shard_map/ppermute | solution.py:20
  50.8 5.7 %collective-permute-done.2 = f32[2,264,128]{2,1,0:T(8,128)S(1)} collective-permute-done((f32[2,264,128]{2,1,0:T(8,128)S(1)}, f32[2,264,128]{2,1,0:T(8,128)S(1)}, u32[]{:S(2)}, u32[]{:S(2)}) %collective-permute-start.2) | collective-permute-done | bytes 270368 | tf_op jit(solution)/shard_map/ppermute | solution.py:20
  58.3 4.9 %collective-permute-start.10 = (f32[2,264,128]{2,1,0:T(8,128)S(1)}, f32[2,264,128]{2,1,0:T(8,128)S(1)}, u32[]{:S(2)}, u32[]{:S(2)}) collective-permute-start(f32[2,264,128]{2,1,0:T(8,128)S(1)} %get-tuple-element.172), channel_id=1, source_target_pairs={{1,2},{2,1},{3,4},{4,3},{5,6},{6,5},{7,8},{8,7},{9,10},{10,9},{11,... | collective-permute-start | bytes 811016 | tf_op jit(solution)/shard_map/ppermute | solution.py:20
  63.7 4.3 %collective-permute-start.4 = (f32[2,264,128]{2,1,0:T(8,128)S(1)}, f32[2,264,128]{2,1,0:T(8,128)S(1)}, u32[]{:S(2)}, u32[]{:S(2)}) collective-permute-start(f32[2,264,128]{2,1,0:T(8,128)S(1)} %get-tuple-element.156), channel_id=1, source_target_pairs={{1,2},{2,1},{3,4},{4,3},{5,6},{6,5},{7,8},{8,7},{9,10},{10,9},{11,... | collective-permute-start | bytes 811016 | tf_op jit(solution)/shard_map/ppermute | solution.py:20
  70.6 4.5 %collective-permute-done.4 = f32[2,264,128]{2,1,0:T(8,128)S(1)} collective-permute-done((f32[2,264,128]{2,1,0:T(8,128)S(1)}, f32[2,264,128]{2,1,0:T(8,128)S(1)}, u32[]{:S(2)}, u32[]{:S(2)}) %collective-permute-start.4) | collective-permute-done | bytes 270368 | tf_op jit(solution)/shard_map/ppermute | solution.py:20
  77.0 4.3 %collective-permute-start.12 = (f32[2,264,128]{2,1,0:T(8,128)S(1)}, f32[2,264,128]{2,1,0:T(8,128)S(1)}, u32[]{:S(2)}, u32[]{:S(2)}) collective-permute-start(f32[2,264,128]{2,1,0:T(8,128)S(1)} %get-tuple-element.168), channel_id=1, source_target_pairs={{1,2},{2,1},{3,4},{4,3},{5,6},{6,5},{7,8},{8,7},{9,10},{10,9},{11,... | collective-permute-start | bytes 811016 | tf_op jit(solution)/shard_map/ppermute | solution.py:20
  81.8 4.9 %collective-permute-start.6 = (f32[2,264,128]{2,1,0:T(8,128)S(1)}, f32[2,264,128]{2,1,0:T(8,128)S(1)}, u32[]{:S(2)}, u32[]{:S(2)}) collective-permute-start(f32[2,264,128]{2,1,0:T(8,128)S(1)} %get-tuple-element.152), channel_id=1, source_target_pairs={{1,2},{2,1},{3,4},{4,3},{5,6},{6,5},{7,8},{8,7},{9,10},{10,9},{11,... | collective-permute-start | bytes 811016 | tf_op jit(solution)/shard_map/ppermute | solution.py:20
  95.0 4.9 %collective-permute-start.14 = (f32[2,264,128]{2,1,0:T(8,128)S(1)}, f32[2,264,128]{2,1,0:T(8,128)S(1)}, u32[]{:S(2)}, u32[]{:S(2)}) collective-permute-start(f32[2,264,128]{2,1,0:T(8,128)S(1)} %get-tuple-element.164), channel_id=1, source_target_pairs={{1,2},{2,1},{3,4},{4,3},{5,6},{6,5},{7,8},{8,7},{9,10},{10,9},{11,... | collective-permute-start | bytes 811016 | tf_op jit(solution)/shard_map/ppermute | solution.py:20
  100.4 6.1 %collective-permute-done.14 = f32[2,264,128]{2,1,0:T(8,128)S(1)} collective-permute-done((f32[2,264,128]{2,1,0:T(8,128)S(1)}, f32[2,264,128]{2,1,0:T(8,128)S(1)}, u32[]{:S(2)}, u32[]{:S(2)}) %collective-permute-start.14) | collective-permute-done | bytes 270368 | tf_op jit(solution)/shard_map/ppermute | solution.py:20
  109.9 9.3 %all-to-all-start = ((f32[16,4,64,128]{3,2,1,0:T(8,128)}), f32[16,4,64,128]{3,2,1,0:T(8,128)}, u32[]{:S(2)}, u32[]{:S(2)}) async-start(f32[16,4,64,128]{3,2,1,0:T(8,128)} %copy_bitcast_fusion), calls=%async_computation | async-start | bytes 4194304 | tf_op jit(solution)/shard_map/all_to_all | solution.py:113
  119.3 44.9 %all-to-all-done = f32[16,4,64,128]{3,2,1,0:T(8,128)} async-done(((f32[16,4,64,128]{3,2,1,0:T(8,128)}), f32[16,4,64,128]{3,2,1,0:T(8,128)}, u32[]{:S(2)}, u32[]{:S(2)}) %all-to-all-start) | async-done | bytes 2097184 | tf_op jit(solution)/shard_map/all_to_all | solution.py:113
  176.9 5.0 %collective-permute-start.16 = (f32[28,64,128]{2,1,0:T(8,128)S(1)}, f32[28,64,128]{2,1,0:T(8,128)S(1)}, u32[]{:S(2)}, u32[]{:S(2)}) collective-permute-start(f32[28,64,128]{2,1,0:T(8,128)S(1)} %get-tuple-element.64), channel_id=1, source_target_pairs={{1,2},{2,1},{3,4},{4,3},{5,6},{6,5},{7,8},{8,7},{9,10},{10,9},{11,... | collective-permute-start | bytes 2752520 | tf_op jit(solution)/shard_map/ppermute | solution.py:20
  186.0 9.2 %collective-permute-done.16 = f32[28,64,128]{2,1,0:T(8,128)S(1)} collective-permute-done((f32[28,64,128]{2,1,0:T(8,128)S(1)}, f32[28,64,128]{2,1,0:T(8,128)S(1)}, u32[]{:S(2)}, u32[]{:S(2)}) %collective-permute-start.16) | collective-permute-done | bytes 917536 | tf_op jit(solution)/shard_map/ppermute | solution.py:20
  197.8 5.0 %collective-permute-start.18 = (f32[4,64,128]{2,1,0:T(8,128)S(1)}, f32[4,64,128]{2,1,0:T(8,128)S(1)}, u32[]{:S(2)}, u32[]{:S(2)}) collective-permute-start(f32[4,64,128]{2,1,0:T(8,128)S(1)} %get-tuple-element.7), channel_id=1, source_target_pairs={{1,2},{2,1},{3,4},{4,3},{5,6},{6,5},{7,8},{8,7},{9,10},{10,9},{11,... | collective-permute-start | bytes 393224 | tf_op jit(solution)/shard_map/ppermute | solution.py:20
  202.8 4.9 %collective-permute-done.18 = f32[4,64,128]{2,1,0:T(8,128)S(1)} collective-permute-done((f32[4,64,128]{2,1,0:T(8,128)S(1)}, f32[4,64,128]{2,1,0:T(8,128)S(1)}, u32[]{:S(2)}, u32[]{:S(2)}) %collective-permute-start.18) | collective-permute-done | bytes 131104 | tf_op jit(solution)/shard_map/ppermute | solution.py:20
  209.7 5.0 %collective-permute-start.20 = (f32[4,64,128]{2,1,0:T(8,128)S(1)}, f32[4,64,128]{2,1,0:T(8,128)S(1)}, u32[]{:S(2)}, u32[]{:S(2)}) collective-permute-start(f32[4,64,128]{2,1,0:T(8,128)S(1)} %get-tuple-element.5), channel_id=1, source_target_pairs={{1,2},{2,1},{3,4},{4,3},{5,6},{6,5},{7,8},{8,7},{9,10},{10,9},{11,... | collective-permute-start | bytes 393224 | tf_op jit(solution)/shard_map/ppermute | solution.py:20
  214.7 4.9 %collective-permute-done.20 = f32[4,64,128]{2,1,0:T(8,128)S(1)} collective-permute-done((f32[4,64,128]{2,1,0:T(8,128)S(1)}, f32[4,64,128]{2,1,0:T(8,128)S(1)}, u32[]{:S(2)}, u32[]{:S(2)}) %collective-permute-start.20) | collective-permute-done | bytes 131104 | tf_op jit(solution)/shard_map/ppermute | solution.py:20
  221.5 5.0 %collective-permute-start.22 = (f32[4,64,128]{2,1,0:T(8,128)S(1)}, f32[4,64,128]{2,1,0:T(8,128)S(1)}, u32[]{:S(2)}, u32[]{:S(2)}) collective-permute-start(f32[4,64,128]{2,1,0:T(8,128)S(1)} %get-tuple-element.3), channel_id=1, source_target_pairs={{1,2},{2,1},{3,4},{4,3},{5,6},{6,5},{7,8},{8,7},{9,10},{10,9},{11,... | collective-permute-start | bytes 393224 | tf_op jit(solution)/shard_map/ppermute | solution.py:20
  226.6 4.9 %collective-permute-done.22 = f32[4,64,128]{2,1,0:T(8,128)S(1)} collective-permute-done((f32[4,64,128]{2,1,0:T(8,128)S(1)}, f32[4,64,128]{2,1,0:T(8,128)S(1)}, u32[]{:S(2)}, u32[]{:S(2)}) %collective-permute-start.22) | collective-permute-done | bytes 131104 | tf_op jit(solution)/shard_map/ppermute | solution.py:20
  232.4 31.0 %all_to_all.10 = f32[16,4,32,128]{3,2,1,0:T(8,128)S(1)} all-to-all(f32[16,4,32,128]{3,2,1,0:T(8,128)S(1)} %slice.1949), channel_id=1, replica_groups=mesh['tm'=16,'space'=16] {'tm'}, dimensions={0} | all-to-all | bytes 2097152 | tf_op jit(solution)/shard_map/all_to_all | solution.py:141
  264.9 20.8 %collective-permute-done.24 = f32[4,512,128]{2,1,0:T(8,128)S(1)} collective-permute-done((f32[4,512,128]{2,1,0:T(8,128)S(1)}, f32[4,512,128]{2,1,0:T(8,128)S(1)}, u32[]{:S(2)}, u32[]{:S(2)}) %collective-permute-start.24) | collective-permute-done | bytes 1048608 | tf_op jit(solution)/shard_map/ppermute | solution.py:143
  (189 shorter events, 63.2 us)
Async XLA Ops:
  7.9 30.2 %collective-permute-start = (f32[3152,128]{1,0:T(8,128)}, f32[3152,128]{1,0:T(8,128)}, u32[]{:S(2)}, u32[]{:S(2)}) collective-permute-start(f32[3152,128]{1,0:T(8,128)} %get-tuple-element.22), channel_id=1, source_target_pairs={{1,2},{2,1},{3,4},{4,3},{5,6},{6,5},{7,8},{8,7},{9,10},{10,9},{11,... | collective-permute-start | bytes 4841480 | tf_op jit(solution)/shard_map/ppermute | solution.py:20
  12.8 25.3 %collective-permute-start.1 = (f32[3152,128]{1,0:T(8,128)}, f32[3152,128]{1,0:T(8,128)}, u32[]{:S(2)}, u32[]{:S(2)}) collective-permute-start(f32[3152,128]{1,0:T(8,128)} %get-tuple-element.23), channel_id=1, source_target_pairs={{0,1},{1,0},{2,3},{3,2},{4,5},{5,4},{6,7},{7,6},{8,9},{9,8},{10,11... | collective-permute-start | bytes 4841480 | tf_op jit(solution)/shard_map/ppermute | solution.py:21
  12.9 24.0 %collective-permute-start.8 = (f32[2,264,128]{2,1,0:T(8,128)}, f32[2,264,128]{2,1,0:T(8,128)}, u32[]{:S(2)}, u32[]{:S(2)}) collective-permute-start(f32[2,264,128]{2,1,0:T(8,128)} %get-tuple-element.100), channel_id=1, source_target_pairs={{1,2},{2,1},{3,4},{4,3},{5,6},{6,5},{7,8},{8,7},{9,10},{10,9},{11,... | collective-permute-start | bytes 811016 | tf_op jit(solution)/shard_map/ppermute | solution.py:20
  17.2 19.7 %collective-permute-start.9 = (f32[2,264,128]{2,1,0:T(8,128)S(1)}, f32[2,264,128]{2,1,0:T(8,128)}, u32[]{:S(2)}, u32[]{:S(2)}) collective-permute-start(f32[2,264,128]{2,1,0:T(8,128)S(1)} %get-tuple-element.101), channel_id=1, source_target_pairs={{0,1},{1,0},{2,3},{3,2},{4,5},{5,4},{6,7},{7,6},{8,9},{9,8},{10,11... | collective-permute-start | bytes 811016 | tf_op jit(solution)/shard_map/ppermute | solution.py:21
  45.1 11.4 %collective-permute-start.2 = (f32[2,264,128]{2,1,0:T(8,128)S(1)}, f32[2,264,128]{2,1,0:T(8,128)S(1)}, u32[]{:S(2)}, u32[]{:S(2)}) collective-permute-start(f32[2,264,128]{2,1,0:T(8,128)S(1)} %get-tuple-element.160), channel_id=1, source_target_pairs={{1,2},{2,1},{3,4},{4,3},{5,6},{6,5},{7,8},{8,7},{9,10},{10,9},{11,... | collective-permute-start | bytes 811016 | tf_op jit(solution)/shard_map/ppermute | solution.py:20
  50.0 6.5 %collective-permute-start.3 = (f32[2,264,128]{2,1,0:T(8,128)S(1)}, f32[2,264,128]{2,1,0:T(8,128)S(1)}, u32[]{:S(2)}, u32[]{:S(2)}) collective-permute-start(f32[2,264,128]{2,1,0:T(8,128)S(1)} %get-tuple-element.161), channel_id=1, source_target_pairs={{0,1},{1,0},{2,3},{3,2},{4,5},{5,4},{6,7},{7,6},{8,9},{9,8},{10,11... | collective-permute-start | bytes 811016 | tf_op jit(solution)/shard_map/ppermute | solution.py:21
  58.3 11.4 %collective-permute-start.10 = (f32[2,264,128]{2,1,0:T(8,128)S(1)}, f32[2,264,128]{2,1,0:T(8,128)S(1)}, u32[]{:S(2)}, u32[]{:S(2)}) collective-permute-start(f32[2,264,128]{2,1,0:T(8,128)S(1)} %get-tuple-element.172), channel_id=1, source_target_pairs={{1,2},{2,1},{3,4},{4,3},{5,6},{6,5},{7,8},{8,7},{9,10},{10,9},{11,... | collective-permute-start | bytes 811016 | tf_op jit(solution)/shard_map/ppermute | solution.py:20
  63.2 6.5 %collective-permute-start.11 = (f32[2,264,128]{2,1,0:T(8,128)S(1)}, f32[2,264,128]{2,1,0:T(8,128)S(1)}, u32[]{:S(2)}, u32[]{:S(2)}) collective-permute-start(f32[2,264,128]{2,1,0:T(8,128)S(1)} %get-tuple-element.173), channel_id=1, source_target_pairs={{0,1},{1,0},{2,3},{3,2},{4,5},{5,4},{6,7},{7,6},{8,9},{9,8},{10,11... | collective-permute-start | bytes 811016 | tf_op jit(solution)/shard_map/ppermute | solution.py:21
  63.7 11.4 %collective-permute-start.4 = (f32[2,264,128]{2,1,0:T(8,128)S(1)}, f32[2,264,128]{2,1,0:T(8,128)S(1)}, u32[]{:S(2)}, u32[]{:S(2)}) collective-permute-start(f32[2,264,128]{2,1,0:T(8,128)S(1)} %get-tuple-element.156), channel_id=1, source_target_pairs={{1,2},{2,1},{3,4},{4,3},{5,6},{6,5},{7,8},{8,7},{9,10},{10,9},{11,... | collective-permute-start | bytes 811016 | tf_op jit(solution)/shard_map/ppermute | solution.py:20
  68.0 7.1 %collective-permute-start.5 = (f32[2,264,128]{2,1,0:T(8,128)S(1)}, f32[2,264,128]{2,1,0:T(8,128)S(1)}, u32[]{:S(2)}, u32[]{:S(2)}) collective-permute-start(f32[2,264,128]{2,1,0:T(8,128)S(1)} %get-tuple-element.157), channel_id=1, source_target_pairs={{0,1},{1,0},{2,3},{3,2},{4,5},{5,4},{6,7},{7,6},{8,9},{9,8},{10,11... | collective-permute-start | bytes 811016 | tf_op jit(solution)/shard_map/ppermute | solution.py:21
  77.0 11.4 %collective-permute-start.12 = (f32[2,264,128]{2,1,0:T(8,128)S(1)}, f32[2,264,128]{2,1,0:T(8,128)S(1)}, u32[]{:S(2)}, u32[]{:S(2)}) collective-permute-start(f32[2,264,128]{2,1,0:T(8,128)S(1)} %get-tuple-element.168), channel_id=1, source_target_pairs={{1,2},{2,1},{3,4},{4,3},{5,6},{6,5},{7,8},{8,7},{9,10},{10,9},{11,... | collective-permute-start | bytes 811016 | tf_op jit(solution)/shard_map/ppermute | solution.py:20
  81.3 7.1 %collective-permute-start.13 = (f32[2,264,128]{2,1,0:T(8,128)S(1)}, f32[2,264,128]{2,1,0:T(8,128)S(1)}, u32[]{:S(2)}, u32[]{:S(2)}) collective-permute-start(f32[2,264,128]{2,1,0:T(8,128)S(1)} %get-tuple-element.169), channel_id=1, source_target_pairs={{0,1},{1,0},{2,3},{3,2},{4,5},{5,4},{6,7},{7,6},{8,9},{9,8},{10,11... | collective-permute-start | bytes 811016 | tf_op jit(solution)/shard_map/ppermute | solution.py:21
  81.8 11.4 %collective-permute-start.6 = (f32[2,264,128]{2,1,0:T(8,128)S(1)}, f32[2,264,128]{2,1,0:T(8,128)S(1)}, u32[]{:S(2)}, u32[]{:S(2)}) collective-permute-start(f32[2,264,128]{2,1,0:T(8,128)S(1)} %get-tuple-element.152), channel_id=1, source_target_pairs={{1,2},{2,1},{3,4},{4,3},{5,6},{6,5},{7,8},{8,7},{9,10},{10,9},{11,... | collective-permute-start | bytes 811016 | tf_op jit(solution)/shard_map/ppermute | solution.py:20
  86.7 6.5 %collective-permute-start.7 = (f32[2,264,128]{2,1,0:T(8,128)S(1)}, f32[2,264,128]{2,1,0:T(8,128)S(1)}, u32[]{:S(2)}, u32[]{:S(2)}) collective-permute-start(f32[2,264,128]{2,1,0:T(8,128)S(1)} %get-tuple-element.153), channel_id=1, source_target_pairs={{0,1},{1,0},{2,3},{3,2},{4,5},{5,4},{6,7},{7,6},{8,9},{9,8},{10,11... | collective-permute-start | bytes 811016 | tf_op jit(solution)/shard_map/ppermute | solution.py:21
  95.0 11.4 %collective-permute-start.14 = (f32[2,264,128]{2,1,0:T(8,128)S(1)}, f32[2,264,128]{2,1,0:T(8,128)S(1)}, u32[]{:S(2)}, u32[]{:S(2)}) collective-permute-start(f32[2,264,128]{2,1,0:T(8,128)S(1)} %get-tuple-element.164), channel_id=1, source_target_pairs={{1,2},{2,1},{3,4},{4,3},{5,6},{6,5},{7,8},{8,7},{9,10},{10,9},{11,... | collective-permute-start | bytes 811016 | tf_op jit(solution)/shard_map/ppermute | solution.py:20
  99.9 6.5 %collective-permute-start.15 = (f32[2,264,128]{2,1,0:T(8,128)S(1)}, f32[2,264,128]{2,1,0:T(8,128)S(1)}, u32[]{:S(2)}, u32[]{:S(2)}) collective-permute-start(f32[2,264,128]{2,1,0:T(8,128)S(1)} %get-tuple-element.165), channel_id=1, source_target_pairs={{0,1},{1,0},{2,3},{3,2},{4,5},{5,4},{6,7},{7,6},{8,9},{9,8},{10,11... | collective-permute-start | bytes 811016 | tf_op jit(solution)/shard_map/ppermute | solution.py:21
  109.9 54.3 %all-to-all-start = ((f32[16,4,64,128]{3,2,1,0:T(8,128)}), f32[16,4,64,128]{3,2,1,0:T(8,128)}, u32[]{:S(2)}, u32[]{:S(2)}) async-start(f32[16,4,64,128]{3,2,1,0:T(8,128)} %copy_bitcast_fusion), calls=%async_computation | async-start | bytes 4194304 | tf_op jit(solution)/shard_map/all_to_all | solution.py:113
  176.9 18.3 %collective-permute-start.16 = (f32[28,64,128]{2,1,0:T(8,128)S(1)}, f32[28,64,128]{2,1,0:T(8,128)S(1)}, u32[]{:S(2)}, u32[]{:S(2)}) collective-permute-start(f32[28,64,128]{2,1,0:T(8,128)S(1)} %get-tuple-element.64), channel_id=1, source_target_pairs={{1,2},{2,1},{3,4},{4,3},{5,6},{6,5},{7,8},{8,7},{9,10},{10,9},{11,... | collective-permute-start | bytes 2752520 | tf_op jit(solution)/shard_map/ppermute | solution.py:20
  182.0 13.3 %collective-permute-start.17 = (f32[28,64,128]{2,1,0:T(8,128)S(1)}, f32[28,64,128]{2,1,0:T(8,128)S(1)}, u32[]{:S(2)}, u32[]{:S(2)}) collective-permute-start(f32[28,64,128]{2,1,0:T(8,128)S(1)} %get-tuple-element.65), channel_id=1, source_target_pairs={{0,1},{1,0},{2,3},{3,2},{4,5},{5,4},{6,7},{7,6},{8,9},{9,8},{10,11... | collective-permute-start | bytes 2752520 | tf_op jit(solution)/shard_map/ppermute | solution.py:21
  197.8 9.9 %collective-permute-start.18 = (f32[4,64,128]{2,1,0:T(8,128)S(1)}, f32[4,64,128]{2,1,0:T(8,128)S(1)}, u32[]{:S(2)}, u32[]{:S(2)}) collective-permute-start(f32[4,64,128]{2,1,0:T(8,128)S(1)} %get-tuple-element.7), channel_id=1, source_target_pairs={{1,2},{2,1},{3,4},{4,3},{5,6},{6,5},{7,8},{8,7},{9,10},{10,9},{11,... | collective-permute-start | bytes 393224 | tf_op jit(solution)/shard_map/ppermute | solution.py:20
  209.6 5.1 %collective-permute-start.21 = (f32[4,64,128]{2,1,0:T(8,128)S(1)}, f32[4,64,128]{2,1,0:T(8,128)S(1)}, u32[]{:S(2)}, u32[]{:S(2)}) collective-permute-start(f32[4,64,128]{2,1,0:T(8,128)S(1)} %get-tuple-element.5), channel_id=1, source_target_pairs={{0,1},{1,0},{2,3},{3,2},{4,5},{5,4},{6,7},{7,6},{8,9},{9,8},{10,11... | collective-permute-start | bytes 393224 | tf_op jit(solution)/shard_map/ppermute | solution.py:21
  209.7 9.9 %collective-permute-start.20 = (f32[4,64,128]{2,1,0:T(8,128)S(1)}, f32[4,64,128]{2,1,0:T(8,128)S(1)}, u32[]{:S(2)}, u32[]{:S(2)}) collective-permute-start(f32[4,64,128]{2,1,0:T(8,128)S(1)} %get-tuple-element.5), channel_id=1, source_target_pairs={{1,2},{2,1},{3,4},{4,3},{5,6},{6,5},{7,8},{8,7},{9,10},{10,9},{11,... | collective-permute-start | bytes 393224 | tf_op jit(solution)/shard_map/ppermute | solution.py:20
  221.5 9.9 %collective-permute-start.22 = (f32[4,64,128]{2,1,0:T(8,128)S(1)}, f32[4,64,128]{2,1,0:T(8,128)S(1)}, u32[]{:S(2)}, u32[]{:S(2)}) collective-permute-start(f32[4,64,128]{2,1,0:T(8,128)S(1)} %get-tuple-element.3), channel_id=1, source_target_pairs={{1,2},{2,1},{3,4},{4,3},{5,6},{6,5},{7,8},{8,7},{9,10},{10,9},{11,... | collective-permute-start | bytes 393224 | tf_op jit(solution)/shard_map/ppermute | solution.py:20
  263.5 22.2 %collective-permute-start.24 = (f32[4,512,128]{2,1,0:T(8,128)S(1)}, f32[4,512,128]{2,1,0:T(8,128)S(1)}, u32[]{:S(2)}, u32[]{:S(2)}) collective-permute-start(f32[4,512,128]{2,1,0:T(8,128)S(1)} %bitcast.259), channel_id=1, source_target_pairs={{0,16},{16,32},{32,48},{48,64},{64,80},{80,96},{96,112},{112,128},... | collective-permute-start | bytes 3145736 | tf_op jit(solution)/shard_map/ppermute | solution.py:143
  (14 other events, 104.3 us)

commit v3 on v1

v3 whole, which is shorter than its diff:
```python
import jax
import jax.numpy as jnp
from jax import lax
from jax.sharding import PartitionSpec as P

FINE = 8
SPAN = 4
ROUNDS = 2


def swaps(pairs):
    return [route for a, b in pairs for route in ((a, b), (b, a))]


def beside_pairs():
    return swaps([(i, i + 1) for i in range(0, lax.axis_size("space") - 1, 2)])


def exchanged(low, high, even):
    devices = lax.axis_size("space")
    far = swaps([(i, i + 1) for i in range(1, devices - 1, 2)])
    across = lax.ppermute(jnp.where(even, low, high), "space", far)
    beside = lax.ppermute(jnp.where(even, high, low), "space", beside_pairs())
    return jnp.where(even, across, beside), jnp.where(even, beside, across)


def around(wide):
    padded = jnp.pad(wide, ((0, 0), (1, 1), (1, 1)))
    total = padded[2:, 1:-1, 1:-1] + padded[:-2, 1:-1, 1:-1]
    total = total + padded[1:-1, 2:, 1:-1] + padded[1:-1, :-2, 1:-1]
    total = total + padded[1:-1, 1:-1, 2:] + padded[1:-1, 1:-1, :-2]
    return total, wide[:-2]


def on_device(slice_starts, diffusion, courant, loss, heating):
    start = slice_starts[0]
    planes, rows, lanes = start.shape
    slices = lax.axis_size("tm")
    slot = lax.axis_index("tm")
    even = lax.axis_index("space") % 2 == 0
    part = rows // slices
    halo = slices
    window = part + 2 * halo

    denom = 1.0 + FINE * (6.0 * diffusion + courant + loss)
    own = 1.0 / denom
    side = FINE * diffusion / denom
    west = FINE * courant / denom

    edge = ROUNDS - 1

    def flat(*arrays):
        return jnp.concatenate([a.reshape(-1, lanes) for a in arrays])

    raw = (diffusion, courant, loss, heating)
    before, after = exchanged(flat(*(x[:edge] for x in raw)), flat(*(x[planes - edge :] for x in raw)), even)
    before, after = (x.reshape(4, edge, rows, lanes) for x in (before, after))
    fine_terms = [jnp.concatenate([before[i], raw[i], after[i]]) for i in range(4)]

    state = start
    first = None
    for _ in range(FINE // ROUNDS):
        before, after = exchanged(state[:ROUNDS], state[planes - ROUNDS :], even)
        state = jnp.concatenate([before, state, after])
        if first is None:
            first = state[ROUNDS - 1 : ROUNDS + planes + 1]
        for step in range(ROUNDS):
            total, upwind = around(state)
            centre = state[1:-1]
            trim = step
            d, c, l, h = (t[trim : t.shape[0] - trim] for t in fine_terms)
            state = centre + d * (total - 6.0 * centre) - c * (centre - upwind) - l * centre + h
    total, upwind = around(first)
    coarse_old = own * start + side * total + west * upwind
    element = jnp.where(slot > 0, state - coarse_old, state)

    blocks = jnp.pad(element, ((0, 0), (halo, halo), (0, 0))).reshape(planes, -1, part, lanes)
    widened = jnp.concatenate([blocks[:, :-1], blocks[:, 1:]], axis=2)
    terms = lax.all_to_all(widened.transpose(1, 0, 2, 3), "tm", 0, 0, tiled=True)

    last = slices - 2
    groups = [(g, min(g + SPAN, last)) for g in range(0, last, SPAN)]
    width = {g: end - g + (end == last) for g, end in groups}
    depth = [0] * slices
    for g, end in groups:
        for n in range(g, end + 1):
            depth[n] = width[g] - (n - g)
    deep = SPAN - 1
    inner = [0 if n in width and n else depth[n] for n in range(last + 1)]
    tall = jnp.pad(jnp.stack([own, side, west]), ((0, 0), (0, 0), (halo, halo), (0, 0)))
    factors = lax.dynamic_slice_in_dim(tall, slot * part, window, axis=2)
    before, after = exchanged(
        jnp.concatenate([terms[n, :k] for n, k in enumerate(inner) if k] + [factors[i, :deep] for i in range(3)]),
        jnp.concatenate([terms[n, planes - k :] for n, k in enumerate(inner) if k] + [factors[i, planes - deep :] for i in range(3)]),
        even,
    )
    offsets = [sum(inner[:n]) for n in range(last + 2)]

    def term(n):
        k, o = inner[n], offsets[n]
        return jnp.concatenate([before[o : o + k], terms[n], after[o : o + k]]) if k else terms[n]

    def factor(i):
        o = offsets[last + 1] + i * deep
        return jnp.concatenate([before[o : o + deep], factors[i], after[o : o + deep]])

    coarse_terms = [factor(i) for i in range(3)]
    state = term(0)
    sent = [jnp.zeros((planes + 1, part, lanes), state.dtype)]
    for n in range(last + 1):
        if n:
            k = inner[n]
            trim = deep - k
            o, s, w = (t[trim : t.shape[0] - trim] for t in coarse_terms)
            wide = state[depth[n - 1] - 1 - k : state.shape[0] - (depth[n - 1] - 1 - k)]
            total, upwind = around(wide)
            state = o * wide[1:-1] + s * total + w * upwind + term(n)
            if n in width:
                k = width[n]
                low, high = exchanged(state[:k], state[planes - k :], even)
                state = jnp.concatenate([low, state, high])
        k = depth[n]
        kept = state[:, halo : halo + part]
        sent.append(jnp.concatenate([kept[k : k + planes], jnp.where(even, kept[k - 1 : k], kept[k + planes : k + planes + 1])]))

    back = lax.all_to_all(jnp.stack(sent), "tm", 0, 0, tiled=True)
    arrived = back.transpose(1, 0, 2, 3).reshape(planes + 1, rows, lanes)
    following, across = arrived[:planes], arrived[planes:]
    beside = lax.ppermute(jnp.where(even, following[planes - 1 :], following[:1]), "space", beside_pairs())
    low, high = jnp.where(even, across, beside), jnp.where(even, beside, across)
    total, upwind = around(jnp.concatenate([low, following, high]))
    end_state = jnp.where(slot > 0, own * following + side * total + west * upwind, 0.0) + element
    following = jnp.where(slot == 0, start, following)
    return end_state[None], following[None]


def solution(mesh):
    return jax.shard_map(
        on_device,
        mesh=mesh,
        in_specs=(
            P("tm", "space", None, None),
            P("space", None, None),
            P("space", None, None),
            P("space", None, None),
            P("space", None, None),
        ),
        out_specs=(P("tm", "space", None, None), P("tm", "space", None, None)),
        check_vma=False,
    )
```

time: 262 us -> 269 us (1.027)
  blocking collectives: 82.7 us -> 0 us
  waiting for transfers between devices: 91.9 us -> 136 us
  starting transfers between devices: 47.4 us -> 63.7 us
  local copies, waits for them, and re-layouts: 8.08 us -> 24.1 us
  other arithmetic: 27.5 us -> 42.1 us
    all_to_all x2 -> x0, blocking collectives: 82.7 us -> none  [the longest x1 53.2 us: on_device(): lax.all_to_all(widened.transpose(1, 0, 2, 3), 'tm', 0, 0, tiled=True)]
    all_to_all x0 -> x2, waiting for transfers between devices: none -> 73 us  [the longest x1 41.7 us: on_device(): lax.all_to_all(widened.transpose(1, 0, 2, 3), 'tm', 0, 0, tiled=True)]
    ppermute x10, waiting for transfers between devices: 20.8 us -> 0.08 us  [the longest x1 0.05 us: on_device(): lax.ppermute(jnp.where(even, following[planes - 1:], following[:1]), 'spa...]
    all_to_all x0 -> x2, starting transfers between devices: none -> 13.7 us  [the longest x1 9.27 us: on_device(): lax.all_to_all(widened.transpose(1, 0, 2, 3), 'tm', 0, 0, tiled=True)]
    unnamed x63 -> x81, local copies, waits for them, and re-layouts: 5.1 us -> 18 us
    unnamed x3 -> x14, other arithmetic: 0.43 us -> 8.9 us
    ppermute x9, waiting for transfers between devices: 71.1 us -> 63 us  [exchanged(): across = lax.ppermute(jnp.where(even, low, high), 'space', far)]
    add x6 -> x5, other arithmetic: 8.57 us -> 6.75 us  [on_device(): centre + d * (total - 6.0 * centre) - c * (centre - upwind) - l * centre + h]
  transfers between devices with their start and end apart: 19 -> 21, of which waited for: 9 -> 11; matrix products, arithmetic and copies ran while one was open for 1% -> 4% of each run, Pallas kernels for 0% -> 0%
where the time goes in v3:
time: 269 us; the launch traced here: 268 us
  waiting for transfers between devices  136 us (51%)
  starting transfers between devices  63.7 us (24%)
  other arithmetic  42.1 us (16%)
  local copies, waits for them, and re-layouts  24.1 us (9%)
    ppermute x9, waiting for transfers between devices, exchanged(): across = lax.ppermute(jnp.where(even, low, high), 'space', far)  63 us
    ppermute x9, starting transfers between devices, exchanged(): across = lax.ppermute(jnp.where(even, low, high), 'space', far)  44.9 us
    all_to_all x1, waiting for transfers between devices, on_device(): lax.all_to_all(widened.transpose(1, 0, 2, 3), 'tm', 0, 0, tiled=True)  41.7 us
    all_to_all x1, waiting for transfers between devices, on_device(): back = lax.all_to_all(jnp.stack(sent), 'tm', 0, 0, tiled=True)  31.2 us
    unnamed x81, local copies, waits for them, and re-layouts  18 us
    all_to_all x1, starting transfers between devices, on_device(): lax.all_to_all(widened.transpose(1, 0, 2, 3), 'tm', 0, 0, tiled=True)  9.27 us
    unnamed x14, other arithmetic  8.9 us
    add x5, other arithmetic, on_device(): centre + d * (total - 6.0 * centre) - c * (centre - upwind) - l * centre + h  6.75 us
  transfers between devices with their start and end apart: 21, of which 11 were waited for; matrix products, arithmetic and copies ran while one was open for 4% of the time, Pallas kernels for 0%

profile of v3, /device:TPU:25, one launch (start us, length us, event | category | flops | bytes accessed | tf_op | source)
XLA Modules:
  0.0 267.8 jit_solution(1522334141703885743)
XLA Ops:
  3.2 5.0 %collective-permute-start.2 = (f32[2048,128]{1,0:T(8,128)S(1)}, f32[2048,128]{1,0:T(8,128)S(1)}, u32[]{:S(2)}, u32[]{:S(2)}) collective-permute-start(f32[2048,128]{1,0:T(8,128)S(1)} %get-tuple-element.46), channel_id=1, source_target_pairs={{1,2},{2,1},{3,4},{4,3},{5,6},{6,5},{7,8},{8,7},{9,10},{10,9},{11,... | collective-permute-start | bytes 3145736 | tf_op jit(solution)/shard_map/ppermute | solution.py:22
  8.4 4.3 %collective-permute-start = (f32[2,512,128]{2,1,0:T(8,128)S(1)}, f32[2,512,128]{2,1,0:T(8,128)S(1)}, u32[]{:S(2)}, u32[]{:S(2)}) collective-permute-start(f32[2,512,128]{2,1,0:T(8,128)S(1)} %get-tuple-element.110), channel_id=1, source_target_pairs={{1,2},{2,1},{3,4},{4,3},{5,6},{6,5},{7,8},{8,7},{9,10},{10,9},{11,... | collective-permute-start | bytes 1572872 | tf_op jit(solution)/shard_map/ppermute | solution.py:22
  12.8 15.9 %collective-permute-done = f32[2,512,128]{2,1,0:T(8,128)S(1)} collective-permute-done((f32[2,512,128]{2,1,0:T(8,128)S(1)}, f32[2,512,128]{2,1,0:T(8,128)S(1)}, u32[]{:S(2)}, u32[]{:S(2)}) %collective-permute-start) | collective-permute-done | bytes 524320 | tf_op jit(solution)/shard_map/ppermute | solution.py:22
  31.4 2.6 fusion.244
  34.9 4.9 %collective-permute-start.4 = (f32[2,512,128]{2,1,0:T(8,128)S(1)}, f32[2,512,128]{2,1,0:T(8,128)S(1)}, u32[]{:S(2)}, u32[]{:S(2)}) collective-permute-start(f32[2,512,128]{2,1,0:T(8,128)S(1)} %get-tuple-element.90), channel_id=1, source_target_pairs={{1,2},{2,1},{3,4},{4,3},{5,6},{6,5},{7,8},{8,7},{9,10},{10,9},{11,... | collective-permute-start | bytes 1572872 | tf_op jit(solution)/shard_map/ppermute | solution.py:22
  39.9 9.1 %collective-permute-done.4 = f32[2,512,128]{2,1,0:T(8,128)S(1)} collective-permute-done((f32[2,512,128]{2,1,0:T(8,128)S(1)}, f32[2,512,128]{2,1,0:T(8,128)S(1)}, u32[]{:S(2)}, u32[]{:S(2)}) %collective-permute-start.4) | collective-permute-done | bytes 524320 | tf_op jit(solution)/shard_map/ppermute | solution.py:22
  51.9 4.9 %collective-permute-start.6 = (f32[2,512,128]{2,1,0:T(8,128)S(1)}, f32[2,512,128]{2,1,0:T(8,128)S(1)}, u32[]{:S(2)}, u32[]{:S(2)}) collective-permute-start(f32[2,512,128]{2,1,0:T(8,128)S(1)} %get-tuple-element.86), channel_id=1, source_target_pairs={{1,2},{2,1},{3,4},{4,3},{5,6},{6,5},{7,8},{8,7},{9,10},{10,9},{11,... | collective-permute-start | bytes 1572872 | tf_op jit(solution)/shard_map/ppermute | solution.py:22
  56.9 9.1 %collective-permute-done.6 = f32[2,512,128]{2,1,0:T(8,128)S(1)} collective-permute-done((f32[2,512,128]{2,1,0:T(8,128)S(1)}, f32[2,512,128]{2,1,0:T(8,128)S(1)}, u32[]{:S(2)}, u32[]{:S(2)}) %collective-permute-start.6) | collective-permute-done | bytes 524320 | tf_op jit(solution)/shard_map/ppermute | solution.py:22
  68.0 2.7 %fusion.231 = (f32[1,4,512,128]{3,2,1,0:T(8,128)}, f32[1,4,512,128]{3,2,1,0:T(8,128)}, f32[4,512,128]{2,1,0:T(8,128)S(1)}, f32[1,4,512,128]{3,2,1,0:T(8,128)}) fusion(f32[4,512,128]{2,1,0:T(8,128)S(1)} %copy-done.1, f32[4,512,128]{2,1,0:T(8,128)S(1)} %copy-done.2, f32[4,512,128]{2,1,0:T(8,128)S(1)} %copy-done, f32[4,512,128]{2,1,0:T(8,128)S(1)} %copy-done.3, ...), kind=kLoop, calls=%fused_computation.467 | loop fusion | flops 6553600 | bytes 13107200 | tf_op jit(solution)/shard_map/stack | solution.py:90
  72.8 4.9 %collective-permute-start.8 = (f32[2,512,128]{2,1,0:T(8,128)}, f32[2,512,128]{2,1,0:T(8,128)}, u32[]{:S(2)}, u32[]{:S(2)}) collective-permute-start(f32[2,512,128]{2,1,0:T(8,128)} %get-tuple-element.82), channel_id=1, source_target_pairs={{1,2},{2,1},{3,4},{4,3},{5,6},{6,5},{7,8},{8,7},{9,10},{10,9},{11,... | collective-permute-start | bytes 1572872 | tf_op jit(solution)/shard_map/ppermute | solution.py:22
  78.0 9.3 %collective-permute-done.8 = f32[2,512,128]{2,1,0:T(8,128)} collective-permute-done((f32[2,512,128]{2,1,0:T(8,128)}, f32[2,512,128]{2,1,0:T(8,128)}, u32[]{:S(2)}, u32[]{:S(2)}) %collective-permute-start.8) | collective-permute-done | bytes 524320 | tf_op jit(solution)/shard_map/ppermute | solution.py:22
  92.3 2.3 subtract_select_fusion
  97.0 9.3 %all-to-all-start = ((f32[16,4,64,128]{3,2,1,0:T(8,128)}), f32[16,4,64,128]{3,2,1,0:T(8,128)}, u32[]{:S(2)}, u32[]{:S(2)}) async-start(f32[16,4,64,128]{3,2,1,0:T(8,128)} %copy_bitcast_fusion), calls=%async_computation | async-start | bytes 4194304 | tf_op jit(solution)/shard_map/all_to_all | solution.py:79
  107.4 41.7 %all-to-all-done = f32[16,4,64,128]{3,2,1,0:T(8,128)} async-done(((f32[16,4,64,128]{3,2,1,0:T(8,128)}), f32[16,4,64,128]{3,2,1,0:T(8,128)}, u32[]{:S(2)}, u32[]{:S(2)}) %all-to-all-start) | async-done | bytes 2097184 | tf_op jit(solution)/shard_map/all_to_all | solution.py:79
  161.0 5.2 %collective-permute-start.10 = (f32[34,64,128]{2,1,0:T(8,128)S(1)}, f32[34,64,128]{2,1,0:T(8,128)S(1)}, u32[]{:S(2)}, u32[]{:S(2)}) collective-permute-start(f32[34,64,128]{2,1,0:T(8,128)S(1)} %get-tuple-element.8), channel_id=1, source_target_pairs={{1,2},{2,1},{3,4},{4,3},{5,6},{6,5},{7,8},{8,7},{9,10},{10,9},{11,... | collective-permute-start | bytes 3342344 | tf_op jit(solution)/shard_map/ppermute | solution.py:22
  168.6 12.8 %collective-permute-done.10 = f32[34,64,128]{2,1,0:T(8,128)S(1)} collective-permute-done((f32[34,64,128]{2,1,0:T(8,128)S(1)}, f32[34,64,128]{2,1,0:T(8,128)S(1)}, u32[]{:S(2)}, u32[]{:S(2)}) %collective-permute-start.10) | collective-permute-done | bytes 1114144 | tf_op jit(solution)/shard_map/ppermute | solution.py:22
  183.8 5.2 %collective-permute-start.12 = (f32[4,64,128]{2,1,0:T(8,128)S(1)}, f32[4,64,128]{2,1,0:T(8,128)S(1)}, u32[]{:S(2)}, u32[]{:S(2)}) collective-permute-start(f32[4,64,128]{2,1,0:T(8,128)S(1)} %fusion.213), channel_id=1, source_target_pairs={{1,2},{2,1},{3,4},{4,3},{5,6},{6,5},{7,8},{8,7},{9,10},{10,9},{11,... | collective-permute-start | bytes 393224 | tf_op jit(solution)/shard_map/ppermute | solution.py:22
  195.5 5.2 %collective-permute-start.14 = (f32[4,64,128]{2,1,0:T(8,128)S(1)}, f32[4,64,128]{2,1,0:T(8,128)S(1)}, u32[]{:S(2)}, u32[]{:S(2)}) collective-permute-start(f32[4,64,128]{2,1,0:T(8,128)S(1)} %fusion.221), channel_id=1, source_target_pairs={{1,2},{2,1},{3,4},{4,3},{5,6},{6,5},{7,8},{8,7},{9,10},{10,9},{11,... | collective-permute-start | bytes 393224 | tf_op jit(solution)/shard_map/ppermute | solution.py:22
  200.9 4.5 %collective-permute-done.14 = f32[4,64,128]{2,1,0:T(8,128)S(1)} collective-permute-done((f32[4,64,128]{2,1,0:T(8,128)S(1)}, f32[4,64,128]{2,1,0:T(8,128)S(1)}, u32[]{:S(2)}, u32[]{:S(2)}) %collective-permute-start.14) | collective-permute-done | bytes 131104 | tf_op jit(solution)/shard_map/ppermute | solution.py:22
  207.3 5.2 %collective-permute-start.16 = (f32[3,64,128]{2,1,0:T(8,128)S(1)}, f32[3,64,128]{2,1,0:T(8,128)S(1)}, u32[]{:S(2)}, u32[]{:S(2)}) collective-permute-start(f32[3,64,128]{2,1,0:T(8,128)S(1)} %get-tuple-element.131), channel_id=1, source_target_pairs={{1,2},{2,1},{3,4},{4,3},{5,6},{6,5},{7,8},{8,7},{9,10},{10,9},{11,... | collective-permute-start | bytes 294920 | tf_op jit(solution)/shard_map/ppermute | solution.py:22
  220.6 4.4 %all-to-all-start.1 = ((f32[16,5,32,128]{3,2,1,0:T(8,128)}), f32[16,5,32,128]{3,2,1,0:T(8,128)}, u32[]{:S(2)}, u32[]{:S(2)}) async-start(f32[16,5,32,128]{3,2,1,0:T(8,128)} %constant_dynamic-update-slice_fusion.18), calls=%async_computation.1 | async-start | bytes 2621440 | tf_op jit(solution)/shard_map/all_to_all | solution.py:126
  225.0 31.2 %all-to-all-done.1 = f32[16,5,32,128]{3,2,1,0:T(8,128)} async-done(((f32[16,5,32,128]{3,2,1,0:T(8,128)}), f32[16,5,32,128]{3,2,1,0:T(8,128)}, u32[]{:S(2)}, u32[]{:S(2)}) %all-to-all-start.1) | async-done | bytes 1310752 | tf_op jit(solution)/shard_map/all_to_all | solution.py:126
  259.0 4.2 %collective-permute-start.18 = (f32[1,512,128]{2,1,0:T(8,128)S(1)}, f32[1,512,128]{2,1,0:T(8,128)S(1)}, u32[]{:S(2)}, u32[]{:S(2)}) collective-permute-start(f32[1,512,128]{2,1,0:T(8,128)S(1)} %bitcast.297), channel_id=1, source_target_pairs={{0,1},{1,0},{2,3},{3,2},{4,5},{5,4},{6,7},{7,6},{8,9},{9,8},{10,11... | collective-permute-start | bytes 786440 | tf_op jit(solution)/shard_map/ppermute | solution.py:129
  265.6 2.3 fusion.105
  (215 shorter events, 59.7 us)
Async XLA Ops:
  3.2 25.7 %collective-permute-start.2 = (f32[2048,128]{1,0:T(8,128)S(1)}, f32[2048,128]{1,0:T(8,128)S(1)}, u32[]{:S(2)}, u32[]{:S(2)}) collective-permute-start(f32[2048,128]{1,0:T(8,128)S(1)} %get-tuple-element.46), channel_id=1, source_target_pairs={{1,2},{2,1},{3,4},{4,3},{5,6},{6,5},{7,8},{8,7},{9,10},{10,9},{11,... | collective-permute-start | bytes 3145736 | tf_op jit(solution)/shard_map/ppermute | solution.py:22
  8.2 20.7 %collective-permute-start.3 = (f32[2048,128]{1,0:T(8,128)S(1)}, f32[2048,128]{1,0:T(8,128)S(1)}, u32[]{:S(2)}, u32[]{:S(2)}) collective-permute-start(f32[2048,128]{1,0:T(8,128)S(1)} %get-tuple-element.47), channel_id=1, source_target_pairs={{0,1},{1,0},{2,3},{3,2},{4,5},{5,4},{6,7},{7,6},{8,9},{9,8},{10,11... | collective-permute-start | bytes 3145736 | tf_op jit(solution)/shard_map/ppermute | solution.py:23
  8.4 20.3 %collective-permute-start = (f32[2,512,128]{2,1,0:T(8,128)S(1)}, f32[2,512,128]{2,1,0:T(8,128)S(1)}, u32[]{:S(2)}, u32[]{:S(2)}) collective-permute-start(f32[2,512,128]{2,1,0:T(8,128)S(1)} %get-tuple-element.110), channel_id=1, source_target_pairs={{1,2},{2,1},{3,4},{4,3},{5,6},{6,5},{7,8},{8,7},{9,10},{10,9},{11,... | collective-permute-start | bytes 1572872 | tf_op jit(solution)/shard_map/ppermute | solution.py:22
  12.7 16.0 %collective-permute-start.1 = (f32[2,512,128]{2,1,0:T(8,128)S(1)}, f32[2,512,128]{2,1,0:T(8,128)S(1)}, u32[]{:S(2)}, u32[]{:S(2)}) collective-permute-start(f32[2,512,128]{2,1,0:T(8,128)S(1)} %get-tuple-element.111), channel_id=1, source_target_pairs={{0,1},{1,0},{2,3},{3,2},{4,5},{5,4},{6,7},{7,6},{8,9},{9,8},{10,11... | collective-permute-start | bytes 1572872 | tf_op jit(solution)/shard_map/ppermute | solution.py:23
  29.2 37.0 %copy-start.16 = (f32[1,512,128]{2,1,0:T(8,128)}, f32[1,512,128]{2,1,0:T(8,128)S(1)}, u32[]{:S(2)}) copy-start(f32[1,512,128]{2,1,0:T(8,128)S(1)} %get-tuple-element.93) | copy-start | bytes 786436
  29.2 37.0 %copy-start.18 = (f32[1,512,128]{2,1,0:T(8,128)}, f32[1,512,128]{2,1,0:T(8,128)S(1)}, u32[]{:S(2)}) copy-start(f32[1,512,128]{2,1,0:T(8,128)S(1)} %get-tuple-element.94) | copy-start | bytes 786436
  29.2 37.0 %copy-start.20 = (f32[1,512,128]{2,1,0:T(8,128)}, f32[1,512,128]{2,1,0:T(8,128)S(1)}, u32[]{:S(2)}) copy-start(f32[1,512,128]{2,1,0:T(8,128)S(1)} %get-tuple-element.95) | copy-start | bytes 786436
  34.9 14.1 %collective-permute-start.4 = (f32[2,512,128]{2,1,0:T(8,128)S(1)}, f32[2,512,128]{2,1,0:T(8,128)S(1)}, u32[]{:S(2)}, u32[]{:S(2)}) collective-permute-start(f32[2,512,128]{2,1,0:T(8,128)S(1)} %get-tuple-element.90), channel_id=1, source_target_pairs={{1,2},{2,1},{3,4},{4,3},{5,6},{6,5},{7,8},{8,7},{9,10},{10,9},{11,... | collective-permute-start | bytes 1572872 | tf_op jit(solution)/shard_map/ppermute | solution.py:22
  39.8 9.2 %collective-permute-start.5 = (f32[2,512,128]{2,1,0:T(8,128)S(1)}, f32[2,512,128]{2,1,0:T(8,128)S(1)}, u32[]{:S(2)}, u32[]{:S(2)}) collective-permute-start(f32[2,512,128]{2,1,0:T(8,128)S(1)} %get-tuple-element.91), channel_id=1, source_target_pairs={{0,1},{1,0},{2,3},{3,2},{4,5},{5,4},{6,7},{7,6},{8,9},{9,8},{10,11... | collective-permute-start | bytes 1572872 | tf_op jit(solution)/shard_map/ppermute | solution.py:23
  51.9 14.1 %collective-permute-start.6 = (f32[2,512,128]{2,1,0:T(8,128)S(1)}, f32[2,512,128]{2,1,0:T(8,128)S(1)}, u32[]{:S(2)}, u32[]{:S(2)}) collective-permute-start(f32[2,512,128]{2,1,0:T(8,128)S(1)} %get-tuple-element.86), channel_id=1, source_target_pairs={{1,2},{2,1},{3,4},{4,3},{5,6},{6,5},{7,8},{8,7},{9,10},{10,9},{11,... | collective-permute-start | bytes 1572872 | tf_op jit(solution)/shard_map/ppermute | solution.py:22
  56.8 9.2 %collective-permute-start.7 = (f32[2,512,128]{2,1,0:T(8,128)S(1)}, f32[2,512,128]{2,1,0:T(8,128)S(1)}, u32[]{:S(2)}, u32[]{:S(2)}) collective-permute-start(f32[2,512,128]{2,1,0:T(8,128)S(1)} %get-tuple-element.87), channel_id=1, source_target_pairs={{0,1},{1,0},{2,3},{3,2},{4,5},{5,4},{6,7},{7,6},{8,9},{9,8},{10,11... | collective-permute-start | bytes 1572872 | tf_op jit(solution)/shard_map/ppermute | solution.py:23
  72.8 14.4 %collective-permute-start.8 = (f32[2,512,128]{2,1,0:T(8,128)}, f32[2,512,128]{2,1,0:T(8,128)}, u32[]{:S(2)}, u32[]{:S(2)}) collective-permute-start(f32[2,512,128]{2,1,0:T(8,128)} %get-tuple-element.82), channel_id=1, source_target_pairs={{1,2},{2,1},{3,4},{4,3},{5,6},{6,5},{7,8},{8,7},{9,10},{10,9},{11,... | collective-permute-start | bytes 1572872 | tf_op jit(solution)/shard_map/ppermute | solution.py:22
  77.7 9.6 %collective-permute-start.9 = (f32[2,512,128]{2,1,0:T(8,128)}, f32[2,512,128]{2,1,0:T(8,128)}, u32[]{:S(2)}, u32[]{:S(2)}) collective-permute-start(f32[2,512,128]{2,1,0:T(8,128)} %get-tuple-element.83), channel_id=1, source_target_pairs={{0,1},{1,0},{2,3},{3,2},{4,5},{5,4},{6,7},{7,6},{8,9},{9,8},{10,11... | collective-permute-start | bytes 1572872 | tf_op jit(solution)/shard_map/ppermute | solution.py:23
  97.0 52.1 %all-to-all-start = ((f32[16,4,64,128]{3,2,1,0:T(8,128)}), f32[16,4,64,128]{3,2,1,0:T(8,128)}, u32[]{:S(2)}, u32[]{:S(2)}) async-start(f32[16,4,64,128]{3,2,1,0:T(8,128)} %copy_bitcast_fusion), calls=%async_computation | async-start | bytes 4194304 | tf_op jit(solution)/shard_map/all_to_all | solution.py:79
  161.0 20.4 %collective-permute-start.10 = (f32[34,64,128]{2,1,0:T(8,128)S(1)}, f32[34,64,128]{2,1,0:T(8,128)S(1)}, u32[]{:S(2)}, u32[]{:S(2)}) collective-permute-start(f32[34,64,128]{2,1,0:T(8,128)S(1)} %get-tuple-element.8), channel_id=1, source_target_pairs={{1,2},{2,1},{3,4},{4,3},{5,6},{6,5},{7,8},{8,7},{9,10},{10,9},{11,... | collective-permute-start | bytes 3342344 | tf_op jit(solution)/shard_map/ppermute | solution.py:22
  166.3 15.2 %collective-permute-start.11 = (f32[34,64,128]{2,1,0:T(8,128)S(1)}, f32[34,64,128]{2,1,0:T(8,128)S(1)}, u32[]{:S(2)}, u32[]{:S(2)}) collective-permute-start(f32[34,64,128]{2,1,0:T(8,128)S(1)} %get-tuple-element.9), channel_id=1, source_target_pairs={{0,1},{1,0},{2,3},{3,2},{4,5},{5,4},{6,7},{7,6},{8,9},{9,8},{10,11... | collective-permute-start | bytes 3342344 | tf_op jit(solution)/shard_map/ppermute | solution.py:23
  183.8 9.9 %collective-permute-start.12 = (f32[4,64,128]{2,1,0:T(8,128)S(1)}, f32[4,64,128]{2,1,0:T(8,128)S(1)}, u32[]{:S(2)}, u32[]{:S(2)}) collective-permute-start(f32[4,64,128]{2,1,0:T(8,128)S(1)} %fusion.213), channel_id=1, source_target_pairs={{1,2},{2,1},{3,4},{4,3},{5,6},{6,5},{7,8},{8,7},{9,10},{10,9},{11,... | collective-permute-start | bytes 393224 | tf_op jit(solution)/shard_map/ppermute | solution.py:22
  189.0 4.6 %collective-permute-start.13 = (f32[4,64,128]{2,1,0:T(8,128)S(1)}, f32[4,64,128]{2,1,0:T(8,128)S(1)}, u32[]{:S(2)}, u32[]{:S(2)}) collective-permute-start(f32[4,64,128]{2,1,0:T(8,128)S(1)} %fusion.213), channel_id=1, source_target_pairs={{0,1},{1,0},{2,3},{3,2},{4,5},{5,4},{6,7},{7,6},{8,9},{9,8},{10,11... | collective-permute-start | bytes 393224 | tf_op jit(solution)/shard_map/ppermute | solution.py:23
  195.5 9.9 %collective-permute-start.14 = (f32[4,64,128]{2,1,0:T(8,128)S(1)}, f32[4,64,128]{2,1,0:T(8,128)S(1)}, u32[]{:S(2)}, u32[]{:S(2)}) collective-permute-start(f32[4,64,128]{2,1,0:T(8,128)S(1)} %fusion.221), channel_id=1, source_target_pairs={{1,2},{2,1},{3,4},{4,3},{5,6},{6,5},{7,8},{8,7},{9,10},{10,9},{11,... | collective-permute-start | bytes 393224 | tf_op jit(solution)/shard_map/ppermute | solution.py:22
  200.8 4.6 %collective-permute-start.15 = (f32[4,64,128]{2,1,0:T(8,128)S(1)}, f32[4,64,128]{2,1,0:T(8,128)S(1)}, u32[]{:S(2)}, u32[]{:S(2)}) collective-permute-start(f32[4,64,128]{2,1,0:T(8,128)S(1)} %fusion.221), channel_id=1, source_target_pairs={{0,1},{1,0},{2,3},{3,2},{4,5},{5,4},{6,7},{7,6},{8,9},{9,8},{10,11... | collective-permute-start | bytes 393224 | tf_op jit(solution)/shard_map/ppermute | solution.py:23
  207.3 9.5 %collective-permute-start.16 = (f32[3,64,128]{2,1,0:T(8,128)S(1)}, f32[3,64,128]{2,1,0:T(8,128)S(1)}, u32[]{:S(2)}, u32[]{:S(2)}) collective-permute-start(f32[3,64,128]{2,1,0:T(8,128)S(1)} %get-tuple-element.131), channel_id=1, source_target_pairs={{1,2},{2,1},{3,4},{4,3},{5,6},{6,5},{7,8},{8,7},{9,10},{10,9},{11,... | collective-permute-start | bytes 294920 | tf_op jit(solution)/shard_map/ppermute | solution.py:22
  212.6 4.3 %collective-permute-start.17 = (f32[3,64,128]{2,1,0:T(8,128)S(1)}, f32[3,64,128]{2,1,0:T(8,128)S(1)}, u32[]{:S(2)}, u32[]{:S(2)}) collective-permute-start(f32[3,64,128]{2,1,0:T(8,128)S(1)} %get-tuple-element.132), channel_id=1, source_target_pairs={{0,1},{1,0},{2,3},{3,2},{4,5},{5,4},{6,7},{7,6},{8,9},{9,8},{10,11... | collective-permute-start | bytes 294920 | tf_op jit(solution)/shard_map/ppermute | solution.py:23
  220.6 35.6 %all-to-all-start.1 = ((f32[16,5,32,128]{3,2,1,0:T(8,128)}), f32[16,5,32,128]{3,2,1,0:T(8,128)}, u32[]{:S(2)}, u32[]{:S(2)}) async-start(f32[16,5,32,128]{3,2,1,0:T(8,128)} %constant_dynamic-update-slice_fusion.18), calls=%async_computation.1 | async-start | bytes 2621440 | tf_op jit(solution)/shard_map/all_to_all | solution.py:126
  259.0 5.3 %collective-permute-start.18 = (f32[1,512,128]{2,1,0:T(8,128)S(1)}, f32[1,512,128]{2,1,0:T(8,128)S(1)}, u32[]{:S(2)}, u32[]{:S(2)}) collective-permute-start(f32[1,512,128]{2,1,0:T(8,128)S(1)} %bitcast.297), channel_id=1, source_target_pairs={{0,1},{1,0},{2,3},{3,2},{4,5},{5,4},{6,7},{7,6},{8,9},{9,8},{10,11... | collective-permute-start | bytes 786440 | tf_op jit(solution)/shard_map/ppermute | solution.py:129
  (30 other events, 212.9 us)

commit v4 on v3

--- a/solution.py
+++ b/solution.py
@@ -76,7 +76,11 @@
 
     blocks = jnp.pad(element, ((0, 0), (halo, halo), (0, 0))).reshape(planes, -1, part, lanes)
     widened = jnp.concatenate([blocks[:, :-1], blocks[:, 1:]], axis=2)
+    tall = jnp.pad(jnp.stack([own, side, west]), ((0, 0), (0, 0), (halo, halo), (0, 0)))
+    factors = lax.dynamic_slice_in_dim(tall, slot * part, window, axis=2)
+    widened, element, factors, own, side, west, start = lax.optimization_barrier((widened, element, factors, own, side, west, start))
     terms = lax.all_to_all(widened.transpose(1, 0, 2, 3), "tm", 0, 0, tiled=True)
+    terms, element, factors, own, side, west, start = lax.optimization_barrier((terms, element, factors, own, side, west, start))
 
     last = slices - 2
     groups = [(g, min(g + SPAN, last)) for g in range(0, last, SPAN)]
@@ -87,8 +91,6 @@
             depth[n] = width[g] - (n - g)
     deep = SPAN - 1
     inner = [0 if n in width and n else depth[n] for n in range(last + 1)]
-    tall = jnp.pad(jnp.stack([own, side, west]), ((0, 0), (0, 0), (halo, halo), (0, 0)))
-    factors = lax.dynamic_slice_in_dim(tall, slot * part, window, axis=2)
     before, after = exchanged(
         jnp.concatenate([terms[n, :k] for n, k in enumerate(inner) if k] + [factors[i, :deep] for i in range(3)]),
         jnp.concatenate([terms[n, planes - k :] for n, k in enumerate(inner) if k] + [factors[i, planes - deep :] for i in range(3)]),
@@ -123,7 +125,11 @@
         kept = state[:, halo : halo + part]
         sent.append(jnp.concatenate([kept[k : k + planes], jnp.where(even, kept[k - 1 : k], kept[k + planes : k + planes + 1])]))
 
-    back = lax.all_to_all(jnp.stack(sent), "tm", 0, 0, tiled=True)
+    sent, element, own, side, west, start, slot, even = lax.optimization_barrier(
+        (jnp.stack(sent), element, own, side, west, start, slot, even)
+    )
+    back = lax.all_to_all(sent, "tm", 0, 0, tiled=True)
+    back, element, own, side, west, start, slot, even = lax.optimization_barrier((back, element, own, side, west, start, slot, even))
     arrived = back.transpose(1, 0, 2, 3).reshape(planes + 1, rows, lanes)
     following, across = arrived[:planes], arrived[planes:]
     beside = lax.ppermute(jnp.where(even, following[planes - 1 :], following[:1]), "space", beside_pairs())

time: 269 us -> 247 us (0.918)
  blocking collectives: 0 us -> 88.6 us
  waiting for transfers between devices: 136 us -> 71.5 us
  starting transfers between devices: 63.7 us -> 46 us
  other arithmetic: 42.1 us -> 25.7 us
  local copies, waits for them, and re-layouts: 24.1 us -> 12.8 us
    all_to_all x0 -> x2, blocking collectives: none -> 88.6 us  [the longest x1 53.2 us: on_device(): lax.all_to_all(widened.transpose(1, 0, 2, 3), 'tm', 0, 0, tiled=True)]
    all_to_all x2 -> x0, waiting for transfers between devices: 73 us -> none  [the longest x1 41.7 us: on_device(): lax.all_to_all(widened.transpose(1, 0, 2, 3), 'tm', 0, 0, tiled=True)]
    all_to_all x2 -> x0, starting transfers between devices: 13.7 us -> none  [the longest x1 9.27 us: on_device(): lax.all_to_all(widened.transpose(1, 0, 2, 3), 'tm', 0, 0, tiled=True)]
    unnamed x81 -> x93, local copies, waits for them, and re-layouts: 18 us -> 8.59 us
    unnamed x14, other arithmetic: 8.9 us -> 0.12 us
    ppermute x9, waiting for transfers between devices: 63 us -> 71.5 us  [exchanged(): across = lax.ppermute(jnp.where(even, low, high), 'space', far)]
    ppermute x1, starting transfers between devices: 4.16 us -> 0.09 us  [on_device(): lax.ppermute(jnp.where(even, following[planes - 1:], following[:1]), 'spa...]
    another operation x2 -> x1, other arithmetic: 3.8 us -> 0.06 us  [on_device(): jnp.stack([own, side, west])]
  transfers between devices with their start and end apart: 21 -> 19, of which waited for: 11 -> 8; matrix products, arithmetic and copies ran while one was open for 4% -> 1% of each run, Pallas kernels for 0% -> 0%
where the time goes in v4:
time: 247 us
  blocking collectives  88.6 us (36%)
  waiting for transfers between devices  71.5 us (29%)
  starting transfers between devices  46 us (19%)
  other arithmetic  25.7 us (10%)
  local copies, waits for them, and re-layouts  12.8 us (5%)
    ppermute x9, waiting for transfers between devices, exchanged(): across = lax.ppermute(jnp.where(even, low, high), 'space', far)  71.5 us
    all_to_all x1, blocking collectives, on_device(): lax.all_to_all(widened.transpose(1, 0, 2, 3), 'tm', 0, 0, tiled=True)  53.2 us
    ppermute x9, starting transfers between devices, exchanged(): across = lax.ppermute(jnp.where(even, low, high), 'space', far)  44.9 us
    all_to_all x1, blocking collectives, on_device(): back = lax.all_to_all(sent, 'tm', 0, 0, tiled=True)  35.4 us
    unnamed x93, local copies, waits for them, and re-layouts  8.59 us
    add x5, other arithmetic, on_device(): centre + d * (total - 6.0 * centre) - c * (centre - upwind) - l * centre + h  6.75 us
  transfers between devices with their start and end apart: 19, of which 8 were waited for; matrix products, arithmetic and copies ran while one was open for 1% of the time, Pallas kernels for 0%

profile of v4, /device:TPU:25, one launch (start us, length us, event | category | flops | bytes accessed | tf_op | source)
XLA Modules:
  0.0 246.8 jit_solution(12620418883633956567)
XLA Ops:
  3.2 5.0 %collective-permute-start.2 = (f32[2048,128]{1,0:T(8,128)S(1)}, f32[2048,128]{1,0:T(8,128)S(1)}, u32[]{:S(2)}, u32[]{:S(2)}) collective-permute-start(f32[2048,128]{1,0:T(8,128)S(1)} %get-tuple-element.108), channel_id=1, source_target_pairs={{1,2},{2,1},{3,4},{4,3},{5,6},{6,5},{7,8},{8,7},{9,10},{10,9},{11,... | collective-permute-start | bytes 3145736 | tf_op jit(solution)/shard_map/ppermute | solution.py:22
  8.4 4.3 %collective-permute-start = (f32[2,512,128]{2,1,0:T(8,128)S(1)}, f32[2,512,128]{2,1,0:T(8,128)S(1)}, u32[]{:S(2)}, u32[]{:S(2)}) collective-permute-start(f32[2,512,128]{2,1,0:T(8,128)S(1)} %get-tuple-element.173), channel_id=1, source_target_pairs={{1,2},{2,1},{3,4},{4,3},{5,6},{6,5},{7,8},{8,7},{9,10},{10,9},{11,... | collective-permute-start | bytes 1572872 | tf_op jit(solution)/shard_map/ppermute | solution.py:22
  12.8 15.9 %collective-permute-done = f32[2,512,128]{2,1,0:T(8,128)S(1)} collective-permute-done((f32[2,512,128]{2,1,0:T(8,128)S(1)}, f32[2,512,128]{2,1,0:T(8,128)S(1)}, u32[]{:S(2)}, u32[]{:S(2)}) %collective-permute-start) | collective-permute-done | bytes 524320 | tf_op jit(solution)/shard_map/ppermute | solution.py:22
  31.4 2.6 %fusion.230 = (f32[6,512,128]{2,1,0:T(8,128)}, f32[6,512,128]{2,1,0:T(8,128)S(1)}) fusion(f32[8,512,128]{2,1,0:T(8,128)S(1)} %pad_maximum_fusion, f32[1,512,128]{2,1,0:T(8,128)S(1)} %get-tuple-element.160, f32[4,512,128]{2,1,0:T(8,128)S(1)} %copy-done, f32[1,512,128]{2,1,0:T(8,128)S(1)} %get-tuple-element.156, f32[1,512,128]{2,1,0:T(8,128)S(1)} %get-tuple-element.161, ...), kind=kLoop, calls=%fused_computation.546 | loop fusion | flops 9830400 | bytes 15204352 | tf_op jit(solution)/shard_map/slice | solution.py:69
  34.9 4.9 %collective-permute-start.4 = (f32[2,512,128]{2,1,0:T(8,128)S(1)}, f32[2,512,128]{2,1,0:T(8,128)S(1)}, u32[]{:S(2)}, u32[]{:S(2)}) collective-permute-start(f32[2,512,128]{2,1,0:T(8,128)S(1)} %get-tuple-element.153), channel_id=1, source_target_pairs={{1,2},{2,1},{3,4},{4,3},{5,6},{6,5},{7,8},{8,7},{9,10},{10,9},{11,... | collective-permute-start | bytes 1572872 | tf_op jit(solution)/shard_map/ppermute | solution.py:22
  39.9 9.1 %collective-permute-done.4 = f32[2,512,128]{2,1,0:T(8,128)S(1)} collective-permute-done((f32[2,512,128]{2,1,0:T(8,128)S(1)}, f32[2,512,128]{2,1,0:T(8,128)S(1)}, u32[]{:S(2)}, u32[]{:S(2)}) %collective-permute-start.4) | collective-permute-done | bytes 524320 | tf_op jit(solution)/shard_map/ppermute | solution.py:22
  51.8 4.9 %collective-permute-start.6 = (f32[2,512,128]{2,1,0:T(8,128)S(1)}, f32[2,512,128]{2,1,0:T(8,128)S(1)}, u32[]{:S(2)}, u32[]{:S(2)}) collective-permute-start(f32[2,512,128]{2,1,0:T(8,128)S(1)} %get-tuple-element.149), channel_id=1, source_target_pairs={{1,2},{2,1},{3,4},{4,3},{5,6},{6,5},{7,8},{8,7},{9,10},{10,9},{11,... | collective-permute-start | bytes 1572872 | tf_op jit(solution)/shard_map/ppermute | solution.py:22
  56.8 9.1 %collective-permute-done.6 = f32[2,512,128]{2,1,0:T(8,128)S(1)} collective-permute-done((f32[2,512,128]{2,1,0:T(8,128)S(1)}, f32[2,512,128]{2,1,0:T(8,128)S(1)}, u32[]{:S(2)}, u32[]{:S(2)}) %collective-permute-start.6) | collective-permute-done | bytes 524320 | tf_op jit(solution)/shard_map/ppermute | solution.py:22
  67.9 2.3 broadcast_divide_fusion
  72.3 4.9 %collective-permute-start.8 = (f32[2,512,128]{2,1,0:T(8,128)}, f32[2,512,128]{2,1,0:T(8,128)}, u32[]{:S(2)}, u32[]{:S(2)}) collective-permute-start(f32[2,512,128]{2,1,0:T(8,128)} %get-tuple-element.145), channel_id=1, source_target_pairs={{1,2},{2,1},{3,4},{4,3},{5,6},{6,5},{7,8},{8,7},{9,10},{10,9},{11,... | collective-permute-start | bytes 1572872 | tf_op jit(solution)/shard_map/ppermute | solution.py:22
  77.5 9.3 %collective-permute-done.8 = f32[2,512,128]{2,1,0:T(8,128)} collective-permute-done((f32[2,512,128]{2,1,0:T(8,128)}, f32[2,512,128]{2,1,0:T(8,128)}, u32[]{:S(2)}, u32[]{:S(2)}) %collective-permute-start.8) | collective-permute-done | bytes 524320 | tf_op jit(solution)/shard_map/ppermute | solution.py:22
  89.8 1.7 fusion.43
  92.1 2.2 subtract_select_fusion
  96.0 53.2 %all_to_all.10 = f32[16,4,64,128]{3,2,1,0:T(8,128)S(1)} all-to-all(f32[16,4,64,128]{3,2,1,0:T(8,128)S(1)} %bitcast.235), channel_id=1, replica_groups=mesh['tm'=16,'space'=16] {'tm'}, dimensions={0} | all-to-all | bytes 4194304 | tf_op jit(solution)/shard_map/all_to_all | solution.py:82
  149.9 5.2 %collective-permute-start.10 = (f32[34,64,128]{2,1,0:T(8,128)S(1)}, f32[34,64,128]{2,1,0:T(8,128)S(1)}, u32[]{:S(2)}, u32[]{:S(2)}) collective-permute-start(f32[34,64,128]{2,1,0:T(8,128)S(1)} %get-tuple-element.70), channel_id=1, source_target_pairs={{1,2},{2,1},{3,4},{4,3},{5,6},{6,5},{7,8},{8,7},{9,10},{10,9},{11,... | collective-permute-start | bytes 3342344 | tf_op jit(solution)/shard_map/ppermute | solution.py:22
  155.4 14.8 %collective-permute-done.10 = f32[34,64,128]{2,1,0:T(8,128)S(1)} collective-permute-done((f32[34,64,128]{2,1,0:T(8,128)S(1)}, f32[34,64,128]{2,1,0:T(8,128)S(1)}, u32[]{:S(2)}, u32[]{:S(2)}) %collective-permute-start.10) | collective-permute-done | bytes 1114144 | tf_op jit(solution)/shard_map/ppermute | solution.py:22
  172.0 5.2 %collective-permute-start.12 = (f32[4,64,128]{2,1,0:T(8,128)S(1)}, f32[4,64,128]{2,1,0:T(8,128)S(1)}, u32[]{:S(2)}, u32[]{:S(2)}) collective-permute-start(f32[4,64,128]{2,1,0:T(8,128)S(1)} %fusion.212), channel_id=1, source_target_pairs={{1,2},{2,1},{3,4},{4,3},{5,6},{6,5},{7,8},{8,7},{9,10},{10,9},{11,... | collective-permute-start | bytes 393224 | tf_op jit(solution)/shard_map/ppermute | solution.py:22
  177.3 4.5 %collective-permute-done.12 = f32[4,64,128]{2,1,0:T(8,128)S(1)} collective-permute-done((f32[4,64,128]{2,1,0:T(8,128)S(1)}, f32[4,64,128]{2,1,0:T(8,128)S(1)}, u32[]{:S(2)}, u32[]{:S(2)}) %collective-permute-start.12) | collective-permute-done | bytes 131104 | tf_op jit(solution)/shard_map/ppermute | solution.py:22
  183.0 5.2 %collective-permute-start.14 = (f32[4,64,128]{2,1,0:T(8,128)S(1)}, f32[4,64,128]{2,1,0:T(8,128)S(1)}, u32[]{:S(2)}, u32[]{:S(2)}) collective-permute-start(f32[4,64,128]{2,1,0:T(8,128)S(1)} %fusion.220), channel_id=1, source_target_pairs={{1,2},{2,1},{3,4},{4,3},{5,6},{6,5},{7,8},{8,7},{9,10},{10,9},{11,... | collective-permute-start | bytes 393224 | tf_op jit(solution)/shard_map/ppermute | solution.py:22
  188.2 4.6 %collective-permute-done.14 = f32[4,64,128]{2,1,0:T(8,128)S(1)} collective-permute-done((f32[4,64,128]{2,1,0:T(8,128)S(1)}, f32[4,64,128]{2,1,0:T(8,128)S(1)}, u32[]{:S(2)}, u32[]{:S(2)}) %collective-permute-start.14) | collective-permute-done | bytes 131104 | tf_op jit(solution)/shard_map/ppermute | solution.py:22
  193.9 5.2 %collective-permute-start.16 = (f32[3,64,128]{2,1,0:T(8,128)S(1)}, f32[3,64,128]{2,1,0:T(8,128)S(1)}, u32[]{:S(2)}, u32[]{:S(2)}) collective-permute-start(f32[3,64,128]{2,1,0:T(8,128)S(1)} %get-tuple-element.194), channel_id=1, source_target_pairs={{1,2},{2,1},{3,4},{4,3},{5,6},{6,5},{7,8},{8,7},{9,10},{10,9},{11,... | collective-permute-start | bytes 294920 | tf_op jit(solution)/shard_map/ppermute | solution.py:22
  199.3 4.1 %collective-permute-done.16 = f32[3,64,128]{2,1,0:T(8,128)S(1)} collective-permute-done((f32[3,64,128]{2,1,0:T(8,128)S(1)}, f32[3,64,128]{2,1,0:T(8,128)S(1)}, u32[]{:S(2)}, u32[]{:S(2)}) %collective-permute-start.16) | collective-permute-done | bytes 98336 | tf_op jit(solution)/shard_map/ppermute | solution.py:22
  204.6 35.4 %all_to_all.11 = f32[16,5,32,128]{3,2,1,0:T(8,128)S(1)} all-to-all(f32[16,5,32,128]{3,2,1,0:T(8,128)S(1)} %constant_dynamic-update-slice_fusion.18), channel_id=1, replica_groups=mesh['tm'=16,'space'=16] {'tm'}, dimensions={0} | all-to-all | bytes 2621440 | tf_op jit(solution)/shard_map/all_to_all | solution.py:131
  244.6 2.1 fusion.105
  (226 shorter events, 28.8 us)
Async XLA Ops:
  3.2 25.7 %collective-permute-start.2 = (f32[2048,128]{1,0:T(8,128)S(1)}, f32[2048,128]{1,0:T(8,128)S(1)}, u32[]{:S(2)}, u32[]{:S(2)}) collective-permute-start(f32[2048,128]{1,0:T(8,128)S(1)} %get-tuple-element.108), channel_id=1, source_target_pairs={{1,2},{2,1},{3,4},{4,3},{5,6},{6,5},{7,8},{8,7},{9,10},{10,9},{11,... | collective-permute-start | bytes 3145736 | tf_op jit(solution)/shard_map/ppermute | solution.py:22
  8.2 20.7 %collective-permute-start.3 = (f32[2048,128]{1,0:T(8,128)S(1)}, f32[2048,128]{1,0:T(8,128)S(1)}, u32[]{:S(2)}, u32[]{:S(2)}) collective-permute-start(f32[2048,128]{1,0:T(8,128)S(1)} %get-tuple-element.109), channel_id=1, source_target_pairs={{0,1},{1,0},{2,3},{3,2},{4,5},{5,4},{6,7},{7,6},{8,9},{9,8},{10,11... | collective-permute-start | bytes 3145736 | tf_op jit(solution)/shard_map/ppermute | solution.py:23
  8.4 20.3 %collective-permute-start = (f32[2,512,128]{2,1,0:T(8,128)S(1)}, f32[2,512,128]{2,1,0:T(8,128)S(1)}, u32[]{:S(2)}, u32[]{:S(2)}) collective-permute-start(f32[2,512,128]{2,1,0:T(8,128)S(1)} %get-tuple-element.173), channel_id=1, source_target_pairs={{1,2},{2,1},{3,4},{4,3},{5,6},{6,5},{7,8},{8,7},{9,10},{10,9},{11,... | collective-permute-start | bytes 1572872 | tf_op jit(solution)/shard_map/ppermute | solution.py:22
  12.7 16.0 %collective-permute-start.1 = (f32[2,512,128]{2,1,0:T(8,128)S(1)}, f32[2,512,128]{2,1,0:T(8,128)S(1)}, u32[]{:S(2)}, u32[]{:S(2)}) collective-permute-start(f32[2,512,128]{2,1,0:T(8,128)S(1)} %get-tuple-element.174), channel_id=1, source_target_pairs={{0,1},{1,0},{2,3},{3,2},{4,5},{5,4},{6,7},{7,6},{8,9},{9,8},{10,11... | collective-permute-start | bytes 1572872 | tf_op jit(solution)/shard_map/ppermute | solution.py:23
  29.2 37.0 %copy-start.20 = (f32[1,512,128]{2,1,0:T(8,128)}, f32[1,512,128]{2,1,0:T(8,128)S(1)}, u32[]{:S(2)}) copy-start(f32[1,512,128]{2,1,0:T(8,128)S(1)} %get-tuple-element.156) | copy-start | bytes 786436
  29.2 37.0 %copy-start.22 = (f32[1,512,128]{2,1,0:T(8,128)}, f32[1,512,128]{2,1,0:T(8,128)S(1)}, u32[]{:S(2)}) copy-start(f32[1,512,128]{2,1,0:T(8,128)S(1)} %get-tuple-element.157) | copy-start | bytes 786436
  29.2 37.0 %copy-start.24 = (f32[1,512,128]{2,1,0:T(8,128)}, f32[1,512,128]{2,1,0:T(8,128)S(1)}, u32[]{:S(2)}) copy-start(f32[1,512,128]{2,1,0:T(8,128)S(1)} %get-tuple-element.158) | copy-start | bytes 786436
  29.3 36.9 %copy-start.26 = (f32[1,512,128]{2,1,0:T(8,128)}, f32[1,512,128]{2,1,0:T(8,128)S(1)}, u32[]{:S(2)}) copy-start(f32[1,512,128]{2,1,0:T(8,128)S(1)} %get-tuple-element.159) | copy-start | bytes 786436
  29.3 36.9 %copy-start.28 = (f32[1,512,128]{2,1,0:T(8,128)}, f32[1,512,128]{2,1,0:T(8,128)S(1)}, u32[]{:S(2)}) copy-start(f32[1,512,128]{2,1,0:T(8,128)S(1)} %get-tuple-element.160) | copy-start | bytes 786436
  34.9 14.1 %collective-permute-start.4 = (f32[2,512,128]{2,1,0:T(8,128)S(1)}, f32[2,512,128]{2,1,0:T(8,128)S(1)}, u32[]{:S(2)}, u32[]{:S(2)}) collective-permute-start(f32[2,512,128]{2,1,0:T(8,128)S(1)} %get-tuple-element.153), channel_id=1, source_target_pairs={{1,2},{2,1},{3,4},{4,3},{5,6},{6,5},{7,8},{8,7},{9,10},{10,9},{11,... | collective-permute-start | bytes 1572872 | tf_op jit(solution)/shard_map/ppermute | solution.py:22
  39.8 9.2 %collective-permute-start.5 = (f32[2,512,128]{2,1,0:T(8,128)S(1)}, f32[2,512,128]{2,1,0:T(8,128)S(1)}, u32[]{:S(2)}, u32[]{:S(2)}) collective-permute-start(f32[2,512,128]{2,1,0:T(8,128)S(1)} %get-tuple-element.154), channel_id=1, source_target_pairs={{0,1},{1,0},{2,3},{3,2},{4,5},{5,4},{6,7},{7,6},{8,9},{9,8},{10,11... | collective-permute-start | bytes 1572872 | tf_op jit(solution)/shard_map/ppermute | solution.py:23
  51.8 14.1 %collective-permute-start.6 = (f32[2,512,128]{2,1,0:T(8,128)S(1)}, f32[2,512,128]{2,1,0:T(8,128)S(1)}, u32[]{:S(2)}, u32[]{:S(2)}) collective-permute-start(f32[2,512,128]{2,1,0:T(8,128)S(1)} %get-tuple-element.149), channel_id=1, source_target_pairs={{1,2},{2,1},{3,4},{4,3},{5,6},{6,5},{7,8},{8,7},{9,10},{10,9},{11,... | collective-permute-start | bytes 1572872 | tf_op jit(solution)/shard_map/ppermute | solution.py:22
  56.7 9.2 %collective-permute-start.7 = (f32[2,512,128]{2,1,0:T(8,128)S(1)}, f32[2,512,128]{2,1,0:T(8,128)S(1)}, u32[]{:S(2)}, u32[]{:S(2)}) collective-permute-start(f32[2,512,128]{2,1,0:T(8,128)S(1)} %get-tuple-element.150), channel_id=1, source_target_pairs={{0,1},{1,0},{2,3},{3,2},{4,5},{5,4},{6,7},{7,6},{8,9},{9,8},{10,11... | collective-permute-start | bytes 1572872 | tf_op jit(solution)/shard_map/ppermute | solution.py:23
  72.3 14.4 %collective-permute-start.8 = (f32[2,512,128]{2,1,0:T(8,128)}, f32[2,512,128]{2,1,0:T(8,128)}, u32[]{:S(2)}, u32[]{:S(2)}) collective-permute-start(f32[2,512,128]{2,1,0:T(8,128)} %get-tuple-element.145), channel_id=1, source_target_pairs={{1,2},{2,1},{3,4},{4,3},{5,6},{6,5},{7,8},{8,7},{9,10},{10,9},{11,... | collective-permute-start | bytes 1572872 | tf_op jit(solution)/shard_map/ppermute | solution.py:22
  77.2 9.6 %collective-permute-start.9 = (f32[2,512,128]{2,1,0:T(8,128)}, f32[2,512,128]{2,1,0:T(8,128)}, u32[]{:S(2)}, u32[]{:S(2)}) collective-permute-start(f32[2,512,128]{2,1,0:T(8,128)} %get-tuple-element.146), channel_id=1, source_target_pairs={{0,1},{1,0},{2,3},{3,2},{4,5},{5,4},{6,7},{7,6},{8,9},{9,8},{10,11... | collective-permute-start | bytes 1572872 | tf_op jit(solution)/shard_map/ppermute | solution.py:23
  149.9 20.4 %collective-permute-start.10 = (f32[34,64,128]{2,1,0:T(8,128)S(1)}, f32[34,64,128]{2,1,0:T(8,128)S(1)}, u32[]{:S(2)}, u32[]{:S(2)}) collective-permute-start(f32[34,64,128]{2,1,0:T(8,128)S(1)} %get-tuple-element.70), channel_id=1, source_target_pairs={{1,2},{2,1},{3,4},{4,3},{5,6},{6,5},{7,8},{8,7},{9,10},{10,9},{11,... | collective-permute-start | bytes 3342344 | tf_op jit(solution)/shard_map/ppermute | solution.py:22
  155.1 15.2 %collective-permute-start.11 = (f32[34,64,128]{2,1,0:T(8,128)S(1)}, f32[34,64,128]{2,1,0:T(8,128)S(1)}, u32[]{:S(2)}, u32[]{:S(2)}) collective-permute-start(f32[34,64,128]{2,1,0:T(8,128)S(1)} %get-tuple-element.71), channel_id=1, source_target_pairs={{0,1},{1,0},{2,3},{3,2},{4,5},{5,4},{6,7},{7,6},{8,9},{9,8},{10,11... | collective-permute-start | bytes 3342344 | tf_op jit(solution)/shard_map/ppermute | solution.py:23
  171.9 5.5 %collective-permute-start.13 = (f32[4,64,128]{2,1,0:T(8,128)S(1)}, f32[4,64,128]{2,1,0:T(8,128)S(1)}, u32[]{:S(2)}, u32[]{:S(2)}) collective-permute-start(f32[4,64,128]{2,1,0:T(8,128)S(1)} %fusion.212), channel_id=1, source_target_pairs={{0,1},{1,0},{2,3},{3,2},{4,5},{5,4},{6,7},{7,6},{8,9},{9,8},{10,11... | collective-permute-start | bytes 393224 | tf_op jit(solution)/shard_map/ppermute | solution.py:23
  172.0 9.9 %collective-permute-start.12 = (f32[4,64,128]{2,1,0:T(8,128)S(1)}, f32[4,64,128]{2,1,0:T(8,128)S(1)}, u32[]{:S(2)}, u32[]{:S(2)}) collective-permute-start(f32[4,64,128]{2,1,0:T(8,128)S(1)} %fusion.212), channel_id=1, source_target_pairs={{1,2},{2,1},{3,4},{4,3},{5,6},{6,5},{7,8},{8,7},{9,10},{10,9},{11,... | collective-permute-start | bytes 393224 | tf_op jit(solution)/shard_map/ppermute | solution.py:22
  182.9 5.4 %collective-permute-start.15 = (f32[4,64,128]{2,1,0:T(8,128)S(1)}, f32[4,64,128]{2,1,0:T(8,128)S(1)}, u32[]{:S(2)}, u32[]{:S(2)}) collective-permute-start(f32[4,64,128]{2,1,0:T(8,128)S(1)} %fusion.220), channel_id=1, source_target_pairs={{0,1},{1,0},{2,3},{3,2},{4,5},{5,4},{6,7},{7,6},{8,9},{9,8},{10,11... | collective-permute-start | bytes 393224 | tf_op jit(solution)/shard_map/ppermute | solution.py:23
  183.0 9.9 %collective-permute-start.14 = (f32[4,64,128]{2,1,0:T(8,128)S(1)}, f32[4,64,128]{2,1,0:T(8,128)S(1)}, u32[]{:S(2)}, u32[]{:S(2)}) collective-permute-start(f32[4,64,128]{2,1,0:T(8,128)S(1)} %fusion.220), channel_id=1, source_target_pairs={{1,2},{2,1},{3,4},{4,3},{5,6},{6,5},{7,8},{8,7},{9,10},{10,9},{11,... | collective-permute-start | bytes 393224 | tf_op jit(solution)/shard_map/ppermute | solution.py:22
  193.9 9.5 %collective-permute-start.16 = (f32[3,64,128]{2,1,0:T(8,128)S(1)}, f32[3,64,128]{2,1,0:T(8,128)S(1)}, u32[]{:S(2)}, u32[]{:S(2)}) collective-permute-start(f32[3,64,128]{2,1,0:T(8,128)S(1)} %get-tuple-element.194), channel_id=1, source_target_pairs={{1,2},{2,1},{3,4},{4,3},{5,6},{6,5},{7,8},{8,7},{9,10},{10,9},{11,... | collective-permute-start | bytes 294920 | tf_op jit(solution)/shard_map/ppermute | solution.py:22
  199.1 4.3 %collective-permute-start.17 = (f32[3,64,128]{2,1,0:T(8,128)S(1)}, f32[3,64,128]{2,1,0:T(8,128)S(1)}, u32[]{:S(2)}, u32[]{:S(2)}) collective-permute-start(f32[3,64,128]{2,1,0:T(8,128)S(1)} %get-tuple-element.195), channel_id=1, source_target_pairs={{0,1},{1,0},{2,3},{3,2},{4,5},{5,4},{6,7},{7,6},{8,9},{9,8},{10,11... | collective-permute-start | bytes 294920 | tf_op jit(solution)/shard_map/ppermute | solution.py:23
  240.3 2.2 collective-permute-start.18
  (34 other events, 144.7 us)

commit v5 on v3

v5 whole, which is shorter than its diff:
```python
import jax
import jax.numpy as jnp
from jax import lax
from jax.sharding import PartitionSpec as P

FINE = 8
SPAN = 4
ROUNDS = 2
HALO = 8
OLD_TURN = 1


def swaps(pairs):
    return [route for a, b in pairs for route in ((a, b), (b, a))]


def beside_pairs():
    return swaps([(i, i + 1) for i in range(0, lax.axis_size("space") - 1, 2)])


def across_pairs():
    return swaps([(i, i + 1) for i in range(1, lax.axis_size("space") - 1, 2)])


def exchanged(low, high, even):
    across = lax.ppermute(jnp.where(even, low, high), "space", across_pairs())
    beside = lax.ppermute(jnp.where(even, high, low), "space", beside_pairs())
    return jnp.where(even, across, beside), jnp.where(even, beside, across)


def around(wide):
    padded = jnp.pad(wide, ((0, 0), (1, 1), (1, 1)))
    total = padded[2:, 1:-1, 1:-1] + padded[:-2, 1:-1, 1:-1]
    total = total + padded[1:-1, 2:, 1:-1] + padded[1:-1, :-2, 1:-1]
    total = total + padded[1:-1, 1:-1, 2:] + padded[1:-1, 1:-1, :-2]
    return total, wide[:-2]


def fine_step(wide, terms):
    d, c, l, h = terms
    total, upwind = around(wide)
    centre = wide[1:-1]
    return centre + d * (total - 6.0 * centre) - c * (centre - upwind) - l * centre + h


def coarse_linear(wide, terms):
    d, c, l = terms
    total, upwind = around(wide)
    return (wide[1:-1] + FINE * (d * total + c * upwind)) / (1.0 + FINE * (6.0 * d + c + l))


def snake(index):
    turned = (index // 2) % 2
    return index + turned * (1 - 2 * (index % 2))


def on_device(slice_starts, diffusion, courant, loss, heating):
    start = slice_starts[0]
    planes, rows, lanes = start.shape
    slices = lax.axis_size("tm")
    slot = lax.axis_index("tm")
    even = lax.axis_index("space") % 2 == 0
    part = rows // slices
    window = part + 2 * HALO
    order = [snake(i) for i in range(slices)]
    raw = (diffusion, courant, loss, heating)

    def flat(*arrays):
        return jnp.concatenate([a.reshape(-1, lanes) for a in arrays])

    edge = ROUNDS - 1
    before, after = exchanged(flat(*(x[:edge] for x in raw)), flat(*(x[planes - edge :] for x in raw)), even)
    before, after = before.reshape(4, edge, rows, lanes), after.reshape(4, edge, rows, lanes)
    fine_terms = [jnp.concatenate([before[i], raw[i], after[i]]) for i in range(4)]

    state = start
    for turn in range(FINE // ROUNDS):
        low, high = state[:ROUNDS], state[planes - ROUNDS :]
        if turn == OLD_TURN:
            low, high, first = lax.optimization_barrier((low, high, first))
        low, high = exchanged(low, high, even)
        if turn == OLD_TURN:
            old = coarse_linear(first, raw[:3])
        state = jnp.concatenate([low, state, high])
        if turn == 0:
            first = state[ROUNDS - 1 : ROUNDS + planes + 1]
        for step in range(ROUNDS):
            state = fine_step(state, [t[step : t.shape[0] - step] for t in fine_terms])
    element = jnp.where(slot > 0, state - old, state)

    place = snake(slot)
    line = place * part - HALO + lax.broadcasted_iota(jnp.int32, (1, window, 1), 1)
    inside = ((line >= 0) & (line < rows)).astype(jnp.float32)
    d, c, l = (
        lax.dynamic_slice_in_dim(jnp.pad(x, ((0, 0), (HALO, HALO), (0, 0))), place * part, window, axis=1) for x in raw[:3]
    )
    scale = inside / (1.0 + FINE * (6.0 * d + c + l))
    factors = jnp.stack([scale, FINE * d * scale, FINE * c * scale])

    tall = jnp.pad(element, ((0, 0), (HALO, HALO), (0, 0)))
    widened = jnp.stack([tall[:, p * part : p * part + window] for p in order])
    widened, element, factors, slot, even, place = lax.optimization_barrier((widened, element, factors, slot, even, place))
    terms = lax.all_to_all(widened, "tm", 0, 0, tiled=True)
    terms, element, factors, slot, even, place = lax.optimization_barrier((terms, element, factors, slot, even, place))

    last = slices - 2
    groups = [(g, min(g + SPAN, last)) for g in range(0, last, SPAN)]
    width = {g: end - g + (end == last) for g, end in groups}
    depth = [0] * slices
    for g, end in groups:
        for n in range(g, end + 1):
            depth[n] = width[g] - (n - g)
    deep = SPAN - 1
    inner = [0 if n in width and n else depth[n] for n in range(last + 1)]
    before, after = exchanged(
        jnp.concatenate([terms[n, :k] for n, k in enumerate(inner) if k] + [factors[i, :deep] for i in range(3)]),
        jnp.concatenate([terms[n, planes - k :] for n, k in enumerate(inner) if k] + [factors[i, planes - deep :] for i in range(3)]),
        even,
    )
    offsets = [sum(inner[:n]) for n in range(last + 2)]

    def term(n):
        k, o = inner[n], offsets[n]
        return jnp.concatenate([before[o : o + k], terms[n], after[o : o + k]]) if k else terms[n]

    def factor(i):
        o = offsets[last + 1] + i * deep
        return jnp.concatenate([before[o : o + deep], factors[i], after[o : o + deep]])

    def rows_exchanged(state):
        first_of_pair = place % 2 == 0
        top, bottom = state[:, HALO : 2 * HALO], state[:, part : part + HALO]
        within = swaps([(order[i], order[i + 1]) for i in range(0, slices - 1, 2)])
        between = swaps([(order[i], order[i + 1]) for i in range(1, slices - 1, 2)])
        inner_rows = lax.ppermute(jnp.where(first_of_pair, bottom, top), "tm", within)
        outer_rows = lax.ppermute(jnp.where(first_of_pair, top, bottom), "tm", between)
        above = jnp.where(first_of_pair, outer_rows, inner_rows)
        below = jnp.where(first_of_pair, inner_rows, outer_rows)
        return jnp.concatenate([above, state[:, HALO : HALO + part], below], axis=1)

    coarse_terms = [factor(i) for i in range(3)]
    state = term(0)
    sent = [jnp.zeros((planes + 1, part, lanes), state.dtype)]
    for n in range(last + 1):
        if n:
            k = inner[n]
            trim = deep - k
            o, s, w = (t[trim : t.shape[0] - trim] for t in coarse_terms)
            wide = state[depth[n - 1] - 1 - k : state.shape[0] - (depth[n - 1] - 1 - k)]
            total, upwind = around(wide)
            state = o * wide[1:-1] + s * total + w * upwind + term(n)
            if n in width:
                if n % HALO == 0:
                    state = rows_exchanged(state)
                k = width[n]
                low, high = exchanged(state[:k], state[planes - k :], even)
                state = jnp.concatenate([low, state, high])
        k = depth[n]
        kept = state[:, HALO : HALO + part]
        sent.append(jnp.concatenate([kept[k : k + planes], jnp.where(even, kept[k - 1 : k], kept[k + planes : k + planes + 1])]))

    sent, element, slot, even = lax.optimization_barrier((jnp.stack(sent), element, slot, even))
    back = lax.all_to_all(sent, "tm", 0, 0, tiled=True)
    back, element, slot, even = lax.optimization_barrier((back, element, slot, even))
    arrived = jnp.concatenate([back[i] for i in order], axis=1)
    following, across = arrived[:planes], arrived[planes:]
    beside = lax.ppermute(jnp.where(even, following[planes - 1 :], following[:1]), "space", beside_pairs())
    low, high = jnp.where(even, across, beside), jnp.where(even, beside, across)
    coarse = coarse_linear(jnp.concatenate([low, following, high]), raw[:3])
    end_state = jnp.where(slot > 0, coarse, 0.0) + element
    following = jnp.where(slot == 0, start, following)
    return end_state[None], following[None]


def solution(mesh):
    return jax.shard_map(
        on_device,
        mesh=mesh,
        in_specs=(
            P("tm", "space", None, None),
            P("space", None, None),
            P("space", None, None),
            P("space", None, None),
            P("space", None, None),
        ),
        out_specs=(P("tm", "space", None, None), P("tm", "space", None, None)),
        check_vma=False,
    )
```

time: 269 us -> 258 us (0.959)
  blocking collectives: 0 us -> 82.9 us
  waiting for transfers between devices: 136 us -> 64.4 us
  other arithmetic: 42.1 us -> 28.5 us
  starting transfers between devices: 63.7 us -> 50.9 us
  local copies, waits for them, and re-layouts: 24.1 us -> 27.3 us
    all_to_all x0 -> x2, blocking collectives: none -> 82.9 us  [the longest x1 41.9 us: on_device(): terms = lax.all_to_all(widened, 'tm', 0, 0, tiled=True)]
    all_to_all x2 -> x0, waiting for transfers between devices: 73 us -> none  [the longest x1 41.7 us: on_device(): lax.all_to_all(widened.transpose(1, 0, 2, 3), 'tm', 0, 0, tiled=True)]
    all_to_all x2 -> x0, starting transfers between devices: 13.7 us -> none  [the longest x1 9.27 us: on_device(): lax.all_to_all(widened.transpose(1, 0, 2, 3), 'tm', 0, 0, tiled=True)]
    unnamed x14, other arithmetic: 8.9 us -> 0.11 us
    ppermute x9 -> x11, starting transfers between devices: 44.9 us -> 49.8 us  [the longest x9 47.7 us: exchanged(): across = lax.ppermute(jnp.where(even, low, high), 'space', across_pairs())]
    unnamed x81 -> x111, local copies, waits for them, and re-layouts: 18 us -> 22.5 us
    another operation x3 -> x4, other arithmetic: 4.44 us -> 0.14 us  [the longest x3 0.13 us: on_device(): factors = jnp.stack([scale, FINE * d * scale, FINE * c * scale])]
    ppermute x1, starting transfers between devices: 4.16 us -> 0.09 us  [on_device(): lax.ppermute(jnp.where(even, following[planes - 1:], following[:1]), 'spa...]
  transfers between devices with their start and end apart: 21 -> 21, of which waited for: 11 -> 10; matrix products, arithmetic and copies ran while one was open for 4% -> 1% of each run, Pallas kernels for 0% -> 0%
where the time goes in v5:
time: 258 us; the launch traced here: 256 us
  blocking collectives  82.9 us (32%)
  waiting for transfers between devices  64.4 us (25%)
  starting transfers between devices  50.9 us (20%)
  other arithmetic  28.5 us (11%)
  local copies, waits for them, and re-layouts  27.3 us (11%)
    ppermute x9, waiting for transfers between devices, exchanged(): across = lax.ppermute(jnp.where(even, low, high), 'space', across_pairs())  62.8 us
    ppermute x9, starting transfers between devices, exchanged(): across = lax.ppermute(jnp.where(even, low, high), 'space', across_pairs())  47.7 us
    all_to_all x1, blocking collectives, on_device(): terms = lax.all_to_all(widened, 'tm', 0, 0, tiled=True)  41.9 us
    all_to_all x1, blocking collectives, on_device(): back = lax.all_to_all(sent, 'tm', 0, 0, tiled=True)  41 us
    unnamed x111, local copies, waits for them, and re-layouts  22.5 us
    add x6, other arithmetic, fine_step(): centre + d * (total - 6.0 * centre) - c * (centre - upwind) - l * centre + h  7.41 us
  transfers between devices with their start and end apart: 21, of which 10 were waited for; matrix products, arithmetic and copies ran while one was open for 1% of the time, Pallas kernels for 0%

profile of v5, /device:TPU:25, one launch (start us, length us, event | category | flops | bytes accessed | tf_op | source)
XLA Modules:
  0.0 256.2 jit_solution(17793217391035170158)
XLA Ops:
  2.7 5.0 %collective-permute-start.2 = (f32[2048,128]{1,0:T(8,128)S(1)}, f32[2048,128]{1,0:T(8,128)S(1)}, u32[]{:S(2)}, u32[]{:S(2)}) collective-permute-start(f32[2048,128]{1,0:T(8,128)S(1)} %get-tuple-element.54), channel_id=1, source_target_pairs={{1,2},{2,1},{3,4},{4,3},{5,6},{6,5},{7,8},{8,7},{9,10},{10,9},{11,... | collective-permute-start | bytes 3145736 | tf_op jit(solution)/shard_map/ppermute | solution.py:26
  7.9 4.3 %collective-permute-start = (f32[2,512,128]{2,1,0:T(8,128)S(1)}, f32[2,512,128]{2,1,0:T(8,128)S(1)}, u32[]{:S(2)}, u32[]{:S(2)}) collective-permute-start(f32[2,512,128]{2,1,0:T(8,128)S(1)} %get-tuple-element.128), channel_id=1, source_target_pairs={{1,2},{2,1},{3,4},{4,3},{5,6},{6,5},{7,8},{8,7},{9,10},{10,9},{11,... | collective-permute-start | bytes 1572872 | tf_op jit(solution)/shard_map/ppermute | solution.py:26
  12.3 15.9 %collective-permute-done = f32[2,512,128]{2,1,0:T(8,128)S(1)} collective-permute-done((f32[2,512,128]{2,1,0:T(8,128)S(1)}, f32[2,512,128]{2,1,0:T(8,128)S(1)}, u32[]{:S(2)}, u32[]{:S(2)}) %collective-permute-start) | collective-permute-done | bytes 524320 | tf_op jit(solution)/shard_map/ppermute | solution.py:26
  31.2 2.5 fusion.230
  34.7 4.9 %collective-permute-start.4 = (f32[2,512,128]{2,1,0:T(8,128)S(1)}, f32[2,512,128]{2,1,0:T(8,128)S(1)}, u32[]{:S(2)}, u32[]{:S(2)}) collective-permute-start(f32[2,512,128]{2,1,0:T(8,128)S(1)} %get-tuple-element.106), channel_id=1, source_target_pairs={{1,2},{2,1},{3,4},{4,3},{5,6},{6,5},{7,8},{8,7},{9,10},{10,9},{11,... | collective-permute-start | bytes 1572872 | tf_op jit(solution)/shard_map/ppermute | solution.py:26
  39.7 9.1 %collective-permute-done.4 = f32[2,512,128]{2,1,0:T(8,128)S(1)} collective-permute-done((f32[2,512,128]{2,1,0:T(8,128)S(1)}, f32[2,512,128]{2,1,0:T(8,128)S(1)}, u32[]{:S(2)}, u32[]{:S(2)}) %collective-permute-start.4) | collective-permute-done | bytes 524320 | tf_op jit(solution)/shard_map/ppermute | solution.py:26
  49.1 1.7 fusion.22
  53.7 4.9 %collective-permute-start.6 = (f32[2,512,128]{2,1,0:T(8,128)}, f32[2,512,128]{2,1,0:T(8,128)}, u32[]{:S(2)}, u32[]{:S(2)}) collective-permute-start(f32[2,512,128]{2,1,0:T(8,128)} %get-tuple-element.102), channel_id=1, source_target_pairs={{1,2},{2,1},{3,4},{4,3},{5,6},{6,5},{7,8},{8,7},{9,10},{10,9},{11,... | collective-permute-start | bytes 1572872 | tf_op jit(solution)/shard_map/ppermute | solution.py:26
  58.7 9.4 %collective-permute-done.6 = f32[2,512,128]{2,1,0:T(8,128)} collective-permute-done((f32[2,512,128]{2,1,0:T(8,128)}, f32[2,512,128]{2,1,0:T(8,128)}, u32[]{:S(2)}, u32[]{:S(2)}) %collective-permute-start.6) | collective-permute-done | bytes 524320 | tf_op jit(solution)/shard_map/ppermute | solution.py:26
  71.1 1.7 fusion.32
  73.7 4.9 %collective-permute-start.8 = (f32[2,512,128]{2,1,0:T(8,128)S(1)}, f32[2,512,128]{2,1,0:T(8,128)S(1)}, u32[]{:S(2)}, u32[]{:S(2)}) collective-permute-start(f32[2,512,128]{2,1,0:T(8,128)S(1)} %get-tuple-element.98), channel_id=1, source_target_pairs={{1,2},{2,1},{3,4},{4,3},{5,6},{6,5},{7,8},{8,7},{9,10},{10,9},{11,... | collective-permute-start | bytes 1572872 | tf_op jit(solution)/shard_map/ppermute | solution.py:26
  79.0 8.8 %collective-permute-done.8 = f32[2,512,128]{2,1,0:T(8,128)S(1)} collective-permute-done((f32[2,512,128]{2,1,0:T(8,128)S(1)}, f32[2,512,128]{2,1,0:T(8,128)S(1)}, u32[]{:S(2)}, u32[]{:S(2)}) %collective-permute-start.8) | collective-permute-done | bytes 524320 | tf_op jit(solution)/shard_map/ppermute | solution.py:26
  90.5 2.2 subtract_select_fusion
  93.6 41.9 %all_to_all.10 = f32[16,4,48,128]{3,2,1,0:T(8,128)S(1)} all-to-all(f32[16,4,48,128]{3,2,1,0:T(8,128)S(1)} %constant_dynamic-update-slice_fusion), channel_id=1, replica_groups=mesh['tm'=16,'space'=16] {'tm'}, dimensions={0} | all-to-all | bytes 3145728 | tf_op jit(solution)/shard_map/all_to_all | solution.py:103
  138.0 5.2 %collective-permute-start.10 = (f32[34,48,128]{2,1,0:T(8,128)}, f32[34,48,128]{2,1,0:T(8,128)}, u32[]{:S(2)}, u32[]{:S(2)}) collective-permute-start(f32[34,48,128]{2,1,0:T(8,128)} %get-tuple-element.58), channel_id=1, source_target_pairs={{1,2},{2,1},{3,4},{4,3},{5,6},{6,5},{7,8},{8,7},{9,10},{10,9},{11,... | collective-permute-start | bytes 2506760 | tf_op jit(solution)/shard_map/ppermute | solution.py:26
  145.5 10.3 %collective-permute-done.10 = f32[34,48,128]{2,1,0:T(8,128)} collective-permute-done((f32[34,48,128]{2,1,0:T(8,128)}, f32[34,48,128]{2,1,0:T(8,128)}, u32[]{:S(2)}, u32[]{:S(2)}) %collective-permute-start.10) | collective-permute-done | bytes 835616 | tf_op jit(solution)/shard_map/ppermute | solution.py:26
  159.3 5.2 %collective-permute-start.12 = (f32[4,48,128]{2,1,0:T(8,128)S(1)}, f32[4,48,128]{2,1,0:T(8,128)S(1)}, u32[]{:S(2)}, u32[]{:S(2)}) collective-permute-start(f32[4,48,128]{2,1,0:T(8,128)S(1)} %fusion.206), channel_id=1, source_target_pairs={{1,2},{2,1},{3,4},{4,3},{5,6},{6,5},{7,8},{8,7},{9,10},{10,9},{11,... | collective-permute-start | bytes 294920 | tf_op jit(solution)/shard_map/ppermute | solution.py:26
  164.8 4.0 %collective-permute-done.12 = f32[4,48,128]{2,1,0:T(8,128)S(1)} collective-permute-done((f32[4,48,128]{2,1,0:T(8,128)S(1)}, f32[4,48,128]{2,1,0:T(8,128)S(1)}, u32[]{:S(2)}, u32[]{:S(2)}) %collective-permute-start.12) | collective-permute-done | bytes 98336 | tf_op jit(solution)/shard_map/ppermute | solution.py:26
  174.0 6.6 %collective-permute-start.16 = (f32[4,48,128]{2,1,0:T(8,128)S(1)}, f32[4,48,128]{2,1,0:T(8,128)S(1)}, u32[]{:S(2)}, u32[]{:S(2)}) collective-permute-start(f32[4,48,128]{2,1,0:T(8,128)S(1)} %pad_maximum_fusion.24), channel_id=1, source_target_pairs={{1,2},{2,1},{3,4},{4,3},{5,6},{6,5},{7,8},{8,7},{9,10},{10,9},{11,... | collective-permute-start | bytes 294920 | tf_op jit(solution)/shard_map/ppermute | solution.py:26
  180.7 2.8 %collective-permute-done.16 = f32[4,48,128]{2,1,0:T(8,128)S(1)} collective-permute-done((f32[4,48,128]{2,1,0:T(8,128)S(1)}, f32[4,48,128]{2,1,0:T(8,128)S(1)}, u32[]{:S(2)}, u32[]{:S(2)}) %collective-permute-start.16) | collective-permute-done | bytes 98336 | tf_op jit(solution)/shard_map/ppermute | solution.py:26
  185.3 6.6 %collective-permute-start.18 = (f32[3,48,128]{2,1,0:T(8,128)S(1)}, f32[3,48,128]{2,1,0:T(8,128)S(1)}, u32[]{:S(2)}, u32[]{:S(2)}) collective-permute-start(f32[3,48,128]{2,1,0:T(8,128)S(1)} %get-tuple-element.175), channel_id=1, source_target_pairs={{1,2},{2,1},{3,4},{4,3},{5,6},{6,5},{7,8},{8,7},{9,10},{10,9},{11,... | collective-permute-start | bytes 221192 | tf_op jit(solution)/shard_map/ppermute | solution.py:26
  192.1 2.5 collective-permute-done.18
  195.8 41.0 %all_to_all.11 = f32[16,5,32,128]{3,2,1,0:T(8,128)} all-to-all(f32[16,5,32,128]{3,2,1,0:T(8,128)S(1)} %constant_dynamic-update-slice_fusion.46), channel_id=1, replica_groups=mesh['tm'=16,'space'=16] {'tm'}, dimensions={0} | all-to-all | bytes 2621440 | tf_op jit(solution)/shard_map/all_to_all | solution.py:163
  254.1 2.2 fusion.108
  (255 shorter events, 50.5 us)
Async XLA Ops:
  2.7 25.7 %collective-permute-start.2 = (f32[2048,128]{1,0:T(8,128)S(1)}, f32[2048,128]{1,0:T(8,128)S(1)}, u32[]{:S(2)}, u32[]{:S(2)}) collective-permute-start(f32[2048,128]{1,0:T(8,128)S(1)} %get-tuple-element.54), channel_id=1, source_target_pairs={{1,2},{2,1},{3,4},{4,3},{5,6},{6,5},{7,8},{8,7},{9,10},{10,9},{11,... | collective-permute-start | bytes 3145736 | tf_op jit(solution)/shard_map/ppermute | solution.py:26
  7.7 20.7 %collective-permute-start.3 = (f32[2048,128]{1,0:T(8,128)S(1)}, f32[2048,128]{1,0:T(8,128)S(1)}, u32[]{:S(2)}, u32[]{:S(2)}) collective-permute-start(f32[2048,128]{1,0:T(8,128)S(1)} %get-tuple-element.55), channel_id=1, source_target_pairs={{0,1},{1,0},{2,3},{3,2},{4,5},{5,4},{6,7},{7,6},{8,9},{9,8},{10,11... | collective-permute-start | bytes 3145736 | tf_op jit(solution)/shard_map/ppermute | solution.py:27
  7.9 20.3 %collective-permute-start = (f32[2,512,128]{2,1,0:T(8,128)S(1)}, f32[2,512,128]{2,1,0:T(8,128)S(1)}, u32[]{:S(2)}, u32[]{:S(2)}) collective-permute-start(f32[2,512,128]{2,1,0:T(8,128)S(1)} %get-tuple-element.128), channel_id=1, source_target_pairs={{1,2},{2,1},{3,4},{4,3},{5,6},{6,5},{7,8},{8,7},{9,10},{10,9},{11,... | collective-permute-start | bytes 1572872 | tf_op jit(solution)/shard_map/ppermute | solution.py:26
  12.2 16.0 %collective-permute-start.1 = (f32[2,512,128]{2,1,0:T(8,128)S(1)}, f32[2,512,128]{2,1,0:T(8,128)S(1)}, u32[]{:S(2)}, u32[]{:S(2)}) collective-permute-start(f32[2,512,128]{2,1,0:T(8,128)S(1)} %get-tuple-element.129), channel_id=1, source_target_pairs={{0,1},{1,0},{2,3},{3,2},{4,5},{5,4},{6,7},{7,6},{8,9},{9,8},{10,11... | collective-permute-start | bytes 1572872 | tf_op jit(solution)/shard_map/ppermute | solution.py:27
  28.7 20.4 %copy-start.16 = (f32[1,512,128]{2,1,0:T(8,128)}, f32[1,512,128]{2,1,0:T(8,128)S(1)}, u32[]{:S(2)}) copy-start(f32[1,512,128]{2,1,0:T(8,128)S(1)} %get-tuple-element.111) | copy-start | bytes 786436
  28.7 20.4 %copy-start.18 = (f32[1,512,128]{2,1,0:T(8,128)}, f32[1,512,128]{2,1,0:T(8,128)S(1)}, u32[]{:S(2)}) copy-start(f32[1,512,128]{2,1,0:T(8,128)S(1)} %get-tuple-element.112) | copy-start | bytes 786436
  28.7 40.9 %copy-start.14 = (f32[1,512,128]{2,1,0:T(8,128)}, f32[1,512,128]{2,1,0:T(8,128)S(1)}, u32[]{:S(2)}) copy-start(f32[1,512,128]{2,1,0:T(8,128)S(1)} %get-tuple-element.110) | copy-start | bytes 786436
  34.7 14.1 %collective-permute-start.4 = (f32[2,512,128]{2,1,0:T(8,128)S(1)}, f32[2,512,128]{2,1,0:T(8,128)S(1)}, u32[]{:S(2)}, u32[]{:S(2)}) collective-permute-start(f32[2,512,128]{2,1,0:T(8,128)S(1)} %get-tuple-element.106), channel_id=1, source_target_pairs={{1,2},{2,1},{3,4},{4,3},{5,6},{6,5},{7,8},{8,7},{9,10},{10,9},{11,... | collective-permute-start | bytes 1572872 | tf_op jit(solution)/shard_map/ppermute | solution.py:26
  39.6 9.2 %collective-permute-start.5 = (f32[2,512,128]{2,1,0:T(8,128)S(1)}, f32[2,512,128]{2,1,0:T(8,128)S(1)}, u32[]{:S(2)}, u32[]{:S(2)}) collective-permute-start(f32[2,512,128]{2,1,0:T(8,128)S(1)} %get-tuple-element.107), channel_id=1, source_target_pairs={{0,1},{1,0},{2,3},{3,2},{4,5},{5,4},{6,7},{7,6},{8,9},{9,8},{10,11... | collective-permute-start | bytes 1572872 | tf_op jit(solution)/shard_map/ppermute | solution.py:27
  53.7 14.4 %collective-permute-start.6 = (f32[2,512,128]{2,1,0:T(8,128)}, f32[2,512,128]{2,1,0:T(8,128)}, u32[]{:S(2)}, u32[]{:S(2)}) collective-permute-start(f32[2,512,128]{2,1,0:T(8,128)} %get-tuple-element.102), channel_id=1, source_target_pairs={{1,2},{2,1},{3,4},{4,3},{5,6},{6,5},{7,8},{8,7},{9,10},{10,9},{11,... | collective-permute-start | bytes 1572872 | tf_op jit(solution)/shard_map/ppermute | solution.py:26
  58.5 9.6 %collective-permute-start.7 = (f32[2,512,128]{2,1,0:T(8,128)}, f32[2,512,128]{2,1,0:T(8,128)}, u32[]{:S(2)}, u32[]{:S(2)}) collective-permute-start(f32[2,512,128]{2,1,0:T(8,128)} %get-tuple-element.103), channel_id=1, source_target_pairs={{0,1},{1,0},{2,3},{3,2},{4,5},{5,4},{6,7},{7,6},{8,9},{9,8},{10,11... | collective-permute-start | bytes 1572872 | tf_op jit(solution)/shard_map/ppermute | solution.py:27
  73.7 14.1 %collective-permute-start.8 = (f32[2,512,128]{2,1,0:T(8,128)S(1)}, f32[2,512,128]{2,1,0:T(8,128)S(1)}, u32[]{:S(2)}, u32[]{:S(2)}) collective-permute-start(f32[2,512,128]{2,1,0:T(8,128)S(1)} %get-tuple-element.98), channel_id=1, source_target_pairs={{1,2},{2,1},{3,4},{4,3},{5,6},{6,5},{7,8},{8,7},{9,10},{10,9},{11,... | collective-permute-start | bytes 1572872 | tf_op jit(solution)/shard_map/ppermute | solution.py:26
  78.6 9.2 %collective-permute-start.9 = (f32[2,512,128]{2,1,0:T(8,128)S(1)}, f32[2,512,128]{2,1,0:T(8,128)S(1)}, u32[]{:S(2)}, u32[]{:S(2)}) collective-permute-start(f32[2,512,128]{2,1,0:T(8,128)S(1)} %get-tuple-element.99), channel_id=1, source_target_pairs={{0,1},{1,0},{2,3},{3,2},{4,5},{5,4},{6,7},{7,6},{8,9},{9,8},{10,11... | collective-permute-start | bytes 1572872 | tf_op jit(solution)/shard_map/ppermute | solution.py:27
  138.0 17.8 %collective-permute-start.10 = (f32[34,48,128]{2,1,0:T(8,128)}, f32[34,48,128]{2,1,0:T(8,128)}, u32[]{:S(2)}, u32[]{:S(2)}) collective-permute-start(f32[34,48,128]{2,1,0:T(8,128)} %get-tuple-element.58), channel_id=1, source_target_pairs={{1,2},{2,1},{3,4},{4,3},{5,6},{6,5},{7,8},{8,7},{9,10},{10,9},{11,... | collective-permute-start | bytes 2506760 | tf_op jit(solution)/shard_map/ppermute | solution.py:26
  143.3 12.5 %collective-permute-start.11 = (f32[34,48,128]{2,1,0:T(8,128)}, f32[34,48,128]{2,1,0:T(8,128)}, u32[]{:S(2)}, u32[]{:S(2)}) collective-permute-start(f32[34,48,128]{2,1,0:T(8,128)} %get-tuple-element.59), channel_id=1, source_target_pairs={{0,1},{1,0},{2,3},{3,2},{4,5},{5,4},{6,7},{7,6},{8,9},{9,8},{10,11... | collective-permute-start | bytes 2506760 | tf_op jit(solution)/shard_map/ppermute | solution.py:27
  159.3 9.5 %collective-permute-start.12 = (f32[4,48,128]{2,1,0:T(8,128)S(1)}, f32[4,48,128]{2,1,0:T(8,128)S(1)}, u32[]{:S(2)}, u32[]{:S(2)}) collective-permute-start(f32[4,48,128]{2,1,0:T(8,128)S(1)} %fusion.206), channel_id=1, source_target_pairs={{1,2},{2,1},{3,4},{4,3},{5,6},{6,5},{7,8},{8,7},{9,10},{10,9},{11,... | collective-permute-start | bytes 294920 | tf_op jit(solution)/shard_map/ppermute | solution.py:26
  164.5 4.3 %collective-permute-start.13 = (f32[4,48,128]{2,1,0:T(8,128)S(1)}, f32[4,48,128]{2,1,0:T(8,128)S(1)}, u32[]{:S(2)}, u32[]{:S(2)}) collective-permute-start(f32[4,48,128]{2,1,0:T(8,128)S(1)} %fusion.206), channel_id=1, source_target_pairs={{0,1},{1,0},{2,3},{3,2},{4,5},{5,4},{6,7},{7,6},{8,9},{9,8},{10,11... | collective-permute-start | bytes 294920 | tf_op jit(solution)/shard_map/ppermute | solution.py:27
  170.6 2.2 collective-permute-start.14
  171.3 2.7 %collective-permute-start.15 = (f32[4,8,128]{2,1,0:T(8,128)S(1)}, f32[4,8,128]{2,1,0:T(8,128)S(1)}, u32[]{:S(2)}, u32[]{:S(2)}) collective-permute-start(f32[4,8,128]{2,1,0:T(8,128)S(1)} %get-tuple-element.178), channel_id=1, source_target_pairs={{0,16},{16,0},{48,32},{32,48},{64,80},{80,64},{112,96},{96,112},{1... | collective-permute-start | bytes 49160 | tf_op jit(solution)/shard_map/ppermute | solution.py:135
  174.0 9.5 %collective-permute-start.16 = (f32[4,48,128]{2,1,0:T(8,128)S(1)}, f32[4,48,128]{2,1,0:T(8,128)S(1)}, u32[]{:S(2)}, u32[]{:S(2)}) collective-permute-start(f32[4,48,128]{2,1,0:T(8,128)S(1)} %pad_maximum_fusion.24), channel_id=1, source_target_pairs={{1,2},{2,1},{3,4},{4,3},{5,6},{6,5},{7,8},{8,7},{9,10},{10,9},{11,... | collective-permute-start | bytes 294920 | tf_op jit(solution)/shard_map/ppermute | solution.py:26
  180.6 2.9 %collective-permute-start.17 = (f32[4,48,128]{2,1,0:T(8,128)S(1)}, f32[4,48,128]{2,1,0:T(8,128)S(1)}, u32[]{:S(2)}, u32[]{:S(2)}) collective-permute-start(f32[4,48,128]{2,1,0:T(8,128)S(1)} %pad_maximum_fusion.24), channel_id=1, source_target_pairs={{0,1},{1,0},{2,3},{3,2},{4,5},{5,4},{6,7},{7,6},{8,9},{9,8},{10,11... | collective-permute-start | bytes 294920 | tf_op jit(solution)/shard_map/ppermute | solution.py:27
  185.3 9.3 %collective-permute-start.18 = (f32[3,48,128]{2,1,0:T(8,128)S(1)}, f32[3,48,128]{2,1,0:T(8,128)S(1)}, u32[]{:S(2)}, u32[]{:S(2)}) collective-permute-start(f32[3,48,128]{2,1,0:T(8,128)S(1)} %get-tuple-element.175), channel_id=1, source_target_pairs={{1,2},{2,1},{3,4},{4,3},{5,6},{6,5},{7,8},{8,7},{9,10},{10,9},{11,... | collective-permute-start | bytes 221192 | tf_op jit(solution)/shard_map/ppermute | solution.py:26
  192.0 2.6 %collective-permute-start.19 = (f32[3,48,128]{2,1,0:T(8,128)S(1)}, f32[3,48,128]{2,1,0:T(8,128)S(1)}, u32[]{:S(2)}, u32[]{:S(2)}) collective-permute-start(f32[3,48,128]{2,1,0:T(8,128)S(1)} %get-tuple-element.176), channel_id=1, source_target_pairs={{0,1},{1,0},{2,3},{3,2},{4,5},{5,4},{6,7},{7,6},{8,9},{9,8},{10,11... | collective-permute-start | bytes 221192 | tf_op jit(solution)/shard_map/ppermute | solution.py:27
  251.2 1.6 collective-permute-start.20
  (30 other events, 175.6 us)

commit v6 on v5

--- a/solution.py
+++ b/solution.py
@@ -81,6 +81,7 @@
         low, high = exchanged(low, high, even)
         if turn == OLD_TURN:
             old = coarse_linear(first, raw[:3])
+            low, high, old = lax.optimization_barrier((low, high, old))
         state = jnp.concatenate([low, state, high])
         if turn == 0:
             first = state[ROUNDS - 1 : ROUNDS + planes + 1]
@@ -159,10 +160,13 @@
         kept = state[:, HALO : HALO + part]
         sent.append(jnp.concatenate([kept[k : k + planes], jnp.where(even, kept[k - 1 : k], kept[k + planes : k + planes + 1])]))
 
-    sent, element, slot, even = lax.optimization_barrier((jnp.stack(sent), element, slot, even))
+    turned = lax.broadcasted_iota(jnp.int32, (slices // 2, 1, 1, 1, 1), 0) % 2
+    sent, element, slot, even, turned = lax.optimization_barrier((jnp.stack(sent), element, slot, even, turned))
     back = lax.all_to_all(sent, "tm", 0, 0, tiled=True)
-    back, element, slot, even = lax.optimization_barrier((back, element, slot, even))
-    arrived = jnp.concatenate([back[i] for i in order], axis=1)
+    back, element, slot, even, turned = lax.optimization_barrier((back, element, slot, even, turned))
+    pairs = back.reshape((slices // 2, 2) + back.shape[1:])
+    back = jnp.where(turned == 1, pairs[:, ::-1], pairs).reshape(back.shape)
+    arrived = back.transpose(1, 0, 2, 3).reshape(planes + 1, rows, lanes)
     following, across = arrived[:planes], arrived[planes:]
     beside = lax.ppermute(jnp.where(even, following[planes - 1 :], following[:1]), "space", beside_pairs())
     low, high = jnp.where(even, across, beside), jnp.where(even, beside, across)

time: 258 us -> 244 us (0.946)
  local copies, waits for them, and re-layouts: 27.3 us -> 14.1 us
    unnamed x111 -> x96, local copies, waits for them, and re-layouts: 22.5 us -> 9.94 us
    select_n x1 -> x4, other arithmetic: 0.03 us -> 3.21 us  [the longest x1 2.03 us: on_device(): back = jnp.where(turned == 1, pairs[:, ::-1], pairs).reshape(back.shape)]
  transfers between devices with their start and end apart: 21 -> 21, of which waited for: 10 -> 9; matrix products, arithmetic and copies ran while one was open for 1% -> 2% of each run, Pallas kernels for 0% -> 0%
where the time goes in v6:
time: 244 us; the launch traced here: 243 us
  blocking collectives  82.9 us (34%)
  waiting for transfers between devices  62.1 us (25%)
  starting transfers between devices  50.9 us (21%)
  other arithmetic  30.4 us (12%)
  local copies, waits for them, and re-layouts  14.1 us (6%)
    ppermute x9, waiting for transfers between devices, exchanged(): across = lax.ppermute(jnp.where(even, low, high), 'space', across_pairs())  60.9 us
    ppermute x9, starting transfers between devices, exchanged(): across = lax.ppermute(jnp.where(even, low, high), 'space', across_pairs())  47.7 us
    all_to_all x1, blocking collectives, on_device(): terms = lax.all_to_all(widened, 'tm', 0, 0, tiled=True)  41.9 us
    all_to_all x1, blocking collectives, on_device(): back = lax.all_to_all(sent, 'tm', 0, 0, tiled=True)  41 us
    unnamed x96, local copies, waits for them, and re-layouts  9.94 us
    add x6, other arithmetic, fine_step(): centre + d * (total - 6.0 * centre) - c * (centre - upwind) - l * centre + h  7.52 us
    add x13, other arithmetic, on_device(): state = o * wide[1:-1] + s * total + w * upwind + term(n)  5.01 us
  transfers between devices with their start and end apart: 21, of which 9 were waited for; matrix products, arithmetic and copies ran while one was open for 2% of the time, Pallas kernels for 0%

profile of v6, /device:TPU:25, one launch (start us, length us, event | category | flops | bytes accessed | tf_op | source)
XLA Modules:
  0.0 242.8 jit_solution(13095974486089662660)
XLA Ops:
  2.7 5.0 %collective-permute-start.2 = (f32[2048,128]{1,0:T(8,128)S(1)}, f32[2048,128]{1,0:T(8,128)S(1)}, u32[]{:S(2)}, u32[]{:S(2)}) collective-permute-start(f32[2048,128]{1,0:T(8,128)S(1)} %get-tuple-element.64), channel_id=1, source_target_pairs={{1,2},{2,1},{3,4},{4,3},{5,6},{6,5},{7,8},{8,7},{9,10},{10,9},{11,... | collective-permute-start | bytes 3145736 | tf_op jit(solution)/shard_map/ppermute | solution.py:26
  7.9 4.3 %collective-permute-start = (f32[2,512,128]{2,1,0:T(8,128)S(1)}, f32[2,512,128]{2,1,0:T(8,128)S(1)}, u32[]{:S(2)}, u32[]{:S(2)}) collective-permute-start(f32[2,512,128]{2,1,0:T(8,128)S(1)} %get-tuple-element.136), channel_id=1, source_target_pairs={{1,2},{2,1},{3,4},{4,3},{5,6},{6,5},{7,8},{8,7},{9,10},{10,9},{11,... | collective-permute-start | bytes 1572872 | tf_op jit(solution)/shard_map/ppermute | solution.py:26
  12.3 15.9 %collective-permute-done = f32[2,512,128]{2,1,0:T(8,128)S(1)} collective-permute-done((f32[2,512,128]{2,1,0:T(8,128)S(1)}, f32[2,512,128]{2,1,0:T(8,128)S(1)}, u32[]{:S(2)}, u32[]{:S(2)}) %collective-permute-start) | collective-permute-done | bytes 524320 | tf_op jit(solution)/shard_map/ppermute | solution.py:26
  33.8 4.9 %collective-permute-start.4 = (f32[2,512,128]{2,1,0:T(8,128)S(1)}, f32[2,512,128]{2,1,0:T(8,128)S(1)}, u32[]{:S(2)}, u32[]{:S(2)}) collective-permute-start(f32[2,512,128]{2,1,0:T(8,128)S(1)} %get-tuple-element.115), channel_id=1, source_target_pairs={{1,2},{2,1},{3,4},{4,3},{5,6},{6,5},{7,8},{8,7},{9,10},{10,9},{11,... | collective-permute-start | bytes 1572872 | tf_op jit(solution)/shard_map/ppermute | solution.py:26
  38.8 1.8 fusion.69
  40.6 7.3 %collective-permute-done.4 = f32[2,512,128]{2,1,0:T(8,128)S(1)} collective-permute-done((f32[2,512,128]{2,1,0:T(8,128)S(1)}, f32[2,512,128]{2,1,0:T(8,128)S(1)}, u32[]{:S(2)}, u32[]{:S(2)}) %collective-permute-start.4) | collective-permute-done | bytes 524320 | tf_op jit(solution)/shard_map/ppermute | solution.py:26
  48.3 1.7 fusion.22
  52.8 4.9 %collective-permute-start.6 = (f32[2,512,128]{2,1,0:T(8,128)}, f32[2,512,128]{2,1,0:T(8,128)}, u32[]{:S(2)}, u32[]{:S(2)}) collective-permute-start(f32[2,512,128]{2,1,0:T(8,128)} %get-tuple-element.110), channel_id=1, source_target_pairs={{1,2},{2,1},{3,4},{4,3},{5,6},{6,5},{7,8},{8,7},{9,10},{10,9},{11,... | collective-permute-start | bytes 1572872 | tf_op jit(solution)/shard_map/ppermute | solution.py:26
  57.8 9.4 %collective-permute-done.6 = f32[2,512,128]{2,1,0:T(8,128)} collective-permute-done((f32[2,512,128]{2,1,0:T(8,128)}, f32[2,512,128]{2,1,0:T(8,128)}, u32[]{:S(2)}, u32[]{:S(2)}) %collective-permute-start.6) | collective-permute-done | bytes 524320 | tf_op jit(solution)/shard_map/ppermute | solution.py:26
  70.2 1.7 fusion.32
  72.9 4.9 %collective-permute-start.8 = (f32[2,512,128]{2,1,0:T(8,128)S(1)}, f32[2,512,128]{2,1,0:T(8,128)S(1)}, u32[]{:S(2)}, u32[]{:S(2)}) collective-permute-start(f32[2,512,128]{2,1,0:T(8,128)S(1)} %get-tuple-element.106), channel_id=1, source_target_pairs={{1,2},{2,1},{3,4},{4,3},{5,6},{6,5},{7,8},{8,7},{9,10},{10,9},{11,... | collective-permute-start | bytes 1572872 | tf_op jit(solution)/shard_map/ppermute | solution.py:26
  78.2 8.8 %collective-permute-done.8 = f32[2,512,128]{2,1,0:T(8,128)S(1)} collective-permute-done((f32[2,512,128]{2,1,0:T(8,128)S(1)}, f32[2,512,128]{2,1,0:T(8,128)S(1)}, u32[]{:S(2)}, u32[]{:S(2)}) %collective-permute-start.8) | collective-permute-done | bytes 524320 | tf_op jit(solution)/shard_map/ppermute | solution.py:26
  91.7 41.9 %all_to_all.10 = f32[16,4,48,128]{3,2,1,0:T(8,128)S(1)} all-to-all(f32[16,4,48,128]{3,2,1,0:T(8,128)S(1)} %constant_dynamic-update-slice_fusion), channel_id=1, replica_groups=mesh['tm'=16,'space'=16] {'tm'}, dimensions={0} | all-to-all | bytes 3145728 | tf_op jit(solution)/shard_map/all_to_all | solution.py:104
  136.1 5.2 %collective-permute-start.10 = (f32[34,48,128]{2,1,0:T(8,128)}, f32[34,48,128]{2,1,0:T(8,128)}, u32[]{:S(2)}, u32[]{:S(2)}) collective-permute-start(f32[34,48,128]{2,1,0:T(8,128)} %get-tuple-element.68), channel_id=1, source_target_pairs={{1,2},{2,1},{3,4},{4,3},{5,6},{6,5},{7,8},{8,7},{9,10},{10,9},{11,... | collective-permute-start | bytes 2506760 | tf_op jit(solution)/shard_map/ppermute | solution.py:26
  143.5 10.3 %collective-permute-done.10 = f32[34,48,128]{2,1,0:T(8,128)} collective-permute-done((f32[34,48,128]{2,1,0:T(8,128)}, f32[34,48,128]{2,1,0:T(8,128)}, u32[]{:S(2)}, u32[]{:S(2)}) %collective-permute-start.10) | collective-permute-done | bytes 835616 | tf_op jit(solution)/shard_map/ppermute | solution.py:26
  157.3 5.2 %collective-permute-start.12 = (f32[4,48,128]{2,1,0:T(8,128)S(1)}, f32[4,48,128]{2,1,0:T(8,128)S(1)}, u32[]{:S(2)}, u32[]{:S(2)}) collective-permute-start(f32[4,48,128]{2,1,0:T(8,128)S(1)} %fusion.206), channel_id=1, source_target_pairs={{1,2},{2,1},{3,4},{4,3},{5,6},{6,5},{7,8},{8,7},{9,10},{10,9},{11,... | collective-permute-start | bytes 294920 | tf_op jit(solution)/shard_map/ppermute | solution.py:26
  162.9 4.0 %collective-permute-done.12 = f32[4,48,128]{2,1,0:T(8,128)S(1)} collective-permute-done((f32[4,48,128]{2,1,0:T(8,128)S(1)}, f32[4,48,128]{2,1,0:T(8,128)S(1)}, u32[]{:S(2)}, u32[]{:S(2)}) %collective-permute-start.12) | collective-permute-done | bytes 98336 | tf_op jit(solution)/shard_map/ppermute | solution.py:26
  172.0 6.6 %collective-permute-start.16 = (f32[4,48,128]{2,1,0:T(8,128)S(1)}, f32[4,48,128]{2,1,0:T(8,128)S(1)}, u32[]{:S(2)}, u32[]{:S(2)}) collective-permute-start(f32[4,48,128]{2,1,0:T(8,128)S(1)} %pad_maximum_fusion.24), channel_id=1, source_target_pairs={{1,2},{2,1},{3,4},{4,3},{5,6},{6,5},{7,8},{8,7},{9,10},{10,9},{11,... | collective-permute-start | bytes 294920 | tf_op jit(solution)/shard_map/ppermute | solution.py:26
  178.8 2.8 %collective-permute-done.16 = f32[4,48,128]{2,1,0:T(8,128)S(1)} collective-permute-done((f32[4,48,128]{2,1,0:T(8,128)S(1)}, f32[4,48,128]{2,1,0:T(8,128)S(1)}, u32[]{:S(2)}, u32[]{:S(2)}) %collective-permute-start.16) | collective-permute-done | bytes 98336 | tf_op jit(solution)/shard_map/ppermute | solution.py:26
  183.4 6.6 %collective-permute-start.18 = (f32[3,48,128]{2,1,0:T(8,128)S(1)}, f32[3,48,128]{2,1,0:T(8,128)S(1)}, u32[]{:S(2)}, u32[]{:S(2)}) collective-permute-start(f32[3,48,128]{2,1,0:T(8,128)S(1)} %get-tuple-element.185), channel_id=1, source_target_pairs={{1,2},{2,1},{3,4},{4,3},{5,6},{6,5},{7,8},{8,7},{9,10},{10,9},{11,... | collective-permute-start | bytes 221192 | tf_op jit(solution)/shard_map/ppermute | solution.py:26
  190.2 2.5 %collective-permute-done.18 = f32[3,48,128]{2,1,0:T(8,128)S(1)} collective-permute-done((f32[3,48,128]{2,1,0:T(8,128)S(1)}, f32[3,48,128]{2,1,0:T(8,128)S(1)}, u32[]{:S(2)}, u32[]{:S(2)}) %collective-permute-start.18) | collective-permute-done | bytes 73760 | tf_op jit(solution)/shard_map/ppermute | solution.py:26
  193.8 41.0 %all_to_all.11 = f32[16,5,32,128]{3,2,1,0:T(8,128)} all-to-all(f32[16,5,32,128]{3,2,1,0:T(8,128)S(1)} %constant_dynamic-update-slice_fusion.46), channel_id=1, replica_groups=mesh['tm'=16,'space'=16] {'tm'}, dimensions={0} | all-to-all | bytes 2621440 | tf_op jit(solution)/shard_map/all_to_all | solution.py:165
  234.8 2.0 reverse_select_fusion
  240.6 2.2 fusion.108
  (245 shorter events, 39.6 us)
Async XLA Ops:
  2.7 25.7 %collective-permute-start.2 = (f32[2048,128]{1,0:T(8,128)S(1)}, f32[2048,128]{1,0:T(8,128)S(1)}, u32[]{:S(2)}, u32[]{:S(2)}) collective-permute-start(f32[2048,128]{1,0:T(8,128)S(1)} %get-tuple-element.64), channel_id=1, source_target_pairs={{1,2},{2,1},{3,4},{4,3},{5,6},{6,5},{7,8},{8,7},{9,10},{10,9},{11,... | collective-permute-start | bytes 3145736 | tf_op jit(solution)/shard_map/ppermute | solution.py:26
  7.7 20.7 %collective-permute-start.3 = (f32[2048,128]{1,0:T(8,128)S(1)}, f32[2048,128]{1,0:T(8,128)S(1)}, u32[]{:S(2)}, u32[]{:S(2)}) collective-permute-start(f32[2048,128]{1,0:T(8,128)S(1)} %get-tuple-element.65), channel_id=1, source_target_pairs={{0,1},{1,0},{2,3},{3,2},{4,5},{5,4},{6,7},{7,6},{8,9},{9,8},{10,11... | collective-permute-start | bytes 3145736 | tf_op jit(solution)/shard_map/ppermute | solution.py:27
  7.9 20.3 %collective-permute-start = (f32[2,512,128]{2,1,0:T(8,128)S(1)}, f32[2,512,128]{2,1,0:T(8,128)S(1)}, u32[]{:S(2)}, u32[]{:S(2)}) collective-permute-start(f32[2,512,128]{2,1,0:T(8,128)S(1)} %get-tuple-element.136), channel_id=1, source_target_pairs={{1,2},{2,1},{3,4},{4,3},{5,6},{6,5},{7,8},{8,7},{9,10},{10,9},{11,... | collective-permute-start | bytes 1572872 | tf_op jit(solution)/shard_map/ppermute | solution.py:26
  12.2 16.0 %collective-permute-start.1 = (f32[2,512,128]{2,1,0:T(8,128)S(1)}, f32[2,512,128]{2,1,0:T(8,128)S(1)}, u32[]{:S(2)}, u32[]{:S(2)}) collective-permute-start(f32[2,512,128]{2,1,0:T(8,128)S(1)} %get-tuple-element.137), channel_id=1, source_target_pairs={{0,1},{1,0},{2,3},{3,2},{4,5},{5,4},{6,7},{7,6},{8,9},{9,8},{10,11... | collective-permute-start | bytes 1572872 | tf_op jit(solution)/shard_map/ppermute | solution.py:27
  28.7 19.5 %copy-start.15 = (f32[1,512,128]{2,1,0:T(8,128)}, f32[1,512,128]{2,1,0:T(8,128)S(1)}, u32[]{:S(2)}) copy-start(f32[1,512,128]{2,1,0:T(8,128)S(1)} %get-tuple-element.119) | copy-start | bytes 786436
  28.7 19.5 %copy-start.17 = (f32[1,512,128]{2,1,0:T(8,128)}, f32[1,512,128]{2,1,0:T(8,128)S(1)}, u32[]{:S(2)}) copy-start(f32[1,512,128]{2,1,0:T(8,128)S(1)} %get-tuple-element.120) | copy-start | bytes 786436
  28.7 40.0 %copy-start.13 = (f32[1,512,128]{2,1,0:T(8,128)}, f32[1,512,128]{2,1,0:T(8,128)S(1)}, u32[]{:S(2)}) copy-start(f32[1,512,128]{2,1,0:T(8,128)S(1)} %get-tuple-element.118) | copy-start | bytes 786436
  33.8 14.1 %collective-permute-start.4 = (f32[2,512,128]{2,1,0:T(8,128)S(1)}, f32[2,512,128]{2,1,0:T(8,128)S(1)}, u32[]{:S(2)}, u32[]{:S(2)}) collective-permute-start(f32[2,512,128]{2,1,0:T(8,128)S(1)} %get-tuple-element.115), channel_id=1, source_target_pairs={{1,2},{2,1},{3,4},{4,3},{5,6},{6,5},{7,8},{8,7},{9,10},{10,9},{11,... | collective-permute-start | bytes 1572872 | tf_op jit(solution)/shard_map/ppermute | solution.py:26
  38.7 9.2 %collective-permute-start.5 = (f32[2,512,128]{2,1,0:T(8,128)S(1)}, f32[2,512,128]{2,1,0:T(8,128)S(1)}, u32[]{:S(2)}, u32[]{:S(2)}) collective-permute-start(f32[2,512,128]{2,1,0:T(8,128)S(1)} %get-tuple-element.114), channel_id=1, source_target_pairs={{0,1},{1,0},{2,3},{3,2},{4,5},{5,4},{6,7},{7,6},{8,9},{9,8},{10,11... | collective-permute-start | bytes 1572872 | tf_op jit(solution)/shard_map/ppermute | solution.py:27
  52.8 14.4 %collective-permute-start.6 = (f32[2,512,128]{2,1,0:T(8,128)}, f32[2,512,128]{2,1,0:T(8,128)}, u32[]{:S(2)}, u32[]{:S(2)}) collective-permute-start(f32[2,512,128]{2,1,0:T(8,128)} %get-tuple-element.110), channel_id=1, source_target_pairs={{1,2},{2,1},{3,4},{4,3},{5,6},{6,5},{7,8},{8,7},{9,10},{10,9},{11,... | collective-permute-start | bytes 1572872 | tf_op jit(solution)/shard_map/ppermute | solution.py:26
  57.7 9.6 %collective-permute-start.7 = (f32[2,512,128]{2,1,0:T(8,128)}, f32[2,512,128]{2,1,0:T(8,128)}, u32[]{:S(2)}, u32[]{:S(2)}) collective-permute-start(f32[2,512,128]{2,1,0:T(8,128)} %get-tuple-element.111), channel_id=1, source_target_pairs={{0,1},{1,0},{2,3},{3,2},{4,5},{5,4},{6,7},{7,6},{8,9},{9,8},{10,11... | collective-permute-start | bytes 1572872 | tf_op jit(solution)/shard_map/ppermute | solution.py:27
  72.9 14.1 %collective-permute-start.8 = (f32[2,512,128]{2,1,0:T(8,128)S(1)}, f32[2,512,128]{2,1,0:T(8,128)S(1)}, u32[]{:S(2)}, u32[]{:S(2)}) collective-permute-start(f32[2,512,128]{2,1,0:T(8,128)S(1)} %get-tuple-element.106), channel_id=1, source_target_pairs={{1,2},{2,1},{3,4},{4,3},{5,6},{6,5},{7,8},{8,7},{9,10},{10,9},{11,... | collective-permute-start | bytes 1572872 | tf_op jit(solution)/shard_map/ppermute | solution.py:26
  77.8 9.2 %collective-permute-start.9 = (f32[2,512,128]{2,1,0:T(8,128)S(1)}, f32[2,512,128]{2,1,0:T(8,128)S(1)}, u32[]{:S(2)}, u32[]{:S(2)}) collective-permute-start(f32[2,512,128]{2,1,0:T(8,128)S(1)} %get-tuple-element.107), channel_id=1, source_target_pairs={{0,1},{1,0},{2,3},{3,2},{4,5},{5,4},{6,7},{7,6},{8,9},{9,8},{10,11... | collective-permute-start | bytes 1572872 | tf_op jit(solution)/shard_map/ppermute | solution.py:27
  136.1 17.8 %collective-permute-start.10 = (f32[34,48,128]{2,1,0:T(8,128)}, f32[34,48,128]{2,1,0:T(8,128)}, u32[]{:S(2)}, u32[]{:S(2)}) collective-permute-start(f32[34,48,128]{2,1,0:T(8,128)} %get-tuple-element.68), channel_id=1, source_target_pairs={{1,2},{2,1},{3,4},{4,3},{5,6},{6,5},{7,8},{8,7},{9,10},{10,9},{11,... | collective-permute-start | bytes 2506760 | tf_op jit(solution)/shard_map/ppermute | solution.py:26
  141.3 12.5 %collective-permute-start.11 = (f32[34,48,128]{2,1,0:T(8,128)}, f32[34,48,128]{2,1,0:T(8,128)}, u32[]{:S(2)}, u32[]{:S(2)}) collective-permute-start(f32[34,48,128]{2,1,0:T(8,128)} %get-tuple-element.69), channel_id=1, source_target_pairs={{0,1},{1,0},{2,3},{3,2},{4,5},{5,4},{6,7},{7,6},{8,9},{9,8},{10,11... | collective-permute-start | bytes 2506760 | tf_op jit(solution)/shard_map/ppermute | solution.py:27
  157.3 9.5 %collective-permute-start.12 = (f32[4,48,128]{2,1,0:T(8,128)S(1)}, f32[4,48,128]{2,1,0:T(8,128)S(1)}, u32[]{:S(2)}, u32[]{:S(2)}) collective-permute-start(f32[4,48,128]{2,1,0:T(8,128)S(1)} %fusion.206), channel_id=1, source_target_pairs={{1,2},{2,1},{3,4},{4,3},{5,6},{6,5},{7,8},{8,7},{9,10},{10,9},{11,... | collective-permute-start | bytes 294920 | tf_op jit(solution)/shard_map/ppermute | solution.py:26
  162.6 4.3 %collective-permute-start.13 = (f32[4,48,128]{2,1,0:T(8,128)S(1)}, f32[4,48,128]{2,1,0:T(8,128)S(1)}, u32[]{:S(2)}, u32[]{:S(2)}) collective-permute-start(f32[4,48,128]{2,1,0:T(8,128)S(1)} %fusion.206), channel_id=1, source_target_pairs={{0,1},{1,0},{2,3},{3,2},{4,5},{5,4},{6,7},{7,6},{8,9},{9,8},{10,11... | collective-permute-start | bytes 294920 | tf_op jit(solution)/shard_map/ppermute | solution.py:27
  168.7 2.2 collective-permute-start.14
  169.3 2.7 %collective-permute-start.15 = (f32[4,8,128]{2,1,0:T(8,128)S(1)}, f32[4,8,128]{2,1,0:T(8,128)S(1)}, u32[]{:S(2)}, u32[]{:S(2)}) collective-permute-start(f32[4,8,128]{2,1,0:T(8,128)S(1)} %get-tuple-element.188), channel_id=1, source_target_pairs={{0,16},{16,0},{48,32},{32,48},{64,80},{80,64},{112,96},{96,112},{1... | collective-permute-start | bytes 49160 | tf_op jit(solution)/shard_map/ppermute | solution.py:136
  172.0 9.5 %collective-permute-start.16 = (f32[4,48,128]{2,1,0:T(8,128)S(1)}, f32[4,48,128]{2,1,0:T(8,128)S(1)}, u32[]{:S(2)}, u32[]{:S(2)}) collective-permute-start(f32[4,48,128]{2,1,0:T(8,128)S(1)} %pad_maximum_fusion.24), channel_id=1, source_target_pairs={{1,2},{2,1},{3,4},{4,3},{5,6},{6,5},{7,8},{8,7},{9,10},{10,9},{11,... | collective-permute-start | bytes 294920 | tf_op jit(solution)/shard_map/ppermute | solution.py:26
  178.7 2.9 %collective-permute-start.17 = (f32[4,48,128]{2,1,0:T(8,128)S(1)}, f32[4,48,128]{2,1,0:T(8,128)S(1)}, u32[]{:S(2)}, u32[]{:S(2)}) collective-permute-start(f32[4,48,128]{2,1,0:T(8,128)S(1)} %pad_maximum_fusion.24), channel_id=1, source_target_pairs={{0,1},{1,0},{2,3},{3,2},{4,5},{5,4},{6,7},{7,6},{8,9},{9,8},{10,11... | collective-permute-start | bytes 294920 | tf_op jit(solution)/shard_map/ppermute | solution.py:27
  183.4 9.3 %collective-permute-start.18 = (f32[3,48,128]{2,1,0:T(8,128)S(1)}, f32[3,48,128]{2,1,0:T(8,128)S(1)}, u32[]{:S(2)}, u32[]{:S(2)}) collective-permute-start(f32[3,48,128]{2,1,0:T(8,128)S(1)} %get-tuple-element.185), channel_id=1, source_target_pairs={{1,2},{2,1},{3,4},{4,3},{5,6},{6,5},{7,8},{8,7},{9,10},{10,9},{11,... | collective-permute-start | bytes 221192 | tf_op jit(solution)/shard_map/ppermute | solution.py:26
  190.0 2.6 %collective-permute-start.19 = (f32[3,48,128]{2,1,0:T(8,128)S(1)}, f32[3,48,128]{2,1,0:T(8,128)S(1)}, u32[]{:S(2)}, u32[]{:S(2)}) collective-permute-start(f32[3,48,128]{2,1,0:T(8,128)S(1)} %get-tuple-element.186), channel_id=1, source_target_pairs={{0,1},{1,0},{2,3},{3,2},{4,5},{5,4},{6,7},{7,6},{8,9},{9,8},{10,11... | collective-permute-start | bytes 221192 | tf_op jit(solution)/shard_map/ppermute | solution.py:27
  237.2 2.2 collective-permute-start.20
  (30 other events, 159.8 us)

commit v7 on v6

--- a/solution.py
+++ b/solution.py
@@ -1,6 +1,8 @@
 import jax
 import jax.numpy as jnp
 from jax import lax
+from jax.experimental import pallas as pl
+from jax.experimental.pallas import tpu as pltpu
 from jax.sharding import PartitionSpec as P
 
 FINE = 8
@@ -47,6 +49,48 @@
     d, c, l = terms
     total, upwind = around(wide)
     return (wide[1:-1] + FINE * (d * total + c * upwind)) / (1.0 + FINE * (6.0 * d + c + l))
+
+
+def edges_packed(terms, factors, plan):
+    planes, rows, lanes = terms.shape[1:]
+    pieces = [(g, o, k, f, i) for g, group in enumerate(plan) for o, (f, i, k) in zip(offsets_of(group), group)]
+
+    def kernel(terms_ref, factors_ref, *refs):
+        outs, sems = refs[:-1], refs[-1]
+        odd = lax.axis_index("space") % 2
+        copies = []
+        for j, (g, o, k, f, i) in enumerate(pieces):
+            source = (factors_ref if f else terms_ref).at[i]
+            for side in range(2):
+                at = (odd if side == 0 else 1 - odd) * (planes - k)
+                copies.append(
+                    pltpu.make_async_copy(source.at[pl.ds(at, k)], outs[2 * g + side].at[pl.ds(o, k)], sems.at[2 * j + side])
+                )
+        for copy in copies:
+            copy.start()
+        for copy in copies:
+            copy.wait()
+
+    sizes = [sum(k for _, _, k in group) for group in plan]
+    shapes = [jax.ShapeDtypeStruct((n, rows, lanes), terms.dtype) for n in sizes for _ in range(2)]
+    anywhere = pl.BlockSpec(memory_space=pl.ANY)
+    outs = pl.pallas_call(
+        kernel,
+        name="edges_packed",
+        out_shape=shapes,
+        in_specs=[anywhere, anywhere],
+        out_specs=[anywhere] * len(shapes),
+        scratch_shapes=[pltpu.SemaphoreType.DMA((2 * len(pieces),))],
+        compiler_params=pltpu.CompilerParams(vmem_limit_bytes=1 << 20),
+    )(terms, factors)
+    return [(outs[2 * g], outs[2 * g + 1]) for g in range(len(plan))]
+
+
+def offsets_of(group):
+    out = [0]
+    for _, _, k in group:
+        out.append(out[-1] + k)
+    return out
 
 
 def snake(index):
@@ -100,9 +144,11 @@
 
     tall = jnp.pad(element, ((0, 0), (HALO, HALO), (0, 0)))
     widened = jnp.stack([tall[:, p * part : p * part + window] for p in order])
-    widened, element, factors, slot, even, place = lax.optimization_barrier((widened, element, factors, slot, even, place))
+    turned = lax.broadcasted_iota(jnp.int32, (slices // 2, 1, 1, 1, 1), 0) % 2
+    kept = (element, factors, slot, even, place, turned)
+    widened, *kept = lax.optimization_barrier((widened, *kept))
     terms = lax.all_to_all(widened, "tm", 0, 0, tiled=True)
-    terms, element, factors, slot, even, place = lax.optimization_barrier((terms, element, factors, slot, even, place))
+    terms, element, factors, slot, even, place, turned = lax.optimization_barrier((terms, *kept))
 
     last = slices - 2
     groups = [(g, min(g + SPAN, last)) for g in range(0, last, SPAN)]
@@ -113,20 +159,26 @@
             depth[n] = width[g] - (n - g)
     deep = SPAN - 1
     inner = [0 if n in width and n else depth[n] for n in range(last + 1)]
-    before, after = exchanged(
-        jnp.concatenate([terms[n, :k] for n, k in enumerate(inner) if k] + [factors[i, :deep] for i in range(3)]),
-        jnp.concatenate([terms[n, planes - k :] for n, k in enumerate(inner) if k] + [factors[i, planes - deep :] for i in range(3)]),
-        even,
-    )
-    offsets = [sum(inner[:n]) for n in range(last + 2)]
-
-    def term(n):
-        k, o = inner[n], offsets[n]
-        return jnp.concatenate([before[o : o + k], terms[n], after[o : o + k]]) if k else terms[n]
-
-    def factor(i):
-        o = offsets[last + 1] + i * deep
-        return jnp.concatenate([before[o : o + deep], factors[i], after[o : o + deep]])
+    plan = []
+    for g, end in groups:
+        plan.append([(False, n, inner[n]) for n in range(g if g == 0 else g + 1, min(g + SPAN, last) + 1) if inner[n]])
+    plan[0] += [(True, i, deep) for i in range(3)]
+    packed = edges_packed(terms, factors, plan)
+
+    def group_exchanged(g, state):
+        group = plan[g // SPAN]
+        far, near = packed[g // SPAN]
+        pieces = [(factors if f else terms)[i] for f, i, _ in group]
+        starts_at = offsets_of(group)
+        if g:
+            k = width[g]
+            far = jnp.concatenate([jnp.where(even, state[:k], state[planes - k :]), far])
+            near = jnp.concatenate([jnp.where(even, state[planes - k :], state[:k]), near])
+            pieces, starts_at = [state] + pieces, [0] + [o + k for o in starts_at]
+        far = lax.ppermute(far, "space", across_pairs())
+        near = lax.ppermute(near, "space", beside_pairs())
+        low, high = jnp.where(even, far, near), jnp.where(even, near, far)
+        return [jnp.concatenate([low[o:e], x, high[o:e]]) for x, o, e in zip(pieces, starts_at, starts_at[1:])]
 
     def rows_exchanged(state):
         first_of_pair = place % 2 == 0
@@ -139,9 +191,9 @@
         below = jnp.where(first_of_pair, inner_rows, outer_rows)
         return jnp.concatenate([above, state[:, HALO : HALO + part], below], axis=1)
 
-    coarse_terms = [factor(i) for i in range(3)]
-    state = term(0)
-    sent = [jnp.zeros((planes + 1, part, lanes), state.dtype)]
+    wide_terms = {n: terms[n] for n in range(slices)}
+    sent = []
+    state = terms[0]
     for n in range(last + 1):
         if n:
             k = inner[n]
@@ -149,19 +201,20 @@
             o, s, w = (t[trim : t.shape[0] - trim] for t in coarse_terms)
             wide = state[depth[n - 1] - 1 - k : state.shape[0] - (depth[n - 1] - 1 - k)]
             total, upwind = around(wide)
-            state = o * wide[1:-1] + s * total + w * upwind + term(n)
-            if n in width:
-                if n % HALO == 0:
-                    state = rows_exchanged(state)
-                k = width[n]
-                low, high = exchanged(state[:k], state[planes - k :], even)
-                state = jnp.concatenate([low, state, high])
+            state = o * wide[1:-1] + s * total + w * upwind + wide_terms[n]
+        if n in width:
+            if n and n % HALO == 0:
+                state = rows_exchanged(state)
+            state, *more = group_exchanged(n, state)
+            if n == 0:
+                coarse_terms, more = more[-3:], more[:-3]
+            for m, x in zip(range(n + 1, last + 1), more):
+                wide_terms[m] = x
         k = depth[n]
         kept = state[:, HALO : HALO + part]
         sent.append(jnp.concatenate([kept[k : k + planes], jnp.where(even, kept[k - 1 : k], kept[k + planes : k + planes + 1])]))
 
-    turned = lax.broadcasted_iota(jnp.int32, (slices // 2, 1, 1, 1, 1), 0) % 2
-    sent, element, slot, even, turned = lax.optimization_barrier((jnp.stack(sent), element, slot, even, turned))
+    sent, element, slot, even, turned = lax.optimization_barrier((jnp.stack(sent[:1] + sent), element, slot, even, turned))
     back = lax.all_to_all(sent, "tm", 0, 0, tiled=True)
     back, element, slot, even, turned = lax.optimization_barrier((back, element, slot, even, turned))
     pairs = back.reshape((slices // 2, 2) + back.shape[1:])

time: 244 us -> 237 us (0.971)
  other arithmetic: 30.4 us -> 23.2 us
  local copies, waits for them, and re-layouts: 14.1 us -> 11.5 us
  Pallas kernels: 0 us -> 2.48 us
    ppermute x0 -> x8, starting transfers between devices: none -> 24.1 us  [the longest x4 23.8 us: group_exchanged(): far = lax.ppermute(far, 'space', across_pairs())]
    ppermute x9 -> x5, starting transfers between devices: 47.7 us -> 23.9 us  [exchanged(): across = lax.ppermute(jnp.where(even, low, high), 'space', across_pairs())]
    ppermute x0 -> x8, waiting for transfers between devices: none -> 21.3 us  [the longest x4 21.3 us: group_exchanged(): far = lax.ppermute(far, 'space', across_pairs())]
    ppermute x9 -> x5, waiting for transfers between devices: 60.9 us -> 41.4 us  [exchanged(): across = lax.ppermute(jnp.where(even, low, high), 'space', across_pairs())]
    add x13, other arithmetic: 5.01 us -> 2.24 us  [on_device(): state = o * wide[1:-1] + s * total + w * upwind + wide_terms[n]]
    pallas_call x0 -> x1, Pallas kernels: none -> 2.48 us  [edges_packed(): pl.pallas_call(kernel, name='edges_packed', out_shape=shapes, in_specs=[a...]
    unnamed x96 -> x69, local copies, waits for them, and re-layouts: 9.94 us -> 8.88 us
where the time goes in v7:
time: 237 us; the launch traced here: 235 us
  blocking collectives  80.6 us (34%)
  waiting for transfers between devices  63.9 us (27%)
  starting transfers between devices  50.9 us (21%)
  other arithmetic  23.2 us (10%)
  local copies, waits for them, and re-layouts  11.5 us (5%)
  Pallas kernels  2.48 us (1%)
    all_to_all x1, blocking collectives, on_device(): terms = lax.all_to_all(widened, 'tm', 0, 0, tiled=True)  41.9 us
    ppermute x5, waiting for transfers between devices, exchanged(): across = lax.ppermute(jnp.where(even, low, high), 'space', across_pairs())  41.4 us
    all_to_all x1, blocking collectives, on_device(): back = lax.all_to_all(sent, 'tm', 0, 0, tiled=True)  38.7 us
    ppermute x5, starting transfers between devices, exchanged(): across = lax.ppermute(jnp.where(even, low, high), 'space', across_pairs())  23.9 us
    ppermute x4, starting transfers between devices, group_exchanged(): far = lax.ppermute(far, 'space', across_pairs())  23.8 us
    ppermute x4, waiting for transfers between devices, group_exchanged(): far = lax.ppermute(far, 'space', across_pairs())  21.3 us
    unnamed x69, local copies, waits for them, and re-layouts  8.88 us
    add x6, other arithmetic, fine_step(): centre + d * (total - 6.0 * centre) - c * (centre - upwind) - l * centre + h  7.54 us
  transfers between devices with their start and end apart: 21, of which 9 were waited for; matrix products, arithmetic and copies ran while one was open for 2% of the time, Pallas kernels for 0%

profile of v7, /device:TPU:25, one launch (start us, length us, event | category | flops | bytes accessed | tf_op | source)
XLA Modules:
  0.0 234.9 jit_solution(10910151261895012228)
XLA Ops:
  2.7 5.0 %collective-permute-start.2 = (f32[2048,128]{1,0:T(8,128)S(1)}, f32[2048,128]{1,0:T(8,128)S(1)}, u32[]{:S(2)}, u32[]{:S(2)}) collective-permute-start(f32[2048,128]{1,0:T(8,128)S(1)} %get-tuple-element.84), channel_id=1, source_target_pairs={{1,2},{2,1},{3,4},{4,3},{5,6},{6,5},{7,8},{8,7},{9,10},{10,9},{11,... | collective-permute-start | bytes 3145736 | tf_op jit(solution)/shard_map/ppermute | solution.py:28
  7.9 4.3 %collective-permute-start = (f32[2,512,128]{2,1,0:T(8,128)S(1)}, f32[2,512,128]{2,1,0:T(8,128)S(1)}, u32[]{:S(2)}, u32[]{:S(2)}) collective-permute-start(f32[2,512,128]{2,1,0:T(8,128)S(1)} %get-tuple-element.132), channel_id=1, source_target_pairs={{1,2},{2,1},{3,4},{4,3},{5,6},{6,5},{7,8},{8,7},{9,10},{10,9},{11,... | collective-permute-start | bytes 1572872 | tf_op jit(solution)/shard_map/ppermute | solution.py:28
  12.3 15.9 %collective-permute-done = f32[2,512,128]{2,1,0:T(8,128)S(1)} collective-permute-done((f32[2,512,128]{2,1,0:T(8,128)S(1)}, f32[2,512,128]{2,1,0:T(8,128)S(1)}, u32[]{:S(2)}, u32[]{:S(2)}) %collective-permute-start) | collective-permute-done | bytes 524320 | tf_op jit(solution)/shard_map/ppermute | solution.py:28
  33.8 4.9 %collective-permute-start.4 = (f32[2,512,128]{2,1,0:T(8,128)S(1)}, f32[2,512,128]{2,1,0:T(8,128)S(1)}, u32[]{:S(2)}, u32[]{:S(2)}) collective-permute-start(f32[2,512,128]{2,1,0:T(8,128)S(1)} %get-tuple-element.111), channel_id=1, source_target_pairs={{1,2},{2,1},{3,4},{4,3},{5,6},{6,5},{7,8},{8,7},{9,10},{10,9},{11,... | collective-permute-start | bytes 1572872 | tf_op jit(solution)/shard_map/ppermute | solution.py:28
  38.8 1.8 fusion.69
  40.6 7.3 %collective-permute-done.4 = f32[2,512,128]{2,1,0:T(8,128)S(1)} collective-permute-done((f32[2,512,128]{2,1,0:T(8,128)S(1)}, f32[2,512,128]{2,1,0:T(8,128)S(1)}, u32[]{:S(2)}, u32[]{:S(2)}) %collective-permute-start.4) | collective-permute-done | bytes 524320 | tf_op jit(solution)/shard_map/ppermute | solution.py:28
  52.7 4.9 %collective-permute-start.6 = (f32[2,512,128]{2,1,0:T(8,128)}, f32[2,512,128]{2,1,0:T(8,128)}, u32[]{:S(2)}, u32[]{:S(2)}) collective-permute-start(f32[2,512,128]{2,1,0:T(8,128)} %get-tuple-element.106), channel_id=1, source_target_pairs={{1,2},{2,1},{3,4},{4,3},{5,6},{6,5},{7,8},{8,7},{9,10},{10,9},{11,... | collective-permute-start | bytes 1572872 | tf_op jit(solution)/shard_map/ppermute | solution.py:28
  57.8 9.4 %collective-permute-done.6 = f32[2,512,128]{2,1,0:T(8,128)} collective-permute-done((f32[2,512,128]{2,1,0:T(8,128)}, f32[2,512,128]{2,1,0:T(8,128)}, u32[]{:S(2)}, u32[]{:S(2)}) %collective-permute-start.6) | collective-permute-done | bytes 524320 | tf_op jit(solution)/shard_map/ppermute | solution.py:28
  70.2 1.7 fusion.32
  72.8 4.9 %collective-permute-start.8 = (f32[2,512,128]{2,1,0:T(8,128)S(1)}, f32[2,512,128]{2,1,0:T(8,128)S(1)}, u32[]{:S(2)}, u32[]{:S(2)}) collective-permute-start(f32[2,512,128]{2,1,0:T(8,128)S(1)} %get-tuple-element.102), channel_id=1, source_target_pairs={{1,2},{2,1},{3,4},{4,3},{5,6},{6,5},{7,8},{8,7},{9,10},{10,9},{11,... | collective-permute-start | bytes 1572872 | tf_op jit(solution)/shard_map/ppermute | solution.py:28
  78.1 8.8 %collective-permute-done.8 = f32[2,512,128]{2,1,0:T(8,128)S(1)} collective-permute-done((f32[2,512,128]{2,1,0:T(8,128)S(1)}, f32[2,512,128]{2,1,0:T(8,128)S(1)}, u32[]{:S(2)}, u32[]{:S(2)}) %collective-permute-start.8) | collective-permute-done | bytes 524320 | tf_op jit(solution)/shard_map/ppermute | solution.py:28
  87.9 1.7 fusion.42
  91.6 41.9 %all_to_all.10.terms_ref = f32[16,4,48,128]{3,2,1,0:T(8,128)S(1)} all-to-all(f32[16,4,48,128]{3,2,1,0:T(8,128)S(1)} %fusion.232), channel_id=1, replica_groups=mesh['tm'=16,'space'=16] {'tm'}, dimensions={0} | all-to-all | bytes 3145728 | tf_op jit(solution)/shard_map/all_to_all | solution.py:150
  133.5 2.5 %edges_packed.1 = (f32[19,48,128]{2,1,0:T(8,128)S(1)}, f32[19,48,128]{2,1,0:T(8,128)S(1)}, f32[6,48,128]{2,1,0:T(8,128)S(1)}, f32[6,48,128]{2,1,0:T(8,128)S(1)},...) custom-call(f32[16,4,48,128]{3,2,1,0:T(8,128)S(1)} %all_to_all.10.te, ...), custom_call_target="tpu_custom_call" | custom-call | tf_op jit(solution)/shard_map/edges_packed/pallas_call | solution.py:77
  136.0 5.2 %collective-permute-start.10 = (f32[19,48,128]{2,1,0:T(8,128)S(1)}, f32[19,48,128]{2,1,0:T(8,128)S(1)}, u32[]{:S(2)}, u32[]{:S(2)}) collective-permute-start(f32[19,48,128]{2,1,0:T(8,128)S(1)} %get-tuple-element.56), channel_id=1, source_target_pairs={{1,2},{2,1},{3,4},{4,3},{5,6},{6,5},{7,8},{8,7},{9,10},{10,9},{11,... | collective-permute-start | bytes 1400840 | tf_op jit(solution)/shard_map/ppermute | solution.py:178
  141.5 8.0 %collective-permute-done.10 = f32[19,48,128]{2,1,0:T(8,128)S(1)} collective-permute-done((f32[19,48,128]{2,1,0:T(8,128)S(1)}, f32[19,48,128]{2,1,0:T(8,128)S(1)}, u32[]{:S(2)}, u32[]{:S(2)}) %collective-permute-start.10) | collective-permute-done | bytes 466976 | tf_op jit(solution)/shard_map/ppermute | solution.py:178
  150.6 5.2 %collective-permute-start.12 = (f32[10,48,128]{2,1,0:T(8,128)S(1)}, f32[10,48,128]{2,1,0:T(8,128)S(1)}, u32[]{:S(2)}, u32[]{:S(2)}) collective-permute-start(f32[10,48,128]{2,1,0:T(8,128)S(1)} %get-tuple-element.163), channel_id=1, source_target_pairs={{1,2},{2,1},{3,4},{4,3},{5,6},{6,5},{7,8},{8,7},{9,10},{10,9},{11,... | collective-permute-start | bytes 737288 | tf_op jit(solution)/shard_map/ppermute | solution.py:178
  156.1 5.7 %collective-permute-done.12 = f32[10,48,128]{2,1,0:T(8,128)S(1)} collective-permute-done((f32[10,48,128]{2,1,0:T(8,128)S(1)}, f32[10,48,128]{2,1,0:T(8,128)S(1)}, u32[]{:S(2)}, u32[]{:S(2)}) %collective-permute-start.12) | collective-permute-done | bytes 245792 | tf_op jit(solution)/shard_map/ppermute | solution.py:178
  166.1 6.6 %collective-permute-start.16 = (f32[10,48,128]{2,1,0:T(8,128)S(1)}, f32[10,48,128]{2,1,0:T(8,128)S(1)}, u32[]{:S(2)}, u32[]{:S(2)}) collective-permute-start(f32[10,48,128]{2,1,0:T(8,128)S(1)} %get-tuple-element.159), channel_id=1, source_target_pairs={{1,2},{2,1},{3,4},{4,3},{5,6},{6,5},{7,8},{8,7},{9,10},{10,9},{11,... | collective-permute-start | bytes 737288 | tf_op jit(solution)/shard_map/ppermute | solution.py:178
  173.0 4.3 %collective-permute-done.16 = f32[10,48,128]{2,1,0:T(8,128)S(1)} collective-permute-done((f32[10,48,128]{2,1,0:T(8,128)S(1)}, f32[10,48,128]{2,1,0:T(8,128)S(1)}, u32[]{:S(2)}, u32[]{:S(2)}) %collective-permute-start.16) | collective-permute-done | bytes 245792 | tf_op jit(solution)/shard_map/ppermute | solution.py:178
  178.4 6.6 %collective-permute-start.18 = (f32[6,48,128]{2,1,0:T(8,128)S(1)}, f32[6,48,128]{2,1,0:T(8,128)S(1)}, u32[]{:S(2)}, u32[]{:S(2)}) collective-permute-start(f32[6,48,128]{2,1,0:T(8,128)S(1)} %pad_maximum_fusion.28), channel_id=1, source_target_pairs={{1,2},{2,1},{3,4},{4,3},{5,6},{6,5},{7,8},{8,7},{9,10},{10,9},{11,... | collective-permute-start | bytes 442376 | tf_op jit(solution)/shard_map/ppermute | solution.py:178
  185.2 3.3 %collective-permute-done.18 = f32[6,48,128]{2,1,0:T(8,128)S(1)} collective-permute-done((f32[6,48,128]{2,1,0:T(8,128)S(1)}, f32[6,48,128]{2,1,0:T(8,128)S(1)}, u32[]{:S(2)}, u32[]{:S(2)}) %collective-permute-start.18) | collective-permute-done | bytes 147488 | tf_op jit(solution)/shard_map/ppermute | solution.py:178
  189.5 38.7 %all_to_all.11 = f32[16,5,32,128]{3,2,1,0:T(8,128)S(1)} all-to-all(f32[16,5,32,128]{3,2,1,0:T(8,128)S(1)} %fusion.259), channel_id=1, replica_groups=mesh['tm'=16,'space'=16] {'tm'}, dimensions={0} | all-to-all | bytes 2621440 | tf_op jit(solution)/shard_map/all_to_all | solution.py:218
  232.7 2.1 fusion.108
  (244 shorter events, 31.8 us)
Async XLA Ops:
  2.7 25.7 %collective-permute-start.2 = (f32[2048,128]{1,0:T(8,128)S(1)}, f32[2048,128]{1,0:T(8,128)S(1)}, u32[]{:S(2)}, u32[]{:S(2)}) collective-permute-start(f32[2048,128]{1,0:T(8,128)S(1)} %get-tuple-element.84), channel_id=1, source_target_pairs={{1,2},{2,1},{3,4},{4,3},{5,6},{6,5},{7,8},{8,7},{9,10},{10,9},{11,... | collective-permute-start | bytes 3145736 | tf_op jit(solution)/shard_map/ppermute | solution.py:28
  7.7 20.7 %collective-permute-start.3 = (f32[2048,128]{1,0:T(8,128)S(1)}, f32[2048,128]{1,0:T(8,128)S(1)}, u32[]{:S(2)}, u32[]{:S(2)}) collective-permute-start(f32[2048,128]{1,0:T(8,128)S(1)} %get-tuple-element.85), channel_id=1, source_target_pairs={{0,1},{1,0},{2,3},{3,2},{4,5},{5,4},{6,7},{7,6},{8,9},{9,8},{10,11... | collective-permute-start | bytes 3145736 | tf_op jit(solution)/shard_map/ppermute | solution.py:29
  7.9 20.3 %collective-permute-start = (f32[2,512,128]{2,1,0:T(8,128)S(1)}, f32[2,512,128]{2,1,0:T(8,128)S(1)}, u32[]{:S(2)}, u32[]{:S(2)}) collective-permute-start(f32[2,512,128]{2,1,0:T(8,128)S(1)} %get-tuple-element.132), channel_id=1, source_target_pairs={{1,2},{2,1},{3,4},{4,3},{5,6},{6,5},{7,8},{8,7},{9,10},{10,9},{11,... | collective-permute-start | bytes 1572872 | tf_op jit(solution)/shard_map/ppermute | solution.py:28
  12.2 16.0 %collective-permute-start.1 = (f32[2,512,128]{2,1,0:T(8,128)S(1)}, f32[2,512,128]{2,1,0:T(8,128)S(1)}, u32[]{:S(2)}, u32[]{:S(2)}) collective-permute-start(f32[2,512,128]{2,1,0:T(8,128)S(1)} %get-tuple-element.133), channel_id=1, source_target_pairs={{0,1},{1,0},{2,3},{3,2},{4,5},{5,4},{6,7},{7,6},{8,9},{9,8},{10,11... | collective-permute-start | bytes 1572872 | tf_op jit(solution)/shard_map/ppermute | solution.py:29
  28.8 19.4 %copy-start.18 = (f32[1,512,128]{2,1,0:T(8,128)}, f32[1,512,128]{2,1,0:T(8,128)S(1)}, u32[]{:S(2)}) copy-start(f32[1,512,128]{2,1,0:T(8,128)S(1)} %get-tuple-element.119) | copy-start | bytes 786436
  28.8 19.4 %copy-start.20 = (f32[1,512,128]{2,1,0:T(8,128)}, f32[1,512,128]{2,1,0:T(8,128)S(1)}, u32[]{:S(2)}) copy-start(f32[1,512,128]{2,1,0:T(8,128)S(1)} %get-tuple-element.120) | copy-start | bytes 786436
  28.8 39.8 %copy-start.16 = (f32[1,512,128]{2,1,0:T(8,128)}, f32[1,512,128]{2,1,0:T(8,128)S(1)}, u32[]{:S(2)}) copy-start(f32[1,512,128]{2,1,0:T(8,128)S(1)} %get-tuple-element.118) | copy-start | bytes 786436
  33.8 14.1 %collective-permute-start.4 = (f32[2,512,128]{2,1,0:T(8,128)S(1)}, f32[2,512,128]{2,1,0:T(8,128)S(1)}, u32[]{:S(2)}, u32[]{:S(2)}) collective-permute-start(f32[2,512,128]{2,1,0:T(8,128)S(1)} %get-tuple-element.111), channel_id=1, source_target_pairs={{1,2},{2,1},{3,4},{4,3},{5,6},{6,5},{7,8},{8,7},{9,10},{10,9},{11,... | collective-permute-start | bytes 1572872 | tf_op jit(solution)/shard_map/ppermute | solution.py:28
  38.7 9.2 %collective-permute-start.5 = (f32[2,512,128]{2,1,0:T(8,128)S(1)}, f32[2,512,128]{2,1,0:T(8,128)S(1)}, u32[]{:S(2)}, u32[]{:S(2)}) collective-permute-start(f32[2,512,128]{2,1,0:T(8,128)S(1)} %get-tuple-element.110), channel_id=1, source_target_pairs={{0,1},{1,0},{2,3},{3,2},{4,5},{5,4},{6,7},{7,6},{8,9},{9,8},{10,11... | collective-permute-start | bytes 1572872 | tf_op jit(solution)/shard_map/ppermute | solution.py:29
  52.7 14.4 %collective-permute-start.6 = (f32[2,512,128]{2,1,0:T(8,128)}, f32[2,512,128]{2,1,0:T(8,128)}, u32[]{:S(2)}, u32[]{:S(2)}) collective-permute-start(f32[2,512,128]{2,1,0:T(8,128)} %get-tuple-element.106), channel_id=1, source_target_pairs={{1,2},{2,1},{3,4},{4,3},{5,6},{6,5},{7,8},{8,7},{9,10},{10,9},{11,... | collective-permute-start | bytes 1572872 | tf_op jit(solution)/shard_map/ppermute | solution.py:28
  57.6 9.6 %collective-permute-start.7 = (f32[2,512,128]{2,1,0:T(8,128)}, f32[2,512,128]{2,1,0:T(8,128)}, u32[]{:S(2)}, u32[]{:S(2)}) collective-permute-start(f32[2,512,128]{2,1,0:T(8,128)} %get-tuple-element.107), channel_id=1, source_target_pairs={{0,1},{1,0},{2,3},{3,2},{4,5},{5,4},{6,7},{7,6},{8,9},{9,8},{10,11... | collective-permute-start | bytes 1572872 | tf_op jit(solution)/shard_map/ppermute | solution.py:29
  72.8 14.1 %collective-permute-start.8 = (f32[2,512,128]{2,1,0:T(8,128)S(1)}, f32[2,512,128]{2,1,0:T(8,128)S(1)}, u32[]{:S(2)}, u32[]{:S(2)}) collective-permute-start(f32[2,512,128]{2,1,0:T(8,128)S(1)} %get-tuple-element.102), channel_id=1, source_target_pairs={{1,2},{2,1},{3,4},{4,3},{5,6},{6,5},{7,8},{8,7},{9,10},{10,9},{11,... | collective-permute-start | bytes 1572872 | tf_op jit(solution)/shard_map/ppermute | solution.py:28
  77.7 9.2 %collective-permute-start.9 = (f32[2,512,128]{2,1,0:T(8,128)S(1)}, f32[2,512,128]{2,1,0:T(8,128)S(1)}, u32[]{:S(2)}, u32[]{:S(2)}) collective-permute-start(f32[2,512,128]{2,1,0:T(8,128)S(1)} %get-tuple-element.103), channel_id=1, source_target_pairs={{0,1},{1,0},{2,3},{3,2},{4,5},{5,4},{6,7},{7,6},{8,9},{9,8},{10,11... | collective-permute-start | bytes 1572872 | tf_op jit(solution)/shard_map/ppermute | solution.py:29
  136.0 13.5 %collective-permute-start.10 = (f32[19,48,128]{2,1,0:T(8,128)S(1)}, f32[19,48,128]{2,1,0:T(8,128)S(1)}, u32[]{:S(2)}, u32[]{:S(2)}) collective-permute-start(f32[19,48,128]{2,1,0:T(8,128)S(1)} %get-tuple-element.56), channel_id=1, source_target_pairs={{1,2},{2,1},{3,4},{4,3},{5,6},{6,5},{7,8},{8,7},{9,10},{10,9},{11,... | collective-permute-start | bytes 1400840 | tf_op jit(solution)/shard_map/ppermute | solution.py:178
  141.2 8.2 %collective-permute-start.11 = (f32[19,48,128]{2,1,0:T(8,128)S(1)}, f32[19,48,128]{2,1,0:T(8,128)S(1)}, u32[]{:S(2)}, u32[]{:S(2)}) collective-permute-start(f32[19,48,128]{2,1,0:T(8,128)S(1)} %get-tuple-element.57), channel_id=1, source_target_pairs={{0,1},{1,0},{2,3},{3,2},{4,5},{5,4},{6,7},{7,6},{8,9},{9,8},{10,11... | collective-permute-start | bytes 1400840 | tf_op jit(solution)/shard_map/ppermute | solution.py:179
  150.6 11.1 %collective-permute-start.12 = (f32[10,48,128]{2,1,0:T(8,128)S(1)}, f32[10,48,128]{2,1,0:T(8,128)S(1)}, u32[]{:S(2)}, u32[]{:S(2)}) collective-permute-start(f32[10,48,128]{2,1,0:T(8,128)S(1)} %get-tuple-element.163), channel_id=1, source_target_pairs={{1,2},{2,1},{3,4},{4,3},{5,6},{6,5},{7,8},{8,7},{9,10},{10,9},{11,... | collective-permute-start | bytes 737288 | tf_op jit(solution)/shard_map/ppermute | solution.py:178
  155.9 5.9 %collective-permute-start.13 = (f32[10,48,128]{2,1,0:T(8,128)S(1)}, f32[10,48,128]{2,1,0:T(8,128)S(1)}, u32[]{:S(2)}, u32[]{:S(2)}) collective-permute-start(f32[10,48,128]{2,1,0:T(8,128)S(1)} %get-tuple-element.164), channel_id=1, source_target_pairs={{0,1},{1,0},{2,3},{3,2},{4,5},{5,4},{6,7},{7,6},{8,9},{9,8},{10,11... | collective-permute-start | bytes 737288 | tf_op jit(solution)/shard_map/ppermute | solution.py:179
  162.8 2.1 collective-permute-start.14
  163.4 2.7 %collective-permute-start.15 = (f32[4,8,128]{2,1,0:T(8,128)S(1)}, f32[4,8,128]{2,1,0:T(8,128)S(1)}, u32[]{:S(2)}, u32[]{:S(2)}) collective-permute-start(f32[4,8,128]{2,1,0:T(8,128)S(1)} %get-tuple-element.162), channel_id=1, source_target_pairs={{0,16},{16,0},{48,32},{32,48},{64,80},{80,64},{112,96},{96,112},{1... | collective-permute-start | bytes 49160 | tf_op jit(solution)/shard_map/ppermute | solution.py:188
  166.1 11.1 %collective-permute-start.16 = (f32[10,48,128]{2,1,0:T(8,128)S(1)}, f32[10,48,128]{2,1,0:T(8,128)S(1)}, u32[]{:S(2)}, u32[]{:S(2)}) collective-permute-start(f32[10,48,128]{2,1,0:T(8,128)S(1)} %get-tuple-element.159), channel_id=1, source_target_pairs={{1,2},{2,1},{3,4},{4,3},{5,6},{6,5},{7,8},{8,7},{9,10},{10,9},{11,... | collective-permute-start | bytes 737288 | tf_op jit(solution)/shard_map/ppermute | solution.py:178
  172.8 4.5 %collective-permute-start.17 = (f32[10,48,128]{2,1,0:T(8,128)S(1)}, f32[10,48,128]{2,1,0:T(8,128)S(1)}, u32[]{:S(2)}, u32[]{:S(2)}) collective-permute-start(f32[10,48,128]{2,1,0:T(8,128)S(1)} %get-tuple-element.160), channel_id=1, source_target_pairs={{0,1},{1,0},{2,3},{3,2},{4,5},{5,4},{6,7},{7,6},{8,9},{9,8},{10,11... | collective-permute-start | bytes 737288 | tf_op jit(solution)/shard_map/ppermute | solution.py:179
  178.3 6.8 %collective-permute-start.19 = (f32[6,48,128]{2,1,0:T(8,128)S(1)}, f32[6,48,128]{2,1,0:T(8,128)S(1)}, u32[]{:S(2)}, u32[]{:S(2)}) collective-permute-start(f32[6,48,128]{2,1,0:T(8,128)S(1)} %pad_maximum_fusion.29), channel_id=1, source_target_pairs={{0,1},{1,0},{2,3},{3,2},{4,5},{5,4},{6,7},{7,6},{8,9},{9,8},{10,11... | collective-permute-start | bytes 442376 | tf_op jit(solution)/shard_map/ppermute | solution.py:179
  178.4 10.1 %collective-permute-start.18 = (f32[6,48,128]{2,1,0:T(8,128)S(1)}, f32[6,48,128]{2,1,0:T(8,128)S(1)}, u32[]{:S(2)}, u32[]{:S(2)}) collective-permute-start(f32[6,48,128]{2,1,0:T(8,128)S(1)} %pad_maximum_fusion.28), channel_id=1, source_target_pairs={{1,2},{2,1},{3,4},{4,3},{5,6},{6,5},{7,8},{8,7},{9,10},{10,9},{11,... | collective-permute-start | bytes 442376 | tf_op jit(solution)/shard_map/ppermute | solution.py:178
  228.7 2.2 collective-permute-start.20
  (26 other events, 90.0 us)

commit v8 on v7

--- a/solution.py
+++ b/solution.py
@@ -115,7 +115,8 @@
     edge = ROUNDS - 1
     before, after = exchanged(flat(*(x[:edge] for x in raw)), flat(*(x[planes - edge :] for x in raw)), even)
     before, after = before.reshape(4, edge, rows, lanes), after.reshape(4, edge, rows, lanes)
-    fine_terms = [jnp.concatenate([before[i], raw[i], after[i]]) for i in range(4)]
+    fine_terms = lax.optimization_barrier(jnp.concatenate([before, jnp.stack(raw), after], axis=1))
+    raw = [x[edge : edge + planes] for x in fine_terms]
 
     state = start
     for turn in range(FINE // ROUNDS):
@@ -223,7 +224,7 @@
     following, across = arrived[:planes], arrived[planes:]
     beside = lax.ppermute(jnp.where(even, following[planes - 1 :], following[:1]), "space", beside_pairs())
     low, high = jnp.where(even, across, beside), jnp.where(even, beside, across)
-    coarse = coarse_linear(jnp.concatenate([low, following, high]), raw[:3])
+    coarse = coarse_linear(lax.optimization_barrier(jnp.concatenate([low, following, high])), raw[:3])
     end_state = jnp.where(slot > 0, coarse, 0.0) + element
     following = jnp.where(slot == 0, start, following)
     return end_state[None], following[None]

time: 237 us -> 233 us (0.983)
  other arithmetic: 23.2 us -> 28.7 us
  local copies, waits for them, and re-layouts: 11.5 us -> 6.44 us
  waiting for transfers between devices: 63.9 us -> 59.5 us
    unnamed x69 -> x45, local copies, waits for them, and re-layouts: 8.88 us -> 3.69 us
    ppermute x5, waiting for transfers between devices: 41.4 us -> 36.9 us  [exchanged(): across = lax.ppermute(jnp.where(even, low, high), 'space', across_pairs())]
    div x1, other arithmetic: 1.82 us -> 6.1 us  [coarse_linear(): (wide[1:-1] + FINE * (d * total + c * upwind)) / (1.0 + FINE * (6.0 * d +...]
  transfers between devices with their start and end apart: 21 -> 21, of which waited for: 9 -> 9; matrix products, arithmetic and copies ran while one was open for 2% -> 4% of each run, Pallas kernels for 0% -> 0%
where the time goes in v8:
time: 233 us; the launch traced here: 231 us
  blocking collectives  80.6 us (35%)
  waiting for transfers between devices  59.5 us (26%)
  starting transfers between devices  51.1 us (22%)
  other arithmetic  28.7 us (12%)
  local copies, waits for them, and re-layouts  6.44 us (3%)
  Pallas kernels  2.48 us (1%)
    all_to_all x1, blocking collectives, on_device(): terms = lax.all_to_all(widened, 'tm', 0, 0, tiled=True)  41.9 us
    all_to_all x1, blocking collectives, on_device(): back = lax.all_to_all(sent, 'tm', 0, 0, tiled=True)  38.7 us
    ppermute x5, waiting for transfers between devices, exchanged(): across = lax.ppermute(jnp.where(even, low, high), 'space', across_pairs())  36.9 us
    ppermute x5, starting transfers between devices, exchanged(): across = lax.ppermute(jnp.where(even, low, high), 'space', across_pairs())  24.2 us
    ppermute x4, starting transfers between devices, group_exchanged(): far = lax.ppermute(far, 'space', across_pairs())  23.8 us
    ppermute x4, waiting for transfers between devices, group_exchanged(): far = lax.ppermute(far, 'space', across_pairs())  21.3 us
    add x6, other arithmetic, fine_step(): centre + d * (total - 6.0 * centre) - c * (centre - upwind) - l * centre + h  7.66 us
    div x1, other arithmetic, coarse_linear(): (wide[1:-1] + FINE * (d * total + c * upwind)) / (1.0 + FINE * (6.0 * d +...  6.1 us
  transfers between devices with their start and end apart: 21, of which 9 were waited for; matrix products, arithmetic and copies ran while one was open for 4% of the time, Pallas kernels for 0%

profile of v8, /device:TPU:25, one launch (start us, length us, event | category | flops | bytes accessed | tf_op | source)
XLA Modules:
  0.0 230.9 jit_solution(2850313539918871474)
XLA Ops:
  2.7 5.0 %collective-permute-start.2 = (f32[2048,128]{1,0:T(8,128)S(1)}, f32[2048,128]{1,0:T(8,128)S(1)}, u32[]{:S(2)}, u32[]{:S(2)}) collective-permute-start(f32[2048,128]{1,0:T(8,128)S(1)} %get-tuple-element.87), channel_id=1, source_target_pairs={{1,2},{2,1},{3,4},{4,3},{5,6},{6,5},{7,8},{8,7},{9,10},{10,9},{11,... | collective-permute-start | bytes 3145736 | tf_op jit(solution)/shard_map/ppermute | solution.py:28
  7.9 4.3 %collective-permute-start = (f32[2,512,128]{2,1,0:T(8,128)S(1)}, f32[2,512,128]{2,1,0:T(8,128)S(1)}, u32[]{:S(2)}, u32[]{:S(2)}) collective-permute-start(f32[2,512,128]{2,1,0:T(8,128)S(1)} %get-tuple-element.127), channel_id=1, source_target_pairs={{1,2},{2,1},{3,4},{4,3},{5,6},{6,5},{7,8},{8,7},{9,10},{10,9},{11,... | collective-permute-start | bytes 1572872 | tf_op jit(solution)/shard_map/ppermute | solution.py:28
  12.3 15.9 %collective-permute-done = f32[2,512,128]{2,1,0:T(8,128)S(1)} collective-permute-done((f32[2,512,128]{2,1,0:T(8,128)S(1)}, f32[2,512,128]{2,1,0:T(8,128)S(1)}, u32[]{:S(2)}, u32[]{:S(2)}) %collective-permute-start) | collective-permute-done | bytes 524320 | tf_op jit(solution)/shard_map/ppermute | solution.py:28
  30.6 3.1 %fusion.258 = (f32[6,512,128]{2,1,0:T(8,128)}, f32[6,512,128]{2,1,0:T(8,128)S(1)}) fusion(f32[8,512,128]{2,1,0:T(8,128)S(1)} %pad_maximum_fusion.1, f32[4,6,512,128]{3,2,1,0:T(8,128)S(1)} %pad_maximum_fusion, f32[4,512,128]{2,1,0:T(8,128)S(1)} %bitcast.327, f32[2,512,128]{2,1,0:T(8,128)S(1)} %get-tuple-element.125, f32[2,512,128]{2,1,0:T(8,128)S(1)} %get-tuple-element.126), kind=kLoop, calls=%fused_computation.544 | loop fusion | flops 6684672 | bytes 15204352 | tf_op jit(solution)/shard_map/slice | solution.py:44
  35.7 4.9 %collective-permute-start.4 = (f32[2,512,128]{2,1,0:T(8,128)}, f32[2,512,128]{2,1,0:T(8,128)}, u32[]{:S(2)}, u32[]{:S(2)}) collective-permute-start(f32[2,512,128]{2,1,0:T(8,128)} %get-tuple-element.114), channel_id=1, source_target_pairs={{1,2},{2,1},{3,4},{4,3},{5,6},{6,5},{7,8},{8,7},{9,10},{10,9},{11,... | collective-permute-start | bytes 1572872 | tf_op jit(solution)/shard_map/ppermute | solution.py:28
  40.6 6.1 %fusion.66 = f32[4,512,128]{2,1,0:T(8,128)S(1)} fusion(f32[6,512,128]{2,1,0:T(8,128)} %get-tuple-element.42, f32[4,6,512,128]{3,2,1,0:T(8,128)} %copy-done), kind=kLoop, calls=%fused_computation.142 | loop fusion | flops 4194304 | bytes 8912896 | tf_op jit(solution)/shard_map/div | solution.py:51
  46.7 3.4 %collective-permute-done.4 = f32[2,512,128]{2,1,0:T(8,128)} collective-permute-done((f32[2,512,128]{2,1,0:T(8,128)}, f32[2,512,128]{2,1,0:T(8,128)}, u32[]{:S(2)}, u32[]{:S(2)}) %collective-permute-start.4) | collective-permute-done | bytes 524320 | tf_op jit(solution)/shard_map/ppermute | solution.py:28
  54.2 4.9 %collective-permute-start.6 = (f32[2,512,128]{2,1,0:T(8,128)S(1)}, f32[2,512,128]{2,1,0:T(8,128)S(1)}, u32[]{:S(2)}, u32[]{:S(2)}) collective-permute-start(f32[2,512,128]{2,1,0:T(8,128)S(1)} %get-tuple-element.109), channel_id=1, source_target_pairs={{1,2},{2,1},{3,4},{4,3},{5,6},{6,5},{7,8},{8,7},{9,10},{10,9},{11,... | collective-permute-start | bytes 1572872 | tf_op jit(solution)/shard_map/ppermute | solution.py:28
  59.5 8.9 %collective-permute-done.6 = f32[2,512,128]{2,1,0:T(8,128)S(1)} collective-permute-done((f32[2,512,128]{2,1,0:T(8,128)S(1)}, f32[2,512,128]{2,1,0:T(8,128)S(1)}, u32[]{:S(2)}, u32[]{:S(2)}) %collective-permute-start.6) | collective-permute-done | bytes 524320 | tf_op jit(solution)/shard_map/ppermute | solution.py:28
  71.3 5.1 %collective-permute-start.8 = (f32[2,512,128]{2,1,0:T(8,128)S(1)}, f32[2,512,128]{2,1,0:T(8,128)S(1)}, u32[]{:S(2)}, u32[]{:S(2)}) collective-permute-start(f32[2,512,128]{2,1,0:T(8,128)S(1)} %get-tuple-element.105), channel_id=1, source_target_pairs={{1,2},{2,1},{3,4},{4,3},{5,6},{6,5},{7,8},{8,7},{9,10},{10,9},{11,... | collective-permute-start | bytes 1572872 | tf_op jit(solution)/shard_map/ppermute | solution.py:28
  76.8 8.8 %collective-permute-done.8 = f32[2,512,128]{2,1,0:T(8,128)S(1)} collective-permute-done((f32[2,512,128]{2,1,0:T(8,128)S(1)}, f32[2,512,128]{2,1,0:T(8,128)S(1)}, u32[]{:S(2)}, u32[]{:S(2)}) %collective-permute-start.8) | collective-permute-done | bytes 524320 | tf_op jit(solution)/shard_map/ppermute | solution.py:28
  85.9 1.7 fusion.39
  88.8 41.9 %all_to_all.10.terms_ref = f32[16,4,48,128]{3,2,1,0:T(8,128)S(1)} all-to-all(f32[16,4,48,128]{3,2,1,0:T(8,128)S(1)} %fusion.229), channel_id=1, replica_groups=mesh['tm'=16,'space'=16] {'tm'}, dimensions={0} | all-to-all | bytes 3145728 | tf_op jit(solution)/shard_map/all_to_all | solution.py:151
  130.7 2.5 %edges_packed.1 = (f32[19,48,128]{2,1,0:T(8,128)S(1)}, f32[19,48,128]{2,1,0:T(8,128)S(1)}, f32[6,48,128]{2,1,0:T(8,128)S(1)}, f32[6,48,128]{2,1,0:T(8,128)S(1)},...) custom-call(f32[16,4,48,128]{3,2,1,0:T(8,128)S(1)} %all_to_all.10.te, ...), custom_call_target="tpu_custom_call" | custom-call | tf_op jit(solution)/shard_map/edges_packed/pallas_call | solution.py:77
  133.2 5.2 %collective-permute-start.10 = (f32[19,48,128]{2,1,0:T(8,128)S(1)}, f32[19,48,128]{2,1,0:T(8,128)S(1)}, u32[]{:S(2)}, u32[]{:S(2)}) collective-permute-start(f32[19,48,128]{2,1,0:T(8,128)S(1)} %get-tuple-element.56), channel_id=1, source_target_pairs={{1,2},{2,1},{3,4},{4,3},{5,6},{6,5},{7,8},{8,7},{9,10},{10,9},{11,... | collective-permute-start | bytes 1400840 | tf_op jit(solution)/shard_map/ppermute | solution.py:179
  138.7 8.0 %collective-permute-done.10 = f32[19,48,128]{2,1,0:T(8,128)S(1)} collective-permute-done((f32[19,48,128]{2,1,0:T(8,128)S(1)}, f32[19,48,128]{2,1,0:T(8,128)S(1)}, u32[]{:S(2)}, u32[]{:S(2)}) %collective-permute-start.10) | collective-permute-done | bytes 466976 | tf_op jit(solution)/shard_map/ppermute | solution.py:179
  147.8 5.2 %collective-permute-start.12 = (f32[10,48,128]{2,1,0:T(8,128)S(1)}, f32[10,48,128]{2,1,0:T(8,128)S(1)}, u32[]{:S(2)}, u32[]{:S(2)}) collective-permute-start(f32[10,48,128]{2,1,0:T(8,128)S(1)} %get-tuple-element.158), channel_id=1, source_target_pairs={{1,2},{2,1},{3,4},{4,3},{5,6},{6,5},{7,8},{8,7},{9,10},{10,9},{11,... | collective-permute-start | bytes 737288 | tf_op jit(solution)/shard_map/ppermute | solution.py:179
  153.3 5.7 %collective-permute-done.12 = f32[10,48,128]{2,1,0:T(8,128)S(1)} collective-permute-done((f32[10,48,128]{2,1,0:T(8,128)S(1)}, f32[10,48,128]{2,1,0:T(8,128)S(1)}, u32[]{:S(2)}, u32[]{:S(2)}) %collective-permute-start.12) | collective-permute-done | bytes 245792 | tf_op jit(solution)/shard_map/ppermute | solution.py:179
  163.3 6.6 %collective-permute-start.16 = (f32[10,48,128]{2,1,0:T(8,128)S(1)}, f32[10,48,128]{2,1,0:T(8,128)S(1)}, u32[]{:S(2)}, u32[]{:S(2)}) collective-permute-start(f32[10,48,128]{2,1,0:T(8,128)S(1)} %get-tuple-element.154), channel_id=1, source_target_pairs={{1,2},{2,1},{3,4},{4,3},{5,6},{6,5},{7,8},{8,7},{9,10},{10,9},{11,... | collective-permute-start | bytes 737288 | tf_op jit(solution)/shard_map/ppermute | solution.py:179
  170.2 4.3 %collective-permute-done.16 = f32[10,48,128]{2,1,0:T(8,128)S(1)} collective-permute-done((f32[10,48,128]{2,1,0:T(8,128)S(1)}, f32[10,48,128]{2,1,0:T(8,128)S(1)}, u32[]{:S(2)}, u32[]{:S(2)}) %collective-permute-start.16) | collective-permute-done | bytes 245792 | tf_op jit(solution)/shard_map/ppermute | solution.py:179
  175.6 6.6 %collective-permute-start.18 = (f32[6,48,128]{2,1,0:T(8,128)S(1)}, f32[6,48,128]{2,1,0:T(8,128)S(1)}, u32[]{:S(2)}, u32[]{:S(2)}) collective-permute-start(f32[6,48,128]{2,1,0:T(8,128)S(1)} %pad_maximum_fusion.24), channel_id=1, source_target_pairs={{1,2},{2,1},{3,4},{4,3},{5,6},{6,5},{7,8},{8,7},{9,10},{10,9},{11,... | collective-permute-start | bytes 442376 | tf_op jit(solution)/shard_map/ppermute | solution.py:179
  182.4 3.3 %collective-permute-done.18 = f32[6,48,128]{2,1,0:T(8,128)S(1)} collective-permute-done((f32[6,48,128]{2,1,0:T(8,128)S(1)}, f32[6,48,128]{2,1,0:T(8,128)S(1)}, u32[]{:S(2)}, u32[]{:S(2)}) %collective-permute-start.18) | collective-permute-done | bytes 147488 | tf_op jit(solution)/shard_map/ppermute | solution.py:179
  186.7 38.7 %all_to_all.11 = f32[16,5,32,128]{3,2,1,0:T(8,128)S(1)} all-to-all(f32[16,5,32,128]{3,2,1,0:T(8,128)S(1)} %fusion.256), channel_id=1, replica_groups=mesh['tm'=16,'space'=16] {'tm'}, dimensions={0} | all-to-all | bytes 2621440 | tf_op jit(solution)/shard_map/all_to_all | solution.py:219
  229.0 1.9 add_bitcast_fusion
  (223 shorter events, 26.6 us)
Async XLA Ops:
  2.7 25.7 %collective-permute-start.2 = (f32[2048,128]{1,0:T(8,128)S(1)}, f32[2048,128]{1,0:T(8,128)S(1)}, u32[]{:S(2)}, u32[]{:S(2)}) collective-permute-start(f32[2048,128]{1,0:T(8,128)S(1)} %get-tuple-element.87), channel_id=1, source_target_pairs={{1,2},{2,1},{3,4},{4,3},{5,6},{6,5},{7,8},{8,7},{9,10},{10,9},{11,... | collective-permute-start | bytes 3145736 | tf_op jit(solution)/shard_map/ppermute | solution.py:28
  7.7 20.7 %collective-permute-start.3 = (f32[2048,128]{1,0:T(8,128)S(1)}, f32[2048,128]{1,0:T(8,128)S(1)}, u32[]{:S(2)}, u32[]{:S(2)}) collective-permute-start(f32[2048,128]{1,0:T(8,128)S(1)} %get-tuple-element.88), channel_id=1, source_target_pairs={{0,1},{1,0},{2,3},{3,2},{4,5},{5,4},{6,7},{7,6},{8,9},{9,8},{10,11... | collective-permute-start | bytes 3145736 | tf_op jit(solution)/shard_map/ppermute | solution.py:29
  7.9 20.3 %collective-permute-start = (f32[2,512,128]{2,1,0:T(8,128)S(1)}, f32[2,512,128]{2,1,0:T(8,128)S(1)}, u32[]{:S(2)}, u32[]{:S(2)}) collective-permute-start(f32[2,512,128]{2,1,0:T(8,128)S(1)} %get-tuple-element.127), channel_id=1, source_target_pairs={{1,2},{2,1},{3,4},{4,3},{5,6},{6,5},{7,8},{8,7},{9,10},{10,9},{11,... | collective-permute-start | bytes 1572872 | tf_op jit(solution)/shard_map/ppermute | solution.py:28
  12.2 16.0 %collective-permute-start.1 = (f32[2,512,128]{2,1,0:T(8,128)S(1)}, f32[2,512,128]{2,1,0:T(8,128)S(1)}, u32[]{:S(2)}, u32[]{:S(2)}) collective-permute-start(f32[2,512,128]{2,1,0:T(8,128)S(1)} %get-tuple-element.128), channel_id=1, source_target_pairs={{0,1},{1,0},{2,3},{3,2},{4,5},{5,4},{6,7},{7,6},{8,9},{9,8},{10,11... | collective-permute-start | bytes 1572872 | tf_op jit(solution)/shard_map/ppermute | solution.py:29
  34.6 16.9 %slice-start = ((s8[6291456]{0:T(1024)(128)(4,1)}), s8[2097152]{0:T(1024)(128)(4,1)S(1)}, s32[]{:S(2)}) async-start(s8[6291456]{0:T(1024)(128)(4,1)} %bitcast.320), calls=%async_computation.2 | async-start | bytes 4194304
  35.7 11.0 %collective-permute-start.5 = (f32[2,512,128]{2,1,0:T(8,128)}, f32[2,512,128]{2,1,0:T(8,128)}, u32[]{:S(2)}, u32[]{:S(2)}) collective-permute-start(f32[2,512,128]{2,1,0:T(8,128)} %get-tuple-element.113), channel_id=1, source_target_pairs={{0,1},{1,0},{2,3},{3,2},{4,5},{5,4},{6,7},{7,6},{8,9},{9,8},{10,11... | collective-permute-start | bytes 1572872 | tf_op jit(solution)/shard_map/ppermute | solution.py:29
  35.7 14.4 %collective-permute-start.4 = (f32[2,512,128]{2,1,0:T(8,128)}, f32[2,512,128]{2,1,0:T(8,128)}, u32[]{:S(2)}, u32[]{:S(2)}) collective-permute-start(f32[2,512,128]{2,1,0:T(8,128)} %get-tuple-element.114), channel_id=1, source_target_pairs={{1,2},{2,1},{3,4},{4,3},{5,6},{6,5},{7,8},{8,7},{9,10},{10,9},{11,... | collective-permute-start | bytes 1572872 | tf_op jit(solution)/shard_map/ppermute | solution.py:28
  54.2 14.1 %collective-permute-start.6 = (f32[2,512,128]{2,1,0:T(8,128)S(1)}, f32[2,512,128]{2,1,0:T(8,128)S(1)}, u32[]{:S(2)}, u32[]{:S(2)}) collective-permute-start(f32[2,512,128]{2,1,0:T(8,128)S(1)} %get-tuple-element.109), channel_id=1, source_target_pairs={{1,2},{2,1},{3,4},{4,3},{5,6},{6,5},{7,8},{8,7},{9,10},{10,9},{11,... | collective-permute-start | bytes 1572872 | tf_op jit(solution)/shard_map/ppermute | solution.py:28
  59.1 9.2 %collective-permute-start.7 = (f32[2,512,128]{2,1,0:T(8,128)S(1)}, f32[2,512,128]{2,1,0:T(8,128)S(1)}, u32[]{:S(2)}, u32[]{:S(2)}) collective-permute-start(f32[2,512,128]{2,1,0:T(8,128)S(1)} %get-tuple-element.110), channel_id=1, source_target_pairs={{0,1},{1,0},{2,3},{3,2},{4,5},{5,4},{6,7},{7,6},{8,9},{9,8},{10,11... | collective-permute-start | bytes 1572872 | tf_op jit(solution)/shard_map/ppermute | solution.py:29
  70.3 15.6 %slice-start.2 = ((s8[6291456]{0:T(1024)(128)(4,1)}), s8[4194304]{0:T(1024)(128)(4,1)S(1)}, s32[]{:S(2)}) async-start(s8[6291456]{0:T(1024)(128)(4,1)} %bitcast.322), calls=%async_computation.4 | async-start | bytes 8388608
  71.2 14.7 %slice-start.3 = ((s8[6291456]{0:T(1024)(128)(4,1)}), s8[2097152]{0:T(1024)(128)(4,1)S(1)}, s32[]{:S(2)}) async-start(s8[6291456]{0:T(1024)(128)(4,1)} %bitcast.322), calls=%async_computation.5 | async-start | bytes 4194304
  71.3 14.4 %collective-permute-start.8 = (f32[2,512,128]{2,1,0:T(8,128)S(1)}, f32[2,512,128]{2,1,0:T(8,128)S(1)}, u32[]{:S(2)}, u32[]{:S(2)}) collective-permute-start(f32[2,512,128]{2,1,0:T(8,128)S(1)} %get-tuple-element.105), channel_id=1, source_target_pairs={{1,2},{2,1},{3,4},{4,3},{5,6},{6,5},{7,8},{8,7},{9,10},{10,9},{11,... | collective-permute-start | bytes 1572872 | tf_op jit(solution)/shard_map/ppermute | solution.py:28
  76.4 9.2 %collective-permute-start.9 = (f32[2,512,128]{2,1,0:T(8,128)S(1)}, f32[2,512,128]{2,1,0:T(8,128)S(1)}, u32[]{:S(2)}, u32[]{:S(2)}) collective-permute-start(f32[2,512,128]{2,1,0:T(8,128)S(1)} %get-tuple-element.106), channel_id=1, source_target_pairs={{0,1},{1,0},{2,3},{3,2},{4,5},{5,4},{6,7},{7,6},{8,9},{9,8},{10,11... | collective-permute-start | bytes 1572872 | tf_op jit(solution)/shard_map/ppermute | solution.py:29
  133.2 13.5 %collective-permute-start.10 = (f32[19,48,128]{2,1,0:T(8,128)S(1)}, f32[19,48,128]{2,1,0:T(8,128)S(1)}, u32[]{:S(2)}, u32[]{:S(2)}) collective-permute-start(f32[19,48,128]{2,1,0:T(8,128)S(1)} %get-tuple-element.56), channel_id=1, source_target_pairs={{1,2},{2,1},{3,4},{4,3},{5,6},{6,5},{7,8},{8,7},{9,10},{10,9},{11,... | collective-permute-start | bytes 1400840 | tf_op jit(solution)/shard_map/ppermute | solution.py:179
  138.4 8.2 %collective-permute-start.11 = (f32[19,48,128]{2,1,0:T(8,128)S(1)}, f32[19,48,128]{2,1,0:T(8,128)S(1)}, u32[]{:S(2)}, u32[]{:S(2)}) collective-permute-start(f32[19,48,128]{2,1,0:T(8,128)S(1)} %get-tuple-element.57), channel_id=1, source_target_pairs={{0,1},{1,0},{2,3},{3,2},{4,5},{5,4},{6,7},{7,6},{8,9},{9,8},{10,11... | collective-permute-start | bytes 1400840 | tf_op jit(solution)/shard_map/ppermute | solution.py:180
  147.8 11.1 %collective-permute-start.12 = (f32[10,48,128]{2,1,0:T(8,128)S(1)}, f32[10,48,128]{2,1,0:T(8,128)S(1)}, u32[]{:S(2)}, u32[]{:S(2)}) collective-permute-start(f32[10,48,128]{2,1,0:T(8,128)S(1)} %get-tuple-element.158), channel_id=1, source_target_pairs={{1,2},{2,1},{3,4},{4,3},{5,6},{6,5},{7,8},{8,7},{9,10},{10,9},{11,... | collective-permute-start | bytes 737288 | tf_op jit(solution)/shard_map/ppermute | solution.py:179
  153.1 5.9 %collective-permute-start.13 = (f32[10,48,128]{2,1,0:T(8,128)S(1)}, f32[10,48,128]{2,1,0:T(8,128)S(1)}, u32[]{:S(2)}, u32[]{:S(2)}) collective-permute-start(f32[10,48,128]{2,1,0:T(8,128)S(1)} %get-tuple-element.159), channel_id=1, source_target_pairs={{0,1},{1,0},{2,3},{3,2},{4,5},{5,4},{6,7},{7,6},{8,9},{9,8},{10,11... | collective-permute-start | bytes 737288 | tf_op jit(solution)/shard_map/ppermute | solution.py:180
  160.0 2.1 collective-permute-start.14
  160.6 2.7 %collective-permute-start.15 = (f32[4,8,128]{2,1,0:T(8,128)S(1)}, f32[4,8,128]{2,1,0:T(8,128)S(1)}, u32[]{:S(2)}, u32[]{:S(2)}) collective-permute-start(f32[4,8,128]{2,1,0:T(8,128)S(1)} %get-tuple-element.157), channel_id=1, source_target_pairs={{0,16},{16,0},{48,32},{32,48},{64,80},{80,64},{112,96},{96,112},{1... | collective-permute-start | bytes 49160 | tf_op jit(solution)/shard_map/ppermute | solution.py:189
  163.3 11.1 %collective-permute-start.16 = (f32[10,48,128]{2,1,0:T(8,128)S(1)}, f32[10,48,128]{2,1,0:T(8,128)S(1)}, u32[]{:S(2)}, u32[]{:S(2)}) collective-permute-start(f32[10,48,128]{2,1,0:T(8,128)S(1)} %get-tuple-element.154), channel_id=1, source_target_pairs={{1,2},{2,1},{3,4},{4,3},{5,6},{6,5},{7,8},{8,7},{9,10},{10,9},{11,... | collective-permute-start | bytes 737288 | tf_op jit(solution)/shard_map/ppermute | solution.py:179
  170.0 4.5 %collective-permute-start.17 = (f32[10,48,128]{2,1,0:T(8,128)S(1)}, f32[10,48,128]{2,1,0:T(8,128)S(1)}, u32[]{:S(2)}, u32[]{:S(2)}) collective-permute-start(f32[10,48,128]{2,1,0:T(8,128)S(1)} %get-tuple-element.155), channel_id=1, source_target_pairs={{0,1},{1,0},{2,3},{3,2},{4,5},{5,4},{6,7},{7,6},{8,9},{9,8},{10,11... | collective-permute-start | bytes 737288 | tf_op jit(solution)/shard_map/ppermute | solution.py:180
  175.5 6.8 %collective-permute-start.19 = (f32[6,48,128]{2,1,0:T(8,128)S(1)}, f32[6,48,128]{2,1,0:T(8,128)S(1)}, u32[]{:S(2)}, u32[]{:S(2)}) collective-permute-start(f32[6,48,128]{2,1,0:T(8,128)S(1)} %pad_maximum_fusion.25), channel_id=1, source_target_pairs={{0,1},{1,0},{2,3},{3,2},{4,5},{5,4},{6,7},{7,6},{8,9},{9,8},{10,11... | collective-permute-start | bytes 442376 | tf_op jit(solution)/shard_map/ppermute | solution.py:180
  175.6 10.1 %collective-permute-start.18 = (f32[6,48,128]{2,1,0:T(8,128)S(1)}, f32[6,48,128]{2,1,0:T(8,128)S(1)}, u32[]{:S(2)}, u32[]{:S(2)}) collective-permute-start(f32[6,48,128]{2,1,0:T(8,128)S(1)} %pad_maximum_fusion.24), channel_id=1, source_target_pairs={{1,2},{2,1},{3,4},{4,3},{5,6},{6,5},{7,8},{8,7},{9,10},{10,9},{11,... | collective-permute-start | bytes 442376 | tf_op jit(solution)/shard_map/ppermute | solution.py:179
  225.9 2.3 %collective-permute-start.20 = (f32[1,512,128]{2,1,0:T(8,128)S(1)}, f32[1,512,128]{2,1,0:T(8,128)S(1)}, u32[]{:S(2)}, u32[]{:S(2)}) collective-permute-start(f32[1,512,128]{2,1,0:T(8,128)S(1)} %bitcast.338), channel_id=1, source_target_pairs={{0,1},{1,0},{2,3},{3,2},{4,5},{5,4},{6,7},{7,6},{8,9},{9,8},{10,11... | collective-permute-start | bytes 786440 | tf_op jit(solution)/shard_map/ppermute | solution.py:225
  (14 other events, 58.2 us)

commit v9 on v8

--- a/solution.py
+++ b/solution.py
@@ -115,7 +115,7 @@
     edge = ROUNDS - 1
     before, after = exchanged(flat(*(x[:edge] for x in raw)), flat(*(x[planes - edge :] for x in raw)), even)
     before, after = before.reshape(4, edge, rows, lanes), after.reshape(4, edge, rows, lanes)
-    fine_terms = lax.optimization_barrier(jnp.concatenate([before, jnp.stack(raw), after], axis=1))
+    fine_terms = lax.optimization_barrier(jnp.concatenate([before, lax.optimization_barrier(jnp.stack(raw)), after], axis=1))
     raw = [x[edge : edge + planes] for x in fine_terms]
 
     state = start

time: 233 us -> 231 us (level)
  no operation moved by 1% of the time
where the time goes in v9:
time: 231 us; the launch traced here: 230 us
  blocking collectives  80.6 us (35%)
  waiting for transfers between devices  59 us (26%)
  starting transfers between devices  51.1 us (22%)
  other arithmetic  29.1 us (13%)
  local copies, waits for them, and re-layouts  5.07 us (2%)
  Pallas kernels  2.48 us (1%)
    all_to_all x1, blocking collectives, on_device(): terms = lax.all_to_all(widened, 'tm', 0, 0, tiled=True)  41.9 us
    all_to_all x1, blocking collectives, on_device(): back = lax.all_to_all(sent, 'tm', 0, 0, tiled=True)  38.7 us
    ppermute x5, waiting for transfers between devices, exchanged(): across = lax.ppermute(jnp.where(even, low, high), 'space', across_pairs())  36.4 us
    ppermute x5, starting transfers between devices, exchanged(): across = lax.ppermute(jnp.where(even, low, high), 'space', across_pairs())  24.2 us
    ppermute x4, starting transfers between devices, group_exchanged(): far = lax.ppermute(far, 'space', across_pairs())  23.8 us
    ppermute x4, waiting for transfers between devices, group_exchanged(): far = lax.ppermute(far, 'space', across_pairs())  21.3 us
    add x6, other arithmetic, fine_step(): centre + d * (total - 6.0 * centre) - c * (centre - upwind) - l * centre + h  7.69 us
    div x1, other arithmetic, coarse_linear(): (wide[1:-1] + FINE * (d * total + c * upwind)) / (1.0 + FINE * (6.0 * d +...  6.1 us
  transfers between devices with their start and end apart: 21, of which 9 were waited for; matrix products, arithmetic and copies ran while one was open for 4% of the time, Pallas kernels for 0%

profile of v9, /device:TPU:25, one launch (start us, length us, event | category | flops | bytes accessed | tf_op | source)
XLA Modules:
  0.0 229.6 jit_solution(15545570590072262879)
XLA Ops:
  2.7 5.0 %collective-permute-start.2 = (f32[2048,128]{1,0:T(8,128)S(1)}, f32[2048,128]{1,0:T(8,128)S(1)}, u32[]{:S(2)}, u32[]{:S(2)}) collective-permute-start(f32[2048,128]{1,0:T(8,128)S(1)} %get-tuple-element.87), channel_id=1, source_target_pairs={{1,2},{2,1},{3,4},{4,3},{5,6},{6,5},{7,8},{8,7},{9,10},{10,9},{11,... | collective-permute-start | bytes 3145736 | tf_op jit(solution)/shard_map/ppermute | solution.py:28
  7.9 4.3 %collective-permute-start = (f32[2,512,128]{2,1,0:T(8,128)S(1)}, f32[2,512,128]{2,1,0:T(8,128)S(1)}, u32[]{:S(2)}, u32[]{:S(2)}) collective-permute-start(f32[2,512,128]{2,1,0:T(8,128)S(1)} %get-tuple-element.127), channel_id=1, source_target_pairs={{1,2},{2,1},{3,4},{4,3},{5,6},{6,5},{7,8},{8,7},{9,10},{10,9},{11,... | collective-permute-start | bytes 1572872 | tf_op jit(solution)/shard_map/ppermute | solution.py:28
  12.8 15.4 %collective-permute-done = f32[2,512,128]{2,1,0:T(8,128)S(1)} collective-permute-done((f32[2,512,128]{2,1,0:T(8,128)S(1)}, f32[2,512,128]{2,1,0:T(8,128)S(1)}, u32[]{:S(2)}, u32[]{:S(2)}) %collective-permute-start) | collective-permute-done | bytes 524320 | tf_op jit(solution)/shard_map/ppermute | solution.py:28
  29.3 3.1 %fusion.258 = (f32[6,512,128]{2,1,0:T(8,128)}, f32[6,512,128]{2,1,0:T(8,128)S(1)}) fusion(f32[8,512,128]{2,1,0:T(8,128)S(1)} %pad_maximum_fusion.2, f32[4,6,512,128]{3,2,1,0:T(8,128)S(1)} %pad_maximum_fusion, f32[4,512,128]{2,1,0:T(8,128)S(1)} %bitcast.327, f32[2,512,128]{2,1,0:T(8,128)S(1)} %get-tuple-element.125, f32[2,512,128]{2,1,0:T(8,128)S(1)} %get-tuple-element.126), kind=kLoop, calls=%fused_computation.545 | loop fusion | flops 6684672 | bytes 15204352 | tf_op jit(solution)/shard_map/slice | solution.py:44
  34.4 4.9 %collective-permute-start.4 = (f32[2,512,128]{2,1,0:T(8,128)}, f32[2,512,128]{2,1,0:T(8,128)}, u32[]{:S(2)}, u32[]{:S(2)}) collective-permute-start(f32[2,512,128]{2,1,0:T(8,128)} %get-tuple-element.114), channel_id=1, source_target_pairs={{1,2},{2,1},{3,4},{4,3},{5,6},{6,5},{7,8},{8,7},{9,10},{10,9},{11,... | collective-permute-start | bytes 1572872 | tf_op jit(solution)/shard_map/ppermute | solution.py:28
  39.4 6.1 %fusion.66 = f32[4,512,128]{2,1,0:T(8,128)S(1)} fusion(f32[6,512,128]{2,1,0:T(8,128)} %get-tuple-element.42, f32[4,6,512,128]{3,2,1,0:T(8,128)} %copy-done), kind=kLoop, calls=%fused_computation.143 | loop fusion | flops 4194304 | bytes 8912896 | tf_op jit(solution)/shard_map/div | solution.py:51
  45.5 3.3 %collective-permute-done.4 = f32[2,512,128]{2,1,0:T(8,128)} collective-permute-done((f32[2,512,128]{2,1,0:T(8,128)}, f32[2,512,128]{2,1,0:T(8,128)}, u32[]{:S(2)}, u32[]{:S(2)}) %collective-permute-start.4) | collective-permute-done | bytes 524320 | tf_op jit(solution)/shard_map/ppermute | solution.py:28
  52.9 4.9 %collective-permute-start.6 = (f32[2,512,128]{2,1,0:T(8,128)S(1)}, f32[2,512,128]{2,1,0:T(8,128)S(1)}, u32[]{:S(2)}, u32[]{:S(2)}) collective-permute-start(f32[2,512,128]{2,1,0:T(8,128)S(1)} %get-tuple-element.109), channel_id=1, source_target_pairs={{1,2},{2,1},{3,4},{4,3},{5,6},{6,5},{7,8},{8,7},{9,10},{10,9},{11,... | collective-permute-start | bytes 1572872 | tf_op jit(solution)/shard_map/ppermute | solution.py:28
  58.1 8.9 %collective-permute-done.6 = f32[2,512,128]{2,1,0:T(8,128)S(1)} collective-permute-done((f32[2,512,128]{2,1,0:T(8,128)S(1)}, f32[2,512,128]{2,1,0:T(8,128)S(1)}, u32[]{:S(2)}, u32[]{:S(2)}) %collective-permute-start.6) | collective-permute-done | bytes 524320 | tf_op jit(solution)/shard_map/ppermute | solution.py:28
  69.9 5.1 %collective-permute-start.8 = (f32[2,512,128]{2,1,0:T(8,128)S(1)}, f32[2,512,128]{2,1,0:T(8,128)S(1)}, u32[]{:S(2)}, u32[]{:S(2)}) collective-permute-start(f32[2,512,128]{2,1,0:T(8,128)S(1)} %get-tuple-element.105), channel_id=1, source_target_pairs={{1,2},{2,1},{3,4},{4,3},{5,6},{6,5},{7,8},{8,7},{9,10},{10,9},{11,... | collective-permute-start | bytes 1572872 | tf_op jit(solution)/shard_map/ppermute | solution.py:28
  75.5 8.8 %collective-permute-done.8 = f32[2,512,128]{2,1,0:T(8,128)S(1)} collective-permute-done((f32[2,512,128]{2,1,0:T(8,128)S(1)}, f32[2,512,128]{2,1,0:T(8,128)S(1)}, u32[]{:S(2)}, u32[]{:S(2)}) %collective-permute-start.8) | collective-permute-done | bytes 524320 | tf_op jit(solution)/shard_map/ppermute | solution.py:28
  84.6 1.7 fusion.39
  87.4 41.9 %all_to_all.10.terms_ref = f32[16,4,48,128]{3,2,1,0:T(8,128)S(1)} all-to-all(f32[16,4,48,128]{3,2,1,0:T(8,128)S(1)} %fusion.229), channel_id=1, replica_groups=mesh['tm'=16,'space'=16] {'tm'}, dimensions={0} | all-to-all | bytes 3145728 | tf_op jit(solution)/shard_map/all_to_all | solution.py:151
  129.4 2.5 %edges_packed.1 = (f32[19,48,128]{2,1,0:T(8,128)S(1)}, f32[19,48,128]{2,1,0:T(8,128)S(1)}, f32[6,48,128]{2,1,0:T(8,128)S(1)}, f32[6,48,128]{2,1,0:T(8,128)S(1)},...) custom-call(f32[16,4,48,128]{3,2,1,0:T(8,128)S(1)} %all_to_all.10.te, ...), custom_call_target="tpu_custom_call" | custom-call | tf_op jit(solution)/shard_map/edges_packed/pallas_call | solution.py:77
  131.8 5.2 %collective-permute-start.10 = (f32[19,48,128]{2,1,0:T(8,128)S(1)}, f32[19,48,128]{2,1,0:T(8,128)S(1)}, u32[]{:S(2)}, u32[]{:S(2)}) collective-permute-start(f32[19,48,128]{2,1,0:T(8,128)S(1)} %get-tuple-element.56), channel_id=1, source_target_pairs={{1,2},{2,1},{3,4},{4,3},{5,6},{6,5},{7,8},{8,7},{9,10},{10,9},{11,... | collective-permute-start | bytes 1400840 | tf_op jit(solution)/shard_map/ppermute | solution.py:179
  137.3 8.0 %collective-permute-done.10 = f32[19,48,128]{2,1,0:T(8,128)S(1)} collective-permute-done((f32[19,48,128]{2,1,0:T(8,128)S(1)}, f32[19,48,128]{2,1,0:T(8,128)S(1)}, u32[]{:S(2)}, u32[]{:S(2)}) %collective-permute-start.10) | collective-permute-done | bytes 466976 | tf_op jit(solution)/shard_map/ppermute | solution.py:179
  146.5 5.2 %collective-permute-start.12 = (f32[10,48,128]{2,1,0:T(8,128)S(1)}, f32[10,48,128]{2,1,0:T(8,128)S(1)}, u32[]{:S(2)}, u32[]{:S(2)}) collective-permute-start(f32[10,48,128]{2,1,0:T(8,128)S(1)} %get-tuple-element.158), channel_id=1, source_target_pairs={{1,2},{2,1},{3,4},{4,3},{5,6},{6,5},{7,8},{8,7},{9,10},{10,9},{11,... | collective-permute-start | bytes 737288 | tf_op jit(solution)/shard_map/ppermute | solution.py:179
  151.9 5.7 %collective-permute-done.12 = f32[10,48,128]{2,1,0:T(8,128)S(1)} collective-permute-done((f32[10,48,128]{2,1,0:T(8,128)S(1)}, f32[10,48,128]{2,1,0:T(8,128)S(1)}, u32[]{:S(2)}, u32[]{:S(2)}) %collective-permute-start.12) | collective-permute-done | bytes 245792 | tf_op jit(solution)/shard_map/ppermute | solution.py:179
  162.0 6.6 %collective-permute-start.16 = (f32[10,48,128]{2,1,0:T(8,128)S(1)}, f32[10,48,128]{2,1,0:T(8,128)S(1)}, u32[]{:S(2)}, u32[]{:S(2)}) collective-permute-start(f32[10,48,128]{2,1,0:T(8,128)S(1)} %get-tuple-element.154), channel_id=1, source_target_pairs={{1,2},{2,1},{3,4},{4,3},{5,6},{6,5},{7,8},{8,7},{9,10},{10,9},{11,... | collective-permute-start | bytes 737288 | tf_op jit(solution)/shard_map/ppermute | solution.py:179
  168.8 4.3 %collective-permute-done.16 = f32[10,48,128]{2,1,0:T(8,128)S(1)} collective-permute-done((f32[10,48,128]{2,1,0:T(8,128)S(1)}, f32[10,48,128]{2,1,0:T(8,128)S(1)}, u32[]{:S(2)}, u32[]{:S(2)}) %collective-permute-start.16) | collective-permute-done | bytes 245792 | tf_op jit(solution)/shard_map/ppermute | solution.py:179
  174.3 6.6 %collective-permute-start.18 = (f32[6,48,128]{2,1,0:T(8,128)S(1)}, f32[6,48,128]{2,1,0:T(8,128)S(1)}, u32[]{:S(2)}, u32[]{:S(2)}) collective-permute-start(f32[6,48,128]{2,1,0:T(8,128)S(1)} %pad_maximum_fusion.25), channel_id=1, source_target_pairs={{1,2},{2,1},{3,4},{4,3},{5,6},{6,5},{7,8},{8,7},{9,10},{10,9},{11,... | collective-permute-start | bytes 442376 | tf_op jit(solution)/shard_map/ppermute | solution.py:179
  181.0 3.3 %collective-permute-done.18 = f32[6,48,128]{2,1,0:T(8,128)S(1)} collective-permute-done((f32[6,48,128]{2,1,0:T(8,128)S(1)}, f32[6,48,128]{2,1,0:T(8,128)S(1)}, u32[]{:S(2)}, u32[]{:S(2)}) %collective-permute-start.18) | collective-permute-done | bytes 147488 | tf_op jit(solution)/shard_map/ppermute | solution.py:179
  185.4 38.7 %all_to_all.11 = f32[16,5,32,128]{3,2,1,0:T(8,128)S(1)} all-to-all(f32[16,5,32,128]{3,2,1,0:T(8,128)S(1)} %fusion.256), channel_id=1, replica_groups=mesh['tm'=16,'space'=16] {'tm'}, dimensions={0} | all-to-all | bytes 2621440 | tf_op jit(solution)/shard_map/all_to_all | solution.py:219
  227.7 1.9 add_bitcast_fusion
  (224 shorter events, 25.7 us)
Async XLA Ops:
  2.7 25.7 %collective-permute-start.2 = (f32[2048,128]{1,0:T(8,128)S(1)}, f32[2048,128]{1,0:T(8,128)S(1)}, u32[]{:S(2)}, u32[]{:S(2)}) collective-permute-start(f32[2048,128]{1,0:T(8,128)S(1)} %get-tuple-element.87), channel_id=1, source_target_pairs={{1,2},{2,1},{3,4},{4,3},{5,6},{6,5},{7,8},{8,7},{9,10},{10,9},{11,... | collective-permute-start | bytes 3145736 | tf_op jit(solution)/shard_map/ppermute | solution.py:28
  7.8 20.7 %collective-permute-start.3 = (f32[2048,128]{1,0:T(8,128)S(1)}, f32[2048,128]{1,0:T(8,128)S(1)}, u32[]{:S(2)}, u32[]{:S(2)}) collective-permute-start(f32[2048,128]{1,0:T(8,128)S(1)} %get-tuple-element.88), channel_id=1, source_target_pairs={{0,1},{1,0},{2,3},{3,2},{4,5},{5,4},{6,7},{7,6},{8,9},{9,8},{10,11... | collective-permute-start | bytes 3145736 | tf_op jit(solution)/shard_map/ppermute | solution.py:29
  7.9 20.3 %collective-permute-start = (f32[2,512,128]{2,1,0:T(8,128)S(1)}, f32[2,512,128]{2,1,0:T(8,128)S(1)}, u32[]{:S(2)}, u32[]{:S(2)}) collective-permute-start(f32[2,512,128]{2,1,0:T(8,128)S(1)} %get-tuple-element.127), channel_id=1, source_target_pairs={{1,2},{2,1},{3,4},{4,3},{5,6},{6,5},{7,8},{8,7},{9,10},{10,9},{11,... | collective-permute-start | bytes 1572872 | tf_op jit(solution)/shard_map/ppermute | solution.py:28
  12.3 16.0 %collective-permute-start.1 = (f32[2,512,128]{2,1,0:T(8,128)S(1)}, f32[2,512,128]{2,1,0:T(8,128)S(1)}, u32[]{:S(2)}, u32[]{:S(2)}) collective-permute-start(f32[2,512,128]{2,1,0:T(8,128)S(1)} %get-tuple-element.128), channel_id=1, source_target_pairs={{0,1},{1,0},{2,3},{3,2},{4,5},{5,4},{6,7},{7,6},{8,9},{9,8},{10,11... | collective-permute-start | bytes 1572872 | tf_op jit(solution)/shard_map/ppermute | solution.py:29
  33.3 16.9 %slice-start = ((s8[6291456]{0:T(1024)(128)(4,1)}), s8[2097152]{0:T(1024)(128)(4,1)S(1)}, s32[]{:S(2)}) async-start(s8[6291456]{0:T(1024)(128)(4,1)} %bitcast.320), calls=%async_computation.2 | async-start | bytes 4194304
  34.4 14.4 %collective-permute-start.4 = (f32[2,512,128]{2,1,0:T(8,128)}, f32[2,512,128]{2,1,0:T(8,128)}, u32[]{:S(2)}, u32[]{:S(2)}) collective-permute-start(f32[2,512,128]{2,1,0:T(8,128)} %get-tuple-element.114), channel_id=1, source_target_pairs={{1,2},{2,1},{3,4},{4,3},{5,6},{6,5},{7,8},{8,7},{9,10},{10,9},{11,... | collective-permute-start | bytes 1572872 | tf_op jit(solution)/shard_map/ppermute | solution.py:28
  39.2 9.6 %collective-permute-start.5 = (f32[2,512,128]{2,1,0:T(8,128)}, f32[2,512,128]{2,1,0:T(8,128)}, u32[]{:S(2)}, u32[]{:S(2)}) collective-permute-start(f32[2,512,128]{2,1,0:T(8,128)} %get-tuple-element.113), channel_id=1, source_target_pairs={{0,1},{1,0},{2,3},{3,2},{4,5},{5,4},{6,7},{7,6},{8,9},{9,8},{10,11... | collective-permute-start | bytes 1572872 | tf_op jit(solution)/shard_map/ppermute | solution.py:29
  52.9 14.1 %collective-permute-start.6 = (f32[2,512,128]{2,1,0:T(8,128)S(1)}, f32[2,512,128]{2,1,0:T(8,128)S(1)}, u32[]{:S(2)}, u32[]{:S(2)}) collective-permute-start(f32[2,512,128]{2,1,0:T(8,128)S(1)} %get-tuple-element.109), channel_id=1, source_target_pairs={{1,2},{2,1},{3,4},{4,3},{5,6},{6,5},{7,8},{8,7},{9,10},{10,9},{11,... | collective-permute-start | bytes 1572872 | tf_op jit(solution)/shard_map/ppermute | solution.py:28
  57.8 9.2 %collective-permute-start.7 = (f32[2,512,128]{2,1,0:T(8,128)S(1)}, f32[2,512,128]{2,1,0:T(8,128)S(1)}, u32[]{:S(2)}, u32[]{:S(2)}) collective-permute-start(f32[2,512,128]{2,1,0:T(8,128)S(1)} %get-tuple-element.110), channel_id=1, source_target_pairs={{0,1},{1,0},{2,3},{3,2},{4,5},{5,4},{6,7},{7,6},{8,9},{9,8},{10,11... | collective-permute-start | bytes 1572872 | tf_op jit(solution)/shard_map/ppermute | solution.py:29
  69.0 15.6 %slice-start.2 = ((s8[6291456]{0:T(1024)(128)(4,1)}), s8[4194304]{0:T(1024)(128)(4,1)S(1)}, s32[]{:S(2)}) async-start(s8[6291456]{0:T(1024)(128)(4,1)} %bitcast.322), calls=%async_computation.4 | async-start | bytes 8388608
  69.8 14.7 %slice-start.3 = ((s8[6291456]{0:T(1024)(128)(4,1)}), s8[2097152]{0:T(1024)(128)(4,1)S(1)}, s32[]{:S(2)}) async-start(s8[6291456]{0:T(1024)(128)(4,1)} %bitcast.322), calls=%async_computation.5 | async-start | bytes 4194304
  69.9 14.4 %collective-permute-start.8 = (f32[2,512,128]{2,1,0:T(8,128)S(1)}, f32[2,512,128]{2,1,0:T(8,128)S(1)}, u32[]{:S(2)}, u32[]{:S(2)}) collective-permute-start(f32[2,512,128]{2,1,0:T(8,128)S(1)} %get-tuple-element.105), channel_id=1, source_target_pairs={{1,2},{2,1},{3,4},{4,3},{5,6},{6,5},{7,8},{8,7},{9,10},{10,9},{11,... | collective-permute-start | bytes 1572872 | tf_op jit(solution)/shard_map/ppermute | solution.py:28
  75.1 9.2 %collective-permute-start.9 = (f32[2,512,128]{2,1,0:T(8,128)S(1)}, f32[2,512,128]{2,1,0:T(8,128)S(1)}, u32[]{:S(2)}, u32[]{:S(2)}) collective-permute-start(f32[2,512,128]{2,1,0:T(8,128)S(1)} %get-tuple-element.106), channel_id=1, source_target_pairs={{0,1},{1,0},{2,3},{3,2},{4,5},{5,4},{6,7},{7,6},{8,9},{9,8},{10,11... | collective-permute-start | bytes 1572872 | tf_op jit(solution)/shard_map/ppermute | solution.py:29
  131.8 13.5 %collective-permute-start.10 = (f32[19,48,128]{2,1,0:T(8,128)S(1)}, f32[19,48,128]{2,1,0:T(8,128)S(1)}, u32[]{:S(2)}, u32[]{:S(2)}) collective-permute-start(f32[19,48,128]{2,1,0:T(8,128)S(1)} %get-tuple-element.56), channel_id=1, source_target_pairs={{1,2},{2,1},{3,4},{4,3},{5,6},{6,5},{7,8},{8,7},{9,10},{10,9},{11,... | collective-permute-start | bytes 1400840 | tf_op jit(solution)/shard_map/ppermute | solution.py:179
  137.1 8.2 %collective-permute-start.11 = (f32[19,48,128]{2,1,0:T(8,128)S(1)}, f32[19,48,128]{2,1,0:T(8,128)S(1)}, u32[]{:S(2)}, u32[]{:S(2)}) collective-permute-start(f32[19,48,128]{2,1,0:T(8,128)S(1)} %get-tuple-element.57), channel_id=1, source_target_pairs={{0,1},{1,0},{2,3},{3,2},{4,5},{5,4},{6,7},{7,6},{8,9},{9,8},{10,11... | collective-permute-start | bytes 1400840 | tf_op jit(solution)/shard_map/ppermute | solution.py:180
  146.5 11.1 %collective-permute-start.12 = (f32[10,48,128]{2,1,0:T(8,128)S(1)}, f32[10,48,128]{2,1,0:T(8,128)S(1)}, u32[]{:S(2)}, u32[]{:S(2)}) collective-permute-start(f32[10,48,128]{2,1,0:T(8,128)S(1)} %get-tuple-element.158), channel_id=1, source_target_pairs={{1,2},{2,1},{3,4},{4,3},{5,6},{6,5},{7,8},{8,7},{9,10},{10,9},{11,... | collective-permute-start | bytes 737288 | tf_op jit(solution)/shard_map/ppermute | solution.py:179
  151.7 5.9 %collective-permute-start.13 = (f32[10,48,128]{2,1,0:T(8,128)S(1)}, f32[10,48,128]{2,1,0:T(8,128)S(1)}, u32[]{:S(2)}, u32[]{:S(2)}) collective-permute-start(f32[10,48,128]{2,1,0:T(8,128)S(1)} %get-tuple-element.159), channel_id=1, source_target_pairs={{0,1},{1,0},{2,3},{3,2},{4,5},{5,4},{6,7},{7,6},{8,9},{9,8},{10,11... | collective-permute-start | bytes 737288 | tf_op jit(solution)/shard_map/ppermute | solution.py:180
  158.6 2.1 collective-permute-start.14
  159.3 2.7 %collective-permute-start.15 = (f32[4,8,128]{2,1,0:T(8,128)S(1)}, f32[4,8,128]{2,1,0:T(8,128)S(1)}, u32[]{:S(2)}, u32[]{:S(2)}) collective-permute-start(f32[4,8,128]{2,1,0:T(8,128)S(1)} %get-tuple-element.157), channel_id=1, source_target_pairs={{0,16},{16,0},{48,32},{32,48},{64,80},{80,64},{112,96},{96,112},{1... | collective-permute-start | bytes 49160 | tf_op jit(solution)/shard_map/ppermute | solution.py:189
  162.0 11.1 %collective-permute-start.16 = (f32[10,48,128]{2,1,0:T(8,128)S(1)}, f32[10,48,128]{2,1,0:T(8,128)S(1)}, u32[]{:S(2)}, u32[]{:S(2)}) collective-permute-start(f32[10,48,128]{2,1,0:T(8,128)S(1)} %get-tuple-element.154), channel_id=1, source_target_pairs={{1,2},{2,1},{3,4},{4,3},{5,6},{6,5},{7,8},{8,7},{9,10},{10,9},{11,... | collective-permute-start | bytes 737288 | tf_op jit(solution)/shard_map/ppermute | solution.py:179
  168.7 4.5 %collective-permute-start.17 = (f32[10,48,128]{2,1,0:T(8,128)S(1)}, f32[10,48,128]{2,1,0:T(8,128)S(1)}, u32[]{:S(2)}, u32[]{:S(2)}) collective-permute-start(f32[10,48,128]{2,1,0:T(8,128)S(1)} %get-tuple-element.155), channel_id=1, source_target_pairs={{0,1},{1,0},{2,3},{3,2},{4,5},{5,4},{6,7},{7,6},{8,9},{9,8},{10,11... | collective-permute-start | bytes 737288 | tf_op jit(solution)/shard_map/ppermute | solution.py:180
  174.2 6.8 %collective-permute-start.19 = (f32[6,48,128]{2,1,0:T(8,128)S(1)}, f32[6,48,128]{2,1,0:T(8,128)S(1)}, u32[]{:S(2)}, u32[]{:S(2)}) collective-permute-start(f32[6,48,128]{2,1,0:T(8,128)S(1)} %pad_maximum_fusion.26), channel_id=1, source_target_pairs={{0,1},{1,0},{2,3},{3,2},{4,5},{5,4},{6,7},{7,6},{8,9},{9,8},{10,11... | collective-permute-start | bytes 442376 | tf_op jit(solution)/shard_map/ppermute | solution.py:180
  174.3 10.1 %collective-permute-start.18 = (f32[6,48,128]{2,1,0:T(8,128)S(1)}, f32[6,48,128]{2,1,0:T(8,128)S(1)}, u32[]{:S(2)}, u32[]{:S(2)}) collective-permute-start(f32[6,48,128]{2,1,0:T(8,128)S(1)} %pad_maximum_fusion.25), channel_id=1, source_target_pairs={{1,2},{2,1},{3,4},{4,3},{5,6},{6,5},{7,8},{8,7},{9,10},{10,9},{11,... | collective-permute-start | bytes 442376 | tf_op jit(solution)/shard_map/ppermute | solution.py:179
  224.6 2.3 %collective-permute-start.20 = (f32[1,512,128]{2,1,0:T(8,128)S(1)}, f32[1,512,128]{2,1,0:T(8,128)S(1)}, u32[]{:S(2)}, u32[]{:S(2)}) collective-permute-start(f32[1,512,128]{2,1,0:T(8,128)S(1)} %bitcast.338), channel_id=1, source_target_pairs={{0,1},{1,0},{2,3},{3,2},{4,5},{5,4},{6,7},{7,6},{8,9},{9,8},{10,11... | collective-permute-start | bytes 786440 | tf_op jit(solution)/shard_map/ppermute | solution.py:225
  (14 other events, 74.7 us)
